TPU v7x, 32 devices: a whole 2x2x4 slice. The times are simulated.
32 devices in a mesh: shard: 4 (over y, x), rep: 8 (over z, core).
Axes of the slice: x: 2, y: 2, z: 4, core: 2. Of those that a mesh axis runs over, the one named last changes fastest.
Arguments:
- latents: bfloat16 [32, 256, 384], P(('shard', 'rep')), may hold values from -6 to 6
- condition: bfloat16 [32, 384], P(('shard', 'rep')), may hold values from -4 to 4
- cotangent: bfloat16 [32, 256, 384], P(('shard', 'rep')), may hold values from -6 to 6
- w_qkv: bfloat16 [2, 384, 1152], P(None, 'shard'), may hold values from -0.15625 to 0.15625
- b_qv: bfloat16 [2, 768], P(None, 'shard'), may hold values from -3 to 3
- w_proj: bfloat16 [2, 384, 384], P(None, 'shard'), may hold values from -1.75 to 1.75
- b_proj: bfloat16 [2, 384], P(None, 'shard'), may hold values from -3 to 3
- w_fc1: bfloat16 [2, 384, 1536], P(None, 'shard'), may hold values from -0.3125 to 0.3125
- b_fc1: bfloat16 [2, 1536], P(None, 'shard'), may hold values from -3 to 3
- w_fc2: bfloat16 [2, 1536, 384], P(None, 'shard'), may hold values from -0.15625 to 0.15625
- b_fc2: bfloat16 [2, 384], P(None, 'shard'), may hold values from -3 to 3
- w_ada: bfloat16 [2, 384, 2304], P(None, 'shard'), may hold values from -4 to 4
- b_ada: bfloat16 [2, 2304], P(None, 'shard'), may hold values from -3 to 3
Outputs:
- x_out: bfloat16 [32, 256, 384], P(('shard', 'rep'))
- x_grad: float32 [32, 256, 384], P(('shard', 'rep'))
- cond_grad: float32 [32, 384], P(('shard', 'rep'))
- grad_qkv: float32 [2, 384, 1152], P(None, 'shard')
- grad_qv_bias: float32 [2, 768], P(None, 'shard')
- grad_proj: float32 [2, 384, 384], P(None, 'shard')
- grad_proj_bias: float32 [2, 384], P(None, 'shard')
- grad_fc1: float32 [2, 384, 1536], P(None, 'shard')
- grad_fc1_bias: float32 [2, 1536], P(None, 'shard')
- grad_fc2: float32 [2, 1536, 384], P(None, 'shard')
- grad_fc2_bias: float32 [2, 384], P(None, 'shard')
- grad_ada: float32 [2, 384, 2304], P(None, 'shard')
- grad_ada_bias: float32 [2, 2304], P(None, 'shard')
All inputs are finite; a program needn't handle non-finite values.
Results may differ from a plain program's by a relative error of at most 0.017.
Values may be sent and summed in bfloat16 or wider, within the bound.
No kernel may reach another device: no remote copies, remote signals or barrier semaphores. Data moves between devices by JAX's collectives and lax.ppermute only.
A program may use at most 128 MiB of HBM per device.

v0:
```python
import jax
import jax.numpy as jnp
from jax import lax
from jax.sharding import PartitionSpec as P

HEADS = 6


def layer_norm(residual_state):
    center = residual_state - jnp.mean(residual_state, axis=-1, keepdims=True)
    inverse = lax.rsqrt(jnp.mean(center * center, axis=-1, keepdims=True) + 1e-06)
    return (center * inverse, inverse)


def norm_back(grad_norm, normed, inverse):
    centered = grad_norm - jnp.mean(grad_norm, axis=-1, keepdims=True)
    return inverse * (centered - normed * jnp.mean(grad_norm * normed, axis=-1, keepdims=True))


def project(left, right):
    return jnp.einsum("lsd,de->lse", left, right, preferred_element_type=jnp.float32)


def project_back(left, right):
    return jnp.einsum("lse,de->lsd", left, right, preferred_element_type=jnp.float32)


def weight_grad(left, right):
    return jnp.einsum("lsd,lse->de", left, right, preferred_element_type=jnp.float32)


def column_sums(grad_low):
    return jnp.sum(grad_low.astype(jnp.float32), axis=(0, 1))


def split_heads(tensor):
    return tensor.reshape(tensor.shape[0], tensor.shape[1], HEADS, tensor.shape[2] // HEADS)


def forward_layer(gathered, residual_state, condition_activation):
    w_qkv, b_qv, w_proj, b_proj, w_fc1, b_fc1, w_fc2, b_fc2, w_ada, b_ada = gathered
    width = residual_state.shape[2]
    modulate = jnp.dot(
        condition_activation, w_ada, preferred_element_type=jnp.float32
    ) + b_ada.astype(jnp.float32)
    pieces = [part_mod[:, None, :] for part_mod in jnp.split(modulate, 6, axis=-1)]
    shift_one, scale_one, gate_one, shift_two, scale_two, gate_two = pieces
    normed_one, inverse_one = layer_norm(residual_state)
    h_one = (normed_one * (1.0 + scale_one) + shift_one).astype(jnp.bfloat16)
    mixed = project(h_one, w_qkv)
    bias_wide = b_qv.astype(jnp.float32)
    queries = split_heads((mixed[..., :width] + bias_wide[:width]).astype(jnp.bfloat16))
    key_rows = split_heads(mixed[..., width : 2 * width].astype(jnp.bfloat16))
    value_rows = split_heads((mixed[..., 2 * width :] + bias_wide[width:]).astype(jnp.bfloat16))
    scale_dot = (width // HEADS) ** (-0.5)
    scores = (
        jnp.einsum("lqhd,lkhd->lhqk", queries, key_rows, preferred_element_type=jnp.float32)
        * scale_dot
    )
    top_score = jnp.max(scores, axis=-1, keepdims=True)
    log_total = top_score + jnp.log(jnp.sum(jnp.exp(scores - top_score), axis=-1, keepdims=True))
    probs_low = jnp.exp(scores - log_total).astype(jnp.bfloat16)
    attended = jnp.einsum(
        "lhqk,lkhd->lqhd", probs_low, value_rows, preferred_element_type=jnp.float32
    )
    attended = attended.reshape(residual_state.shape).astype(jnp.bfloat16)
    branch = project(attended, w_proj) + b_proj.astype(jnp.float32)
    middle = residual_state + gate_one * branch
    normed_two, inverse_two = layer_norm(middle)
    h_two = (normed_two * (1.0 + scale_two) + shift_two).astype(jnp.bfloat16)
    pre_act = project(h_two, w_fc1) + b_fc1.astype(jnp.float32)
    act_low = jax.nn.gelu(pre_act, approximate=True).astype(jnp.bfloat16)
    mlp_out = project(act_low, w_fc2) + b_fc2.astype(jnp.float32)
    stream_next = middle + gate_two * mlp_out
    stored = (
        pieces,
        normed_one,
        inverse_one,
        h_one,
        queries,
        key_rows,
        value_rows,
        log_total,
        attended,
        branch,
        normed_two,
        inverse_two,
        h_two,
        pre_act,
        act_low,
        mlp_out,
    )
    return (stream_next, stored)


def backward_layer(gathered, stored, grad_out, condition_activation):
    w_qkv, b_qv, w_proj, b_proj, w_fc1, b_fc1, w_fc2, b_fc2, w_ada, b_ada = gathered
    (
        pieces,
        normed_one,
        inverse_one,
        h_one,
        queries,
        key_rows,
        value_rows,
        log_total,
        attended,
        branch,
        normed_two,
        inverse_two,
        h_two,
        pre_act,
        act_low,
        mlp_out,
    ) = stored
    shift_one, scale_one, gate_one, shift_two, scale_two, gate_two = pieces
    width = grad_out.shape[2]
    scale_dot = (width // HEADS) ** (-0.5)
    d_gate_two = jnp.sum(grad_out * mlp_out, axis=1)
    d_mlp = (grad_out * gate_two).astype(jnp.bfloat16)
    g_fc2 = weight_grad(act_low, d_mlp)
    gb_fc2 = column_sums(d_mlp)
    d_act = project_back(d_mlp, w_fc2)
    gelu_pull = jax.vjp(lambda pre_in: jax.nn.gelu(pre_in, approximate=True), pre_act)[1]
    d_pre = gelu_pull(d_act)[0].astype(jnp.bfloat16)
    g_fc1 = weight_grad(h_two, d_pre)
    gb_fc1 = column_sums(d_pre)
    d_h_two = project_back(d_pre, w_fc1)
    d_shift_two = jnp.sum(d_h_two, axis=1)
    d_scale_two = jnp.sum(d_h_two * normed_two, axis=1)
    d_middle = grad_out + norm_back(d_h_two * (1.0 + scale_two), normed_two, inverse_two)
    d_gate_one = jnp.sum(d_middle * branch, axis=1)
    d_branch = (d_middle * gate_one).astype(jnp.bfloat16)
    g_proj = weight_grad(attended, d_branch)
    gb_proj = column_sums(d_branch)
    d_attended = split_heads(project_back(d_branch, w_proj).astype(jnp.bfloat16))
    scores = (
        jnp.einsum("lqhd,lkhd->lhqk", queries, key_rows, preferred_element_type=jnp.float32)
        * scale_dot
    )
    probs = jnp.exp(scores - log_total)
    probs_low = probs.astype(jnp.bfloat16)
    d_values = jnp.einsum(
        "lhqk,lqhd->lkhd", probs_low, d_attended, preferred_element_type=jnp.float32
    )
    d_probs = jnp.einsum(
        "lqhd,lkhd->lhqk", d_attended, value_rows, preferred_element_type=jnp.float32
    )
    d_scores = (probs * (d_probs - jnp.sum(probs * d_probs, axis=-1, keepdims=True))).astype(
        jnp.bfloat16
    )
    d_queries = (
        jnp.einsum("lhqk,lkhd->lqhd", d_scores, key_rows, preferred_element_type=jnp.float32)
        * scale_dot
    )
    d_keys = (
        jnp.einsum("lhqk,lqhd->lkhd", d_scores, queries, preferred_element_type=jnp.float32)
        * scale_dot
    )
    flat_shape = grad_out.shape
    d_qkv = jnp.concatenate(
        [d_queries.reshape(flat_shape), d_keys.reshape(flat_shape), d_values.reshape(flat_shape)],
        axis=-1,
    ).astype(jnp.bfloat16)
    g_qkv = weight_grad(h_one, d_qkv)
    qkv_sums = column_sums(d_qkv)
    gb_qv = jnp.concatenate([qkv_sums[:width], qkv_sums[2 * width :]])
    d_h_one = project_back(d_qkv, w_qkv)
    d_shift_one = jnp.sum(d_h_one, axis=1)
    d_scale_one = jnp.sum(d_h_one * normed_one, axis=1)
    d_stream = d_middle + norm_back(d_h_one * (1.0 + scale_one), normed_one, inverse_one)
    d_mod = jnp.concatenate(
        [d_shift_one, d_scale_one, d_gate_one, d_shift_two, d_scale_two, d_gate_two], axis=-1
    ).astype(jnp.bfloat16)
    g_ada = jnp.einsum("ld,le->de", condition_activation, d_mod, preferred_element_type=jnp.float32)
    gb_ada = jnp.sum(d_mod.astype(jnp.float32), axis=0)
    d_cond = jnp.einsum("le,de->ld", d_mod, w_ada, preferred_element_type=jnp.float32)
    grads = (g_qkv, gb_qv, g_proj, gb_proj, g_fc1, gb_fc1, g_fc2, gb_fc2, g_ada, gb_ada)
    return (d_stream, d_cond, grads)


def shards(
    latents,
    condition,
    cotangent,
    w_qkv,
    b_qv,
    w_proj,
    b_proj,
    w_fc1,
    b_fc1,
    w_fc2,
    b_fc2,
    w_ada,
    b_ada,
):
    layers = w_qkv.shape[0]
    total_latents = latents.shape[0] * lax.axis_size("shard") * lax.axis_size("rep")
    cond_in = condition.astype(jnp.float32)
    condition_activation = jax.nn.silu(cond_in).astype(jnp.bfloat16)
    residual_state = latents.astype(jnp.float32)
    gathered_all = []
    stored_all = []
    for layer_number in range(layers):
        gathered = (
            lax.all_gather(w_qkv[layer_number], "shard", axis=0, tiled=True),
            lax.all_gather(b_qv[layer_number], "shard", axis=0, tiled=True),
            lax.all_gather(w_proj[layer_number], "shard", axis=0, tiled=True),
            lax.all_gather(b_proj[layer_number], "shard", axis=0, tiled=True),
            lax.all_gather(w_fc1[layer_number], "shard", axis=0, tiled=True),
            lax.all_gather(b_fc1[layer_number], "shard", axis=0, tiled=True),
            lax.all_gather(w_fc2[layer_number], "shard", axis=0, tiled=True),
            lax.all_gather(b_fc2[layer_number], "shard", axis=0, tiled=True),
            lax.all_gather(w_ada[layer_number], "shard", axis=0, tiled=True),
            lax.all_gather(b_ada[layer_number], "shard", axis=0, tiled=True),
        )
        residual_state, stored = forward_layer(gathered, residual_state, condition_activation)
        gathered_all.append(gathered)
        stored_all.append(stored)
    x_out = residual_state.astype(jnp.bfloat16)
    grad_stream = cotangent.astype(jnp.float32)
    grad_cond = jnp.zeros(cond_in.shape, jnp.float32)
    collected = []
    for layer_number in reversed(range(layers)):
        gathered = (
            lax.all_gather(w_qkv[layer_number], "shard", axis=0, tiled=True),
            lax.all_gather(b_qv[layer_number], "shard", axis=0, tiled=True),
            lax.all_gather(w_proj[layer_number], "shard", axis=0, tiled=True),
            lax.all_gather(b_proj[layer_number], "shard", axis=0, tiled=True),
            lax.all_gather(w_fc1[layer_number], "shard", axis=0, tiled=True),
            lax.all_gather(b_fc1[layer_number], "shard", axis=0, tiled=True),
            lax.all_gather(w_fc2[layer_number], "shard", axis=0, tiled=True),
            lax.all_gather(b_fc2[layer_number], "shard", axis=0, tiled=True),
            lax.all_gather(w_ada[layer_number], "shard", axis=0, tiled=True),
            lax.all_gather(b_ada[layer_number], "shard", axis=0, tiled=True),
        )
        grad_stream, d_cond, grads = backward_layer(
            gathered, stored_all[layer_number], grad_stream, condition_activation
        )
        grad_cond = grad_cond + d_cond
        owner_rows = (
            lax.psum_scatter(
                grads[0].astype(jnp.bfloat16), "shard", scatter_dimension=0, tiled=True
            ).astype(jnp.float32),
            lax.psum_scatter(
                grads[1].astype(jnp.bfloat16), "shard", scatter_dimension=0, tiled=True
            ).astype(jnp.float32),
            lax.psum_scatter(
                grads[2].astype(jnp.bfloat16), "shard", scatter_dimension=0, tiled=True
            ).astype(jnp.float32),
            lax.psum_scatter(
                grads[3].astype(jnp.bfloat16), "shard", scatter_dimension=0, tiled=True
            ).astype(jnp.float32),
            lax.psum_scatter(
                grads[4].astype(jnp.bfloat16), "shard", scatter_dimension=0, tiled=True
            ).astype(jnp.float32),
            lax.psum_scatter(
                grads[5].astype(jnp.bfloat16), "shard", scatter_dimension=0, tiled=True
            ).astype(jnp.float32),
            lax.psum_scatter(
                grads[6].astype(jnp.bfloat16), "shard", scatter_dimension=0, tiled=True
            ).astype(jnp.float32),
            lax.psum_scatter(
                grads[7].astype(jnp.bfloat16), "shard", scatter_dimension=0, tiled=True
            ).astype(jnp.float32),
            lax.psum_scatter(
                grads[8].astype(jnp.bfloat16), "shard", scatter_dimension=0, tiled=True
            ).astype(jnp.float32),
            lax.psum_scatter(
                grads[9].astype(jnp.bfloat16), "shard", scatter_dimension=0, tiled=True
            ).astype(jnp.float32),
        )
        owner_rows = (
            lax.psum(owner_rows[0].astype(jnp.bfloat16), "rep").astype(jnp.float32),
            lax.psum(owner_rows[1].astype(jnp.bfloat16), "rep").astype(jnp.float32),
            lax.psum(owner_rows[2].astype(jnp.bfloat16), "rep").astype(jnp.float32),
            lax.psum(owner_rows[3].astype(jnp.bfloat16), "rep").astype(jnp.float32),
            lax.psum(owner_rows[4].astype(jnp.bfloat16), "rep").astype(jnp.float32),
            lax.psum(owner_rows[5].astype(jnp.bfloat16), "rep").astype(jnp.float32),
            lax.psum(owner_rows[6].astype(jnp.bfloat16), "rep").astype(jnp.float32),
            lax.psum(owner_rows[7].astype(jnp.bfloat16), "rep").astype(jnp.float32),
            lax.psum(owner_rows[8].astype(jnp.bfloat16), "rep").astype(jnp.float32),
            lax.psum(owner_rows[9].astype(jnp.bfloat16), "rep").astype(jnp.float32),
        )
        collected.insert(0, owner_rows)
    stacked = [
        jnp.stack([layer_rows[slot_no] for layer_rows in collected]) for slot_no in range(10)
    ]
    silu_pull = jax.vjp(jax.nn.silu, cond_in)[1]
    cond_grad = silu_pull(grad_cond)[0]
    inverse_count = 1.0 / total_latents
    return (
        x_out,
        grad_stream,
        cond_grad,
        stacked[0] * inverse_count,
        stacked[1] * inverse_count,
        stacked[2] * inverse_count,
        stacked[3] * inverse_count,
        stacked[4] * inverse_count,
        stacked[5] * inverse_count,
        stacked[6] * inverse_count,
        stacked[7] * inverse_count,
        stacked[8] * inverse_count,
        stacked[9] * inverse_count,
    )


def solution(mesh):
    return jax.shard_map(
        shards,
        mesh=mesh,
        in_specs=(
            P(("shard", "rep"), None, None),
            P(("shard", "rep"), None),
            P(("shard", "rep"), None, None),
            P(None, "shard", None),
            P(None, "shard"),
            P(None, "shard", None),
            P(None, "shard"),
            P(None, "shard", None),
            P(None, "shard"),
            P(None, "shard", None),
            P(None, "shard"),
            P(None, "shard", None),
            P(None, "shard"),
        ),
        out_specs=(
            P(("shard", "rep"), None, None),
            P(("shard", "rep"), None, None),
            P(("shard", "rep"), None),
            P(None, "shard", None),
            P(None, "shard"),
            P(None, "shard", None),
            P(None, "shard"),
            P(None, "shard", None),
            P(None, "shard"),
            P(None, "shard", None),
            P(None, "shard"),
            P(None, "shard", None),
            P(None, "shard"),
        ),
        check_vma=False,
    )
```

profile of v0, /device:TPU:0, one launch (start us, length us, event | category | flops | bytes accessed | tf_op | source)
XLA Modules:
  0.0 625.9 jit_solution(534134971308301505)
XLA Ops:
  17.0 9.5 %all-gather.17 = bf16[1,1536]{1,0:T(2,128)(2,1)S(1)} all-gather(bf16[1,384]{1,0:T(2,128)(2,1)S(1)} %get-tuple-element.131), channel_id=19, replica_groups=mesh['shard'=4,'rep'=8] {'shard'}, dimensions={1}, use_global_device_ids=true | all-gather | bytes 3840 | tf_op jit(solution)/shard_map/all_gather | solution.py:211
  27.2 8.0 %all-gather.7 = bf16[1,1536]{1,0:T(2,128)(2,1)S(1)} all-gather(bf16[1,384]{1,0:T(2,128)(2,1)S(1)} %get-tuple-element.132), channel_id=9, replica_groups=mesh['shard'=4,'rep'=8] {'shard'}, dimensions={1}, use_global_device_ids=true | all-gather | bytes 3840 | tf_op jit(solution)/shard_map/all_gather | solution.py:211
  37.5 15.8 %all-reduce.21 = (bf16[2304]{0:T(1024)(128)(2,1)S(1)}, bf16[768]{0:T(1024)(128)(2,1)S(1)}, bf16[384]{0:T(512)(128)(2,1)S(1)}, bf16[384]{0:T(512)(128)(2,1)S(1)},...) all-reduce(bf16[2304]{0:T(1024)(128)(2,1)S(1)} %dynamic-update-slic, ...), channel_id=3, replica_groups=mesh['shard'=4,'rep'=8] {'shard'}, use_global_device_ids=true, to_apply=%add | all-reduce | flops 7680 | bytes 30720
  56.3 10.3 %all-gather.14 = bf16[1,384,384]{2,1,0:T(8,128)(2,1)} all-gather(bf16[1,96,384]{2,1,0:T(8,128)(2,1)S(1)} %get-tuple-element.123), channel_id=16, replica_groups=mesh['shard'=4,'rep'=8] {'shard'}, dimensions={1}, use_global_device_ids=true | all-gather | bytes 368640 | tf_op jit(solution)/shard_map/all_gather | solution.py:208
  66.6 11.1 %all-gather.4 = bf16[1,384,384]{2,1,0:T(8,128)(2,1)S(1)} all-gather(bf16[1,96,384]{2,1,0:T(8,128)(2,1)S(1)} %get-tuple-element.124), channel_id=6, replica_groups=mesh['shard'=4,'rep'=8] {'shard'}, dimensions={1}, use_global_device_ids=true | all-gather | bytes 368640 | tf_op jit(solution)/shard_map/all_gather | solution.py:208
  77.7 14.5 %all-gather.12 = bf16[1,384,1152]{2,1,0:T(8,128)(2,1)S(1)} all-gather(bf16[1,96,1152]{2,1,0:T(8,128)(2,1)S(1)} %get-tuple-element.114), channel_id=14, replica_groups=mesh['shard'=4,'rep'=8] {'shard'}, dimensions={1}, use_global_device_ids=true | all-gather | bytes 1105920 | tf_op jit(solution)/shard_map/all_gather | solution.py:206
  92.2 14.5 %all-gather.2 = bf16[1,384,1152]{2,1,0:T(8,128)(2,1)S(1)} all-gather(bf16[1,96,1152]{2,1,0:T(8,128)(2,1)S(1)} %get-tuple-element.115), channel_id=4, replica_groups=mesh['shard'=4,'rep'=8] {'shard'}, dimensions={1}, use_global_device_ids=true | all-gather | bytes 1105920 | tf_op jit(solution)/shard_map/all_gather | solution.py:206
  115.7 4.5 all-gather.29.cloned.1.call-done
  120.2 3.0 convolution_add_fusion.1
  123.2 26.4 %all-gather.31.cloned.1.call-done = bf16[1,1536,384]{2,1,0:T(8,128)(2,1)} async-done(((bf16[1,384,384]{2,1,0:T(8,128)(2,1)}), bf16[1,1536,384]{2,1,0:T(8,128)(2,1)}) %all-gather.31.cloned.1.call-update) | async-done | bytes 1179664 | tf_op jit(solution)/shard_map/all_gather | solution.py:212
  149.6 3.2 fusion.152
  161.5 17.6 %all-gather.35.cloned.1.call-done = bf16[1,384,1536]{2,1,0:T(8,128)(2,1)} async-done(((bf16[1,96,1536]{2,1,0:T(8,128)(2,1)}), bf16[1,384,1536]{2,1,0:T(8,128)(2,1)}) %all-gather.35.cloned.1.call-update) | async-done | bytes 1179664 | tf_op jit(solution)/shard_map/all_gather | solution.py:210
  179.0 3.2 convolution_add_fusion
  182.2 26.9 %all-gather.37.cloned.1.call-done = bf16[1,1536,384]{2,1,0:T(8,128)(2,1)} async-done(((bf16[1,384,384]{2,1,0:T(8,128)(2,1)}), bf16[1,1536,384]{2,1,0:T(8,128)(2,1)}) %all-gather.37.cloned.1.call-update) | async-done | bytes 1179664 | tf_op jit(solution)/shard_map/all_gather | solution.py:212
  209.1 4.0 fusion.165
  226.8 2.5 fusion.87
  238.2 2.7 convolution_convert_fusion
  246.9 3.3 convolution_convert_fusion.2
  253.1 3.2 convolution_convert_fusion.3
  256.5 2.8 convolution_convert_fusion.5
  264.4 2.8 multiply_convert_fusion.1
  278.0 30.3 %reduce-scatter.13.cloned.1.call-done = bf16[96,1152]{1,0:T(8,128)(2,1)} async-done(((bf16[384,1152]{1,0:T(8,128)(2,1)}), bf16[96,1152]{1,0:T(8,128)(2,1)}) %reduce-scatter.13.cloned.1.call-update) | async-done | bytes 221200 | tf_op jit(solution)/shard_map/reduce_scatter | solution.py:242
  308.3 29.5 %reduce-scatter.11.cloned.1.call-done = bf16[96,1152]{1,0:T(8,128)(2,1)} async-done(((bf16[384,1152]{1,0:T(8,128)(2,1)}), bf16[96,1152]{1,0:T(8,128)(2,1)}) %reduce-scatter.11.cloned.1.call-update) | async-done | bytes 221200 | tf_op jit(solution)/shard_map/reduce_scatter | solution.py:242
  337.8 31.5 %reduce-scatter.25.cloned.1.call-done = bf16[384,384]{1,0:T(8,128)(2,1)} async-done(((bf16[1536,384]{1,0:T(8,128)(2,1)}), bf16[384,384]{1,0:T(8,128)(2,1)}) %reduce-scatter.25.cloned.1.call-update) | async-done | bytes 294928 | tf_op jit(solution)/shard_map/reduce_scatter | solution.py:260
  369.3 31.9 %reduce-scatter.21.cloned.1.call-done = bf16[96,1536]{1,0:T(8,128)(2,1)} async-done(((bf16[384,1536]{1,0:T(8,128)(2,1)}), bf16[96,1536]{1,0:T(8,128)(2,1)}) %reduce-scatter.21.cloned.1.call-update) | async-done | bytes 294928 | tf_op jit(solution)/shard_map/reduce_scatter | solution.py:254
  401.2 31.5 %reduce-scatter.23.cloned.1.call-done = bf16[384,384]{1,0:T(8,128)(2,1)} async-done(((bf16[1536,384]{1,0:T(8,128)(2,1)}), bf16[384,384]{1,0:T(8,128)(2,1)}) %reduce-scatter.23.cloned.1.call-update) | async-done | bytes 294928 | tf_op jit(solution)/shard_map/reduce_scatter | solution.py:260
  432.7 31.9 %reduce-scatter.19.cloned.1.call-done = bf16[96,1536]{1,0:T(8,128)(2,1)} async-done(((bf16[384,1536]{1,0:T(8,128)(2,1)}), bf16[96,1536]{1,0:T(8,128)(2,1)}) %reduce-scatter.19.cloned.1.call-update) | async-done | bytes 294928 | tf_op jit(solution)/shard_map/reduce_scatter | solution.py:254
  464.6 36.0 %reduce-scatter.27.cloned.1.call-done = bf16[96,2304]{1,0:T(8,128)(2,1)} async-done(((bf16[384,2304]{1,0:T(8,128)(2,1)}), bf16[96,2304]{1,0:T(8,128)(2,1)}) %reduce-scatter.27.cloned.1.call-update) | async-done | bytes 442384 | tf_op jit(solution)/shard_map/reduce_scatter | solution.py:266
  500.6 35.4 %reduce-scatter.29.cloned.1.call-done = bf16[96,2304]{1,0:T(8,128)(2,1)} async-done(((bf16[384,2304]{1,0:T(8,128)(2,1)}), bf16[96,2304]{1,0:T(8,128)(2,1)}) %reduce-scatter.29.cloned.1.call-update) | async-done | bytes 442384 | tf_op jit(solution)/shard_map/reduce_scatter | solution.py:266
  536.1 15.3 %all-reduce.20 = (bf16[768]{0:T(1024)(128)(2,1)S(1)}, bf16[768]{0:T(1024)(128)(2,1)S(1)}, bf16[384]{0:T(512)(128)(2,1)S(1)}, bf16[384]{0:T(512)(128)(2,1)S(1)}, ...) all-reduce(bf16[768]{0:T(1024)(128)(2,1)S(1)} %copy-done.118, ...), channel_id=25, replica_groups=mesh['shard'=4,'rep'=8] {'shard'}, use_global_device_ids=true, to_apply=%region_42.43.clone | all-reduce | flops 10752 | bytes 43008
  552.3 27.0 %all-reduce.18 = (bf16[1,192]{1,0:T(2,128)(2,1)S(1)}, bf16[1,192]{1,0:T(2,128)(2,1)S(1)}, bf16[1,96]{1,0:T(2,128)(2,1)S(1)}, bf16[1,96]{1,0:T(2,128)(2,1)S(1)}, ...) all-reduce(bf16[1,192]{1,0:T(2,128)(2,1)S(1)} %stack.145, ...), channel_id=1, replica_groups=mesh['shard'=4,'rep'=8] {'rep'}, use_global_device_ids=true, to_apply=%region_43.44 | all-reduce | flops 2688 | bytes 10752 | tf_op jit(solution)/shard_map/psum | solution.py:275
  582.8 29.2 %all-reduce.24.cloned.1.call-done = (bf16[1,96,1152]{2,1,0:T(8,128)(2,1)}, bf16[1,96,1152]{2,1,0:T(8,128)(2,1)}, bf16[1,96,384]{2,1,0:T(8,128)(2,1)}, bf16[1,96,...) async-done(((bf16[1,96,1152]{2,1,0:T(8,128)(2,1)}, ...) | async-done | bytes 2654224 | tf_op jit(solution)/shard_map/psum | solution.py:274
  (503 shorter events, 86.7 us)
Async XLA Ops:
  7.2 99.5 %all-gather.27.cloned.1.call-start = ((), (), s32[]{:S(2)}) async-start(), calls=%async_computation.20 | async-start | bytes 2211840 | tf_op jit(solution)/shard_map/all_gather | solution.py:214
  9.4 99.4 %all-gather.33.cloned.1.call-start = ((), (), s32[]{:S(2)}) async-start(), calls=%async_computation.23 | async-start | bytes 2211840 | tf_op jit(solution)/shard_map/all_gather | solution.py:214
  10.2 110.0 %all-gather.29.cloned.1.call-start = ((), (), s32[]{:S(2)}) async-start(), calls=%async_computation.21 | async-start | bytes 1474560 | tf_op jit(solution)/shard_map/all_gather | solution.py:210
  11.2 138.4 %all-gather.31.cloned.1.call-start = ((), (), s32[]{:S(2)}) async-start(), calls=%async_computation.22 | async-start | bytes 1474560 | tf_op jit(solution)/shard_map/all_gather | solution.py:212
  12.1 65.5 %copy-start.53 = (bf16[2,96,1152]{2,1,0:T(8,128)(2,1)S(1)}, bf16[2,96,1152]{2,1,0:T(8,128)(2,1)}, u32[]{:S(2)}) copy-start(bf16[2,96,1152]{2,1,0:T(8,128)(2,1)} %param.16) | copy-start | bytes 1327108
  12.2 166.9 %all-gather.35.cloned.1.call-start = ((), (), s32[]{:S(2)}) async-start(), calls=%async_computation.24 | async-start | bytes 1474560 | tf_op jit(solution)/shard_map/all_gather | solution.py:210
  12.7 196.3 %all-gather.37.cloned.1.call-start = ((), (), s32[]{:S(2)}) async-start(), calls=%async_computation.25 | async-start | bytes 1474560 | tf_op jit(solution)/shard_map/all_gather | solution.py:212
  13.3 262.2 %reduce-scatter.17.cloned.1.call-start = ((), (), s32[]{:S(2)}) async-start(), calls=%async_computation.13 | async-start | bytes 368640 | tf_op jit(solution)/shard_map/reduce_scatter | solution.py:248
  16.1 96.0 %copy-start.92 = (f32[256]{0:T(256)}, f32[256]{0:T(256)S(1)}, u32[]{:S(2)}) copy-start(f32[256]{0:T(256)S(1)} %broadcast_multiply_fusion.11) | copy-start | bytes 3076
  16.3 95.7 %copy-start.103 = (f32[256]{0:T(256)}, f32[256]{0:T(256)S(1)}, u32[]{:S(2)}) copy-start(f32[256]{0:T(256)S(1)} %add_rsqrt_fusion.3) | copy-start | bytes 3076
  17.0 91.9 %copy-start.83 = (f32[1,384]{1,0:T(1,128)}, f32[1,384]{1,0:T(1,128)S(1)}, u32[]{:S(2)}) copy-start(f32[1,384]{1,0:T(1,128)S(1)} %get-tuple-element.97) | copy-start | bytes 4612
  92.2 60.9 %copy-start.13 = (bf16[1,384,1152]{2,1,0:T(8,128)(2,1)}, bf16[1,384,1152]{2,1,0:T(8,128)(2,1)S(1)}, u32[]{:S(2)}) copy-start(bf16[1,384,1152]{2,1,0:T(8,128)(2,1)S(1)} %all-gather.12) | copy-start | bytes 2654212
  226.6 51.4 %reduce-scatter.15.cloned.1.call-start = ((), (), s32[]{:S(2)}) async-start(), calls=%async_computation.12 | async-start | bytes 368640 | tf_op jit(solution)/shard_map/reduce_scatter | solution.py:248
  238.1 70.2 %reduce-scatter.13.cloned.1.call-start = ((), (), s32[]{:S(2)}) async-start(), calls=%async_computation.11 | async-start | bytes 1105920 | tf_op jit(solution)/shard_map/reduce_scatter | solution.py:242
  240.9 97.0 %reduce-scatter.11.cloned.1.call-start = ((), (), s32[]{:S(2)}) async-start(), calls=%async_computation.10 | async-start | bytes 1105920 | tf_op jit(solution)/shard_map/reduce_scatter | solution.py:242
  246.8 122.5 %reduce-scatter.25.cloned.1.call-start = ((), (), s32[]{:S(2)}) async-start(), calls=%async_computation.17 | async-start | bytes 1474560 | tf_op jit(solution)/shard_map/reduce_scatter | solution.py:260
  250.2 151.0 %reduce-scatter.21.cloned.1.call-start = ((), (), s32[]{:S(2)}) async-start(), calls=%async_computation.15 | async-start | bytes 1474560 | tf_op jit(solution)/shard_map/reduce_scatter | solution.py:254
  253.0 179.7 %reduce-scatter.23.cloned.1.call-start = ((), (), s32[]{:S(2)}) async-start(), calls=%async_computation.16 | async-start | bytes 1474560 | tf_op jit(solution)/shard_map/reduce_scatter | solution.py:260
  256.4 208.2 %reduce-scatter.19.cloned.1.call-start = ((), (), s32[]{:S(2)}) async-start(), calls=%async_computation.14 | async-start | bytes 1474560 | tf_op jit(solution)/shard_map/reduce_scatter | solution.py:254
  259.3 241.3 %reduce-scatter.27.cloned.1.call-start = ((), (), s32[]{:S(2)}) async-start(), calls=%async_computation.18 | async-start | bytes 2211840 | tf_op jit(solution)/shard_map/reduce_scatter | solution.py:266
  267.3 268.7 %reduce-scatter.29.cloned.1.call-start = ((), (), s32[]{:S(2)}) async-start(), calls=%async_computation.19 | async-start | bytes 2211840 | tf_op jit(solution)/shard_map/reduce_scatter | solution.py:266
  267.9 344.1 %all-reduce.24.cloned.1.call-start = ((), (), s32[]{:S(2)}) async-start(), calls=%async_computation.26 | async-start | bytes 5308416 | tf_op jit(solution)/shard_map/psum | solution.py:274
  275.4 260.6 %copy-start.118 = (bf16[768]{0:T(1024)(128)(2,1)S(1)}, bf16[768]{0:T(1024)(128)(2,1)}, u32[]{:S(2)}) copy-start(bf16[768]{0:T(1024)(128)(2,1)} %pad_maximum_fusion.7) | copy-start | bytes 4612
  275.4 260.6 %copy-start.123 = (bf16[384]{0:T(512)(128)(2,1)S(1)}, bf16[384]{0:T(512)(128)(2,1)}, u32[]{:S(2)}) copy-start(bf16[384]{0:T(512)(128)(2,1)} %get-tuple-element.93) | copy-start | bytes 2308
  275.4 260.6 %copy-start.124 = (bf16[384]{0:T(512)(128)(2,1)S(1)}, bf16[384]{0:T(512)(128)(2,1)}, u32[]{:S(2)}) copy-start(bf16[384]{0:T(512)(128)(2,1)} %get-tuple-element.122) | copy-start | bytes 2308
  275.5 260.6 %copy-start.125 = (bf16[384]{0:T(512)(128)(2,1)S(1)}, bf16[384]{0:T(512)(128)(2,1)}, u32[]{:S(2)}) copy-start(bf16[384]{0:T(512)(128)(2,1)} %get-tuple-element.87) | copy-start | bytes 2308
  275.5 260.6 %copy-start.126 = (bf16[384]{0:T(512)(128)(2,1)S(1)}, bf16[384]{0:T(512)(128)(2,1)}, u32[]{:S(2)}) copy-start(bf16[384]{0:T(512)(128)(2,1)} %get-tuple-element.90) | copy-start | bytes 2308
  275.5 260.6 %copy-start.129 = (bf16[1536]{0:T(1024)(128)(2,1)S(1)}, bf16[1536]{0:T(1024)(128)(2,1)}, u32[]{:S(2)}) copy-start(bf16[1536]{0:T(1024)(128)(2,1)} %get-tuple-element.154) | copy-start | bytes 9220
  275.5 260.6 %copy-start.130 = (bf16[1536]{0:T(1024)(128)(2,1)S(1)}, bf16[1536]{0:T(1024)(128)(2,1)}, u32[]{:S(2)}) copy-start(bf16[1536]{0:T(1024)(128)(2,1)} %get-tuple-element.156) | copy-start | bytes 9220
  275.5 276.5 %copy-start.119 = (f32[384]{0:T(512)S(1)}, f32[384]{0:T(512)}, u32[]{:S(2)}) copy-start(f32[384]{0:T(512)} %fusion.53) | copy-start | bytes 4612
  275.5 306.7 %copy-start.82 = (bf16[1,384]{1,0:T(2,128)(2,1)S(1)}, bf16[1,384]{1,0:T(2,128)(2,1)}, u32[]{:S(2)}) copy-start(bf16[1,384]{1,0:T(2,128)(2,1)} %param.14) | copy-start | bytes 2308
  275.5 306.7 %copy-start.84 = (f32[1,384]{1,0:T(1,128)S(1)}, f32[1,384]{1,0:T(1,128)}, u32[]{:S(2)}) copy-start(f32[1,384]{1,0:T(1,128)} %copy-done.83) | copy-start | bytes 4612
  (130 other events, 512.2 us)
Sparse Core Ops, SparseCore 0:
  10.4 36.0 all-gather.26
  49.0 39.2 all-gather.32
  90.7 29.4 all-gather.28
  121.8 27.7 all-gather.30
  151.3 27.7 all-gather.34
  181.3 27.7 all-gather.36
  226.7 24.2 reduce-scatter.16
  253.7 24.2 reduce-scatter.14
  281.5 26.7 reduce-scatter.12
  311.1 26.6 reduce-scatter.10
  340.8 28.5 reduce-scatter.24
  372.7 28.5 reduce-scatter.20
  404.1 28.5 reduce-scatter.22
  436.1 28.5 reduce-scatter.18
  468.1 32.4 reduce-scatter.26
  503.5 32.4 reduce-scatter.28
  539.1 72.8 all-reduce.23
where the time goes:
time: 627 us; the launch traced here: 626 us
  waiting for transfers between devices  367 us (59%)
  blocking collectives  126 us (20%)
  matrix products  59.6 us (10%)
  other arithmetic  31.8 us (5%)
  local copies, waits for them, and re-layouts  20.1 us (3%)
  between operations  20 us (3%)
    reduce_scatter x2, waiting for transfers between devices, shards(): lax.psum_scatter(grads[8].astype(jnp.bfloat16), 'shard', scatter_dimensio...  71.4 us
    reduce_scatter x2, waiting for transfers between devices, shards(): lax.psum_scatter(grads[4].astype(jnp.bfloat16), 'shard', scatter_dimensio...  63.8 us
    reduce_scatter x2, waiting for transfers between devices, shards(): lax.psum_scatter(grads[6].astype(jnp.bfloat16), 'shard', scatter_dimensio...  63 us
    reduce_scatter x2, waiting for transfers between devices, shards(): lax.psum_scatter(grads[0].astype(jnp.bfloat16), 'shard', scatter_dimensio...  59.8 us
    all_gather x2, waiting for transfers between devices, shards(): lax.all_gather(w_fc2[layer_number], 'shard', axis=0, tiled=True)  53.2 us
    unnamed x2, blocking collectives  31.1 us
    psum x1, waiting for transfers between devices, shards(): lax.psum(owner_rows[0].astype(jnp.bfloat16), 'rep').astype(jnp.float32)  29.2 us
    all_gather x2, blocking collectives, shards(): lax.all_gather(w_qkv[layer_number], 'shard', axis=0, tiled=True)  28.9 us
  transfers between devices with their start and end apart: 17, of which 14 were waited for; matrix products, arithmetic and copies ran while one was open for 13% of the time, Pallas kernels for 0%

commit v1 on v0

v1 whole, which is shorter than its diff:
```python
import functools

import jax
import jax.numpy as jnp
from jax import lax
from jax.experimental import pallas as pl
from jax.experimental.pallas import tpu as pltpu
from jax.sharding import PartitionSpec as P

HEADS = 6
BF = jnp.bfloat16
F32 = jnp.float32
CORES = 2
VMEM_LIMIT = 40 * 1024 * 1024


def dot(left, right):
    return jnp.dot(left, right, preferred_element_type=F32)


def dot_nt(left, right):
    return lax.dot_general(left, right, (((1,), (1,)), ((), ())), preferred_element_type=F32)


def dot_tn(left, right):
    return lax.dot_general(left, right, (((0,), (0,)), ((), ())), preferred_element_type=F32)


def layer_norm(rows):
    center = rows - jnp.mean(rows, axis=-1, keepdims=True)
    inverse = lax.rsqrt(jnp.mean(center * center, axis=-1, keepdims=True) + 1e-06)
    return center * inverse, inverse


def norm_back(grad_norm, normed, inverse):
    centered = grad_norm - jnp.mean(grad_norm, axis=-1, keepdims=True)
    return inverse * (centered - normed * jnp.mean(grad_norm * normed, axis=-1, keepdims=True))


def col_sum(rows):
    return jnp.sum(rows, axis=0, keepdims=True)


def block_at(start, size):
    return pl.ds(pl.multiple_of(start, size), size)


def start_all(copies):
    for copy in copies:
        copy.start()


def wait_all(copies):
    for copy in copies:
        copy.wait()


def make_copies(pairs, sems):
    return [
        pltpu.make_async_copy(source, target, sems.at[slot])
        for slot, (source, target) in enumerate(pairs)
    ]


def run(body, name, inputs, outputs, scratch=(), flops=0):
    places = {"v": pltpu.VMEM, "a": pl.ANY, "s": pltpu.SMEM}
    moved = sum(arr.size * arr.dtype.itemsize for arr, _ in inputs)
    return pl.pallas_call(
        body,
        out_shape=[jax.ShapeDtypeStruct(shape, dtype) for shape, dtype, _ in outputs],
        in_specs=[pl.BlockSpec(memory_space=places[kind]) for _, kind in inputs],
        out_specs=[pl.BlockSpec(memory_space=places[kind]) for _, _, kind in outputs],
        scratch_shapes=list(scratch),
        compiler_params=pltpu.CompilerParams(vmem_limit_bytes=VMEM_LIMIT),
        cost_estimate=pl.CostEstimate(flops=flops, bytes_accessed=moved, transcendentals=0),
        name=name,
    )(*[arr for arr, _ in inputs])


def qkv_pairs(idx, layer, rows, offset, w_qkv, w_proj, near, far, w_all):
    width = w_proj.shape[-1]
    own = block_at(idx[0] * rows, rows)
    pairs = [
        (w_qkv.at[layer, :, : 2 * width], w_all.at[0, own, :]),
        (w_qkv.at[layer, :, 2 * width :], w_all.at[1, own, :width]),
        (w_proj.at[layer], w_all.at[1, own, width:]),
    ]
    return pairs + piece_pairs(idx, rows, offset, 2 * width, near, far, w_all)


def mlp_pairs(idx, layer, rows, offset, w_fc1, w_fc2, near, far, w_all):
    width = w_fc2.shape[-1]
    hidden = w_fc1.shape[-1]
    own = block_at(idx[0] * rows, rows)
    pairs = [(w_fc1.at[layer], w_all.at[0, own, :])]
    for part in range(hidden // width):
        pairs.append(
            (
                w_fc2.at[layer, part * rows : (part + 1) * rows, :],
                w_all.at[1, own, part * width : (part + 1) * width],
            )
        )
    return pairs + piece_pairs(idx, rows, offset, hidden, near, far, w_all)


def piece_pairs(idx, rows, offset, wide, near, far, w_all):
    pairs = []
    for step, (near_piece, far_piece) in enumerate(zip(near, far)):
        place = block_at(jnp.bitwise_xor(idx[0], step + 1) * rows, rows)
        pairs.append((near_piece.at[:, offset : offset + wide], w_all.at[idx[2], place, :]))
        pairs.append((far_piece.at[:, offset : offset + wide], w_all.at[1 - idx[2], place, :]))
    return pairs


def grad_pairs(idx, rows, shards, grad_all, keep, send):
    pairs = []
    for step in range(shards):
        place = block_at(jnp.bitwise_xor(idx[0], step) * rows, rows)
        pairs.append((grad_all.at[idx[2], place, :], keep.at[step]))
        pairs.append((grad_all.at[1 - idx[2], place, :], send.at[step]))
    return pairs


def fc2_chunk(w_all, rows, chunk):
    width = w_all.shape[1]
    parts = w_all.shape[2] // width
    blocks = []
    for number in range(chunk * width // rows, (chunk + 1) * width // rows):
        at, part = number // parts, number % parts
        blocks.append(w_all[1, at * rows : (at + 1) * rows, part * width : (part + 1) * width])
    return jnp.concatenate(blocks, axis=0)


def attention_forward(layer, rows, offset, peers, *refs):
    idx, stream, mod, b_qv, b_proj, w_qkv, w_proj = refs[:7]
    near, far = refs[7 : 7 + peers], refs[7 + peers : 7 + 2 * peers]
    qkv_out, probs_out, attended_out, branch_out, middle_out, w_all, sems = refs[7 + 2 * peers :]
    copies = make_copies(
        qkv_pairs(idx, layer, rows, offset, w_qkv, w_proj, near, far, w_all), sems
    )
    start_all(copies)
    width = stream.shape[-1]
    head = width // HEADS
    values = stream[...].astype(F32)
    shift, scale, gate = (mod[:, part * width : (part + 1) * width] for part in range(3))
    normed, _ = layer_norm(values)
    h_one = (normed * (1.0 + scale) + shift).astype(BF)
    wait_all(copies)
    mixed = dot(h_one, w_all[0])
    qkv_out[:, :width] = (mixed[:, :width] + b_qv[:, :width]).astype(BF)
    qkv_out[:, width : 2 * width] = mixed[:, width:].astype(BF)
    qkv_out[:, 2 * width :] = (dot(h_one, w_all[1, :, :width]) + b_qv[:, width:]).astype(BF)
    lane = lax.broadcasted_iota(jnp.int32, (1, 2 * head), 1)
    masks = [(lane < head).astype(BF), (lane >= head).astype(BF)]
    for pair in range(HEADS // 2):
        at = pair * 2 * head
        queries = qkv_out[:, at : at + 2 * head]
        keys = qkv_out[:, width + at : width + at + 2 * head]
        vals = qkv_out[:, 2 * width + at : 2 * width + at + 2 * head]
        attended = 0.0
        for side in range(2):
            scores = dot_nt(queries, keys * masks[side]) * head ** (-0.5)
            raised = jnp.exp(scores - jnp.max(scores, axis=-1, keepdims=True))
            probs = raised * (1.0 / jnp.sum(raised, axis=-1, keepdims=True))
            probs_out[2 * pair + side] = probs
            attended = attended + dot(probs.astype(BF), vals * masks[side])
        attended_out[:, at : at + 2 * head] = attended.astype(BF)
    branch = dot(attended_out[...], w_all[1, :, width:]) + b_proj[...]
    branch_out[...] = branch
    middle_out[...] = values + gate * branch


def attention_backward(layer, rows, offset, peers, *refs):
    idx, stream, mod, d_middle_in, qkv, probs_in, attended, branch, w_qkv, w_proj = refs[:10]
    near, far = refs[10 : 10 + peers], refs[10 + peers : 10 + 2 * peers]
    d_stream, vec, keep, send, w_all, d_qkv, grad_all, sems, out_sems = refs[10 + 2 * peers :]
    copies = make_copies(
        qkv_pairs(idx, layer, rows, offset, w_qkv, w_proj, near, far, w_all), sems
    )
    start_all(copies)
    width = stream.shape[-1]
    head = width // HEADS
    root = head ** (-0.5)
    shift, scale, gate = (mod[:, part * width : (part + 1) * width] for part in range(3))
    normed, inverse = layer_norm(stream[...].astype(F32))
    h_one = (normed * (1.0 + scale) + shift).astype(BF)
    d_middle = d_middle_in[...]
    vec[:, 2 * width : 3 * width] = col_sum(d_middle * branch[...])
    d_branch = (d_middle * gate).astype(BF)
    grad_all[1, :, width:] = dot_tn(attended[...], d_branch).astype(BF)
    vec[:, 5 * width :] = col_sum(d_branch.astype(F32))
    wait_all(copies)
    d_attended = dot_nt(d_branch, w_all[1, :, width:]).astype(BF)
    lane = lax.broadcasted_iota(jnp.int32, (1, 2 * head), 1)
    masks = [(lane < head).astype(BF), (lane >= head).astype(BF)]
    for pair in range(HEADS // 2):
        at = pair * 2 * head
        queries = qkv[:, at : at + 2 * head]
        keys = qkv[:, width + at : width + at + 2 * head]
        vals = qkv[:, 2 * width + at : 2 * width + at + 2 * head]
        d_att = d_attended[:, at : at + 2 * head]
        d_queries, d_keys, d_values = 0.0, 0.0, 0.0
        for side in range(2):
            probs = probs_in[2 * pair + side]
            d_values = d_values + dot_tn(probs.astype(BF), d_att * masks[side])
            d_probs = dot_nt(d_att, vals * masks[side])
            inner = jnp.sum(probs * d_probs, axis=-1, keepdims=True)
            d_scores = (probs * (d_probs - inner)).astype(BF)
            d_queries = d_queries + dot(d_scores, keys * masks[side])
            d_keys = d_keys + dot_tn(d_scores, queries * masks[side])
        d_qkv[:, at : at + 2 * head] = (d_queries * root).astype(BF)
        d_qkv[:, width + at : width + at + 2 * head] = (d_keys * root).astype(BF)
        d_qkv[:, 2 * width + at : 2 * width + at + 2 * head] = d_values.astype(BF)
    d_qk, d_val = d_qkv[:, : 2 * width], d_qkv[:, 2 * width :]
    grad_all[0] = dot_tn(h_one, d_qk).astype(BF)
    grad_all[1, :, :width] = dot_tn(h_one, d_val).astype(BF)
    out_copies = make_copies(grad_pairs(idx, rows, peers + 1, grad_all, keep, send), out_sems)
    start_all(out_copies)
    vec[:, 3 * width : 4 * width] = col_sum(d_qk[:, :width].astype(F32))
    vec[:, 4 * width : 5 * width] = col_sum(d_val.astype(F32))
    d_h_one = dot_nt(d_qk, w_all[0]) + dot_nt(d_val, w_all[1, :, :width])
    vec[:, :width] = col_sum(d_h_one)
    vec[:, width : 2 * width] = col_sum(d_h_one * normed)
    d_stream[...] = d_middle + norm_back(d_h_one * (1.0 + scale), normed, inverse)
    wait_all(out_copies)


def gelu_parts(pre_act):
    root = 0.7978845608028654
    square = pre_act * pre_act
    bent = jnp.tanh(root * pre_act * (1.0 + 0.044715 * square))
    half = 0.5 * (1.0 + bent)
    slope = half + 0.5 * pre_act * (1.0 - bent * bent) * (root * (1.0 + 3 * 0.044715 * square))
    return pre_act * half, slope


def mlp_forward_part(rows, h_two, b_fc1, b_fc2, w_all, act_low, slopes):
    width = w_all.shape[1]
    mlp_out = b_fc2[...]
    for chunk in range(w_all.shape[2] // width):
        cols = slice(chunk * width, (chunk + 1) * width)
        act, slope = gelu_parts(dot(h_two, w_all[0, :, cols]) + b_fc1[:, cols])
        act_low[:, cols] = act.astype(BF)
        slopes[:, cols] = slope
        mlp_out = mlp_out + dot(act_low[:, cols], fc2_chunk(w_all, rows, chunk))
    return mlp_out


def mlp_backward_part(
    idx, rows, shards, grad_out, mlp_out, middle, normed, inverse, h_two, scale, gate,
    w_all, act_low, slopes, vec, d_middle_out, grad_all, keep, send, out_sems,
):
    width = w_all.shape[1]
    parts = w_all.shape[2] // width
    vec[:, 2 * width : 3 * width] = col_sum(grad_out * mlp_out)
    d_mlp = (grad_out * gate).astype(BF)
    vec[:, (3 + parts) * width :] = col_sum(d_mlp.astype(F32))
    d_h_two = 0.0
    for chunk in range(parts):
        cols = slice(chunk * width, (chunk + 1) * width)
        d_act = dot_nt(d_mlp, fc2_chunk(w_all, rows, chunk))
        d_pre = (d_act * slopes[:, cols]).astype(BF)
        vec[:, (3 + chunk) * width : (4 + chunk) * width] = col_sum(d_pre.astype(F32))
        grad_all[0, :, cols] = dot_tn(h_two, d_pre).astype(BF)
        grad_fc2 = dot_tn(act_low[:, cols], d_mlp).astype(BF)
        first = chunk * width // rows
        for number in range(first, (chunk + 1) * width // rows):
            at, part = number // parts, number % parts
            grad_all[1, at * rows : (at + 1) * rows, part * width : (part + 1) * width] = grad_fc2[
                (number - first) * rows : (number - first + 1) * rows
            ]
        d_h_two = d_h_two + dot_nt(d_pre, w_all[0, :, cols])
    out_copies = make_copies(grad_pairs(idx, rows, shards, grad_all, keep, send), out_sems)
    start_all(out_copies)
    vec[:, :width] = col_sum(d_h_two)
    vec[:, width : 2 * width] = col_sum(d_h_two * normed)
    d_middle_out[...] = grad_out + norm_back(d_h_two * (1.0 + scale), normed, inverse)
    wait_all(out_copies)


def mlp_forward(layer, rows, offset, peers, *refs):
    idx, middle, mod, b_fc1, b_fc2, w_fc1, w_fc2 = refs[:7]
    near, far = refs[7 : 7 + peers], refs[7 + peers : 7 + 2 * peers]
    act_low, slopes, mlp_out, stream_out, w_all, sems = refs[7 + 2 * peers :]
    copies = make_copies(mlp_pairs(idx, layer, rows, offset, w_fc1, w_fc2, near, far, w_all), sems)
    start_all(copies)
    width = middle.shape[-1]
    shift, scale, gate = (mod[:, part * width : (part + 1) * width] for part in range(3, 6))
    normed, _ = layer_norm(middle[...])
    h_two = (normed * (1.0 + scale) + shift).astype(BF)
    wait_all(copies)
    mlp_out[...] = mlp_forward_part(rows, h_two, b_fc1, b_fc2, w_all, act_low, slopes)
    stream_out[...] = middle[...] + gate * mlp_out[...]


def mlp_backward(layer, rows, offset, peers, *refs):
    idx, middle, mod, grad_out, act_low, slopes, mlp_out, w_fc1, w_fc2 = refs[:9]
    near, far = refs[9 : 9 + peers], refs[9 + peers : 9 + 2 * peers]
    d_middle, vec, keep, send, w_all, grad_all, sems, out_sems = refs[9 + 2 * peers :]
    copies = make_copies(mlp_pairs(idx, layer, rows, offset, w_fc1, w_fc2, near, far, w_all), sems)
    start_all(copies)
    width = middle.shape[-1]
    shift, scale, gate = (mod[:, part * width : (part + 1) * width] for part in range(3, 6))
    normed, inverse = layer_norm(middle[...])
    h_two = (normed * (1.0 + scale) + shift).astype(BF)
    wait_all(copies)
    mlp_backward_part(
        idx, rows, peers + 1, grad_out[...], mlp_out[...], middle, normed, inverse, h_two, scale,
        gate, w_all, act_low, slopes, vec, d_middle, grad_all, keep, send, out_sems,
    )


def mlp_both(layer, rows, offset, peers, *refs):
    idx, middle, mod, b_fc1, b_fc2, cotangent, w_fc1, w_fc2 = refs[:8]
    near, far = refs[8 : 8 + peers], refs[8 + peers : 8 + 2 * peers]
    x_out, d_middle, vec, keep, send = refs[8 + 2 * peers : 13 + 2 * peers]
    w_all, grad_all, act_low, slopes, sems, out_sems = refs[13 + 2 * peers :]
    copies = make_copies(mlp_pairs(idx, layer, rows, offset, w_fc1, w_fc2, near, far, w_all), sems)
    start_all(copies)
    width = middle.shape[-1]
    shift, scale, gate = (mod[:, part * width : (part + 1) * width] for part in range(3, 6))
    normed, inverse = layer_norm(middle[...])
    h_two = (normed * (1.0 + scale) + shift).astype(BF)
    wait_all(copies)
    mlp_out = mlp_forward_part(rows, h_two, b_fc1, b_fc2, w_all, act_low, slopes)
    x_out[...] = (middle[...] + gate * mlp_out).astype(BF)
    mlp_backward_part(
        idx, rows, peers + 1, cotangent[...].astype(F32), mlp_out, middle, normed, inverse, h_two,
        scale, gate, w_all, act_low, slopes, vec, d_middle, grad_all, keep, send, out_sems,
    )


def padded_rows(idx, w_ada, w_pad, sems):
    layers, rows, wide = w_ada.shape
    w_pad[...] = jnp.zeros(w_pad.shape, BF)
    own = block_at(idx[0] * rows, rows)
    return make_copies(
        [
            (w_ada.at[layer], w_pad.at[own, layer * wide : (layer + 1) * wide])
            for layer in range(layers)
        ],
        sems,
    )


def modulate_kernel(shards, *refs):
    idx, w_ada = refs[:2]
    conditions, outs = refs[2 : 2 + shards], refs[2 + shards : 2 + 2 * shards]
    w_pad, sems = refs[2 + 2 * shards :]
    copies = padded_rows(idx, w_ada, w_pad, sems)
    start_all(copies)
    width = w_pad.shape[0]
    acts = []
    for ref in conditions:
        cond = ref[:, :width].astype(F32)
        acts.append(cond / (1.0 + jnp.exp(-cond)))
    acts = jnp.concatenate(acts, axis=0).astype(BF)
    wait_all(copies)
    result = dot(acts, w_pad[...])
    for step in range(shards):
        outs[step][...] = result[step : step + 1]


def condition_back_kernel(shards, *refs):
    idx, w_ada = refs[:2]
    vectors, outs = refs[2 : 2 + shards], refs[2 + shards : 2 + 2 * shards]
    w_pad, sems = refs[2 + 2 * shards :]
    copies = padded_rows(idx, w_ada, w_pad, sems)
    start_all(copies)
    width, wide = w_pad.shape
    d_mod = jnp.concatenate([ref[:, width : width + wide] for ref in vectors], axis=0)
    wait_all(copies)
    result = dot_nt(d_mod, w_pad[...])
    for step in range(shards):
        outs[step][...] = result[step : step + 1]


def ada_grad_kernel(rows, wide, inverse_count, *refs):
    idx, gathered = refs[:2]
    grad_ada, sums, turned = refs[2:]
    layers = grad_ada.shape[0]
    width = turned.shape[0]
    turned[...] = gathered[:, :width].astype(F32).T
    own = turned[block_at(idx[0] * rows, rows), :].astype(BF)
    for layer in range(layers):
        at = width + layer * wide
        grad_ada[layer] = dot(own, gathered[:, at : at + wide]) * inverse_count
    sums[...] = col_sum(gathered[:, width:].astype(F32)) * inverse_count


def core_sum_kernel(shards, count, *refs):
    keeps, recvs, outs = refs[:count], refs[count : 2 * count], refs[2 * count :]
    for step in range(shards):
        at = 0
        for keep, recv in zip(keeps, recvs):
            wide = keep.shape[-1]
            total = keep[step].astype(F32) + recv[step].astype(F32)
            outs[step][:, at : at + wide] = total.astype(BF)
            at += wide


def shard_sum_kernel(shards, levels, *refs):
    idx, terms, outs = refs[0], refs[1 : 1 + shards], refs[1 + shards : 1 + shards + levels]
    units, sems = refs[1 + shards + levels :]
    total = terms[0][...].astype(F32)
    for term in terms[1:]:
        total = total + term[...].astype(F32)
    total = total.astype(BF)
    rows, wide = total.shape
    slot = 0
    for row in range(0, rows, 16):
        for col in range(0, wide, 128):
            units[slot] = total[row : row + 16, col : col + 128]
            slot += 1
    size = units.shape[0] // levels
    for extra in range(slot, units.shape[0]):
        units[extra] = jnp.zeros((16, 128), BF)
    for step in range(levels):
        outs[step][...] = units[pl.ds(jnp.bitwise_xor(idx[1], step) * size, size)]


def level_sum_kernel(*refs):
    total = refs[0][...].astype(F32)
    for term in refs[1:-1]:
        total = total + term[...].astype(F32)
    refs[-1][...] = total.astype(BF)


def unpack_units(idx, near, far, units):
    size = near[0].shape[0]
    for step, (near_piece, far_piece) in enumerate(zip(near, far)):
        place = pl.ds(jnp.bitwise_xor(idx[1], step) * size, size)
        units[idx[2], place] = near_piece[...]
        units[1 - idx[2], place] = far_piece[...]


def place_units(units, half, first, target, rows, wide, at_row, at_col, skip, total_wide, factor):
    for row in range(0, rows, 16):
        for col in range(0, wide, 128):
            slot = first + (row // 16) * (total_wide // 128) + (skip + col) // 128
            target[at_row + row : at_row + row + 16, at_col + col : at_col + col + 128] = (
                units[half, slot].astype(F32) * factor
            )


def finish_qkv(units, target_qkv, target_proj, rows, skip, total_wide, factor):
    width = target_proj.shape[-1]
    put = functools.partial(
        place_units, rows=rows, at_row=0, total_wide=total_wide, factor=factor, first=0
    )
    put(units, 0, target=target_qkv, wide=2 * width, at_col=0, skip=skip)
    put(units, 1, target=target_qkv, wide=width, at_col=2 * width, skip=skip)
    put(units, 1, target=target_proj, wide=width, at_col=0, skip=skip + width)


def finish_mlp(units, target_fc1, target_fc2, rows, skip, total_wide, factor):
    width = target_fc2.shape[-1]
    hidden = target_fc1.shape[-1]
    put = functools.partial(
        place_units, rows=rows, total_wide=total_wide, factor=factor, first=0
    )
    put(units, 0, target=target_fc1, wide=hidden, at_row=0, at_col=0, skip=skip)
    for part in range(hidden // width):
        put(
            units, 1, target=target_fc2, wide=width, at_row=part * rows, at_col=0,
            skip=skip + part * width,
        )


def finish_kernel(rows, levels, plan, factor, *refs):
    idx = refs[0]
    at = 1
    groups = []
    for _ in plan:
        groups.append((refs[at : at + levels], refs[at + levels : at + 2 * levels]))
        at += 2 * levels
    g_qkv, g_proj, g_fc1, g_fc2 = refs[at : at + 4]
    scratch = refs[at + 4 :]
    for (near, far), units, (members, total_wide) in zip(groups, scratch, plan):
        unpack_units(idx, near, far, units)
        for kind, layer, skip in members:
            if kind == "qkv":
                finish_qkv(
                    units, g_qkv.at[layer], g_proj.at[layer], rows, skip, total_wide, factor
                )
            else:
                finish_mlp(units, g_fc1.at[layer], g_fc2.at[layer], rows, skip, total_wide, factor)


def shards(
    latents, condition, cotangent, w_qkv, b_qv, w_proj, b_proj, w_fc1, b_fc1, w_fc2, b_fc2, w_ada,
    b_ada,
):
    layers, rows, _ = w_qkv.shape
    width = w_proj.shape[-1]
    hidden = w_fc1.shape[-1]
    wide = w_ada.shape[-1]
    seq = latents.shape[1]
    n_shard = lax.axis_size("shard")
    n_rep = lax.axis_size("rep")
    levels = n_rep // CORES
    peers = n_shard - 1
    shard_id = lax.axis_index("shard")
    rep_id = lax.axis_index("rep")
    core = rep_id % CORES
    idx = jnp.stack([shard_id, rep_id // CORES, core]).astype(jnp.int32)
    total_latents = latents.shape[0] * n_shard * n_rep
    factor = 1.0 / total_latents

    def exchange(array, by_shard=0, by_level=0, by_core=0):
        moves = []
        for own_shard in range(n_shard):
            for own_rep in range(n_rep):
                peer = (own_shard ^ by_shard) * n_rep + (own_rep ^ (by_level * CORES + by_core))
                moves.append((own_shard * n_rep + own_rep, peer))
        return lax.ppermute(array, ("shard", "rep"), moves)

    def half_qkv(layer):
        other = jnp.concatenate([w_qkv[layer, :, 2 * width :], w_proj[layer]], axis=1)
        return jnp.where(core == 0, w_qkv[layer, :, : 2 * width], other)

    def half_mlp(layer):
        other = jnp.concatenate(
            [w_fc2[layer, part * rows : (part + 1) * rows] for part in range(hidden // width)],
            axis=1,
        )
        return jnp.where(core == 0, w_fc1[layer], other)

    def gather(half):
        near = [exchange(half, by_shard=step) for step in range(1, n_shard)]
        far = [exchange(piece, by_core=1) for piece in near]
        return near, far

    def spread(bias):
        length = bias.shape[0]
        at = lax.broadcasted_iota(jnp.int32, (1, n_shard * length), 1) // length
        return jnp.where(at == shard_id, jnp.tile(bias[None, :], (1, n_shard)), 0).astype(BF)

    small = [condition]
    for layer in range(layers):
        small += [spread(part[layer]) for part in (b_qv, b_proj, b_fc1, b_fc2)]
    small += [spread(b_ada[layer]) for layer in range(layers)]
    small = jnp.concatenate(small, axis=1)

    pieces = [(gather(half_qkv(0)), 0)]
    small_all = [small] + [exchange(small, by_shard=step) for step in range(1, n_shard)]
    mlp_first = gather(half_mlp(0))
    later = [
        gather(jnp.concatenate([half_qkv(layer), half_mlp(layer)], axis=1))
        for layer in range(1, layers)
    ]
    qkv_pieces = pieces + [(item, 0) for item in later]
    mlp_pieces = [(mlp_first, 0)] + [(item, 2 * width) for item in later]

    pad_scratch = [pltpu.VMEM((width, layers * wide), BF), pltpu.SemaphoreType.DMA((layers,))]
    partial = run(
        functools.partial(modulate_kernel, n_shard), "modulate",
        [(idx, "s"), (w_ada, "a")] + [(array, "v") for array in small_all],
        [((1, layers * wide), F32, "v")] * n_shard, pad_scratch, flops=10**7,
    )
    bias_all = sum(array[:, width:].astype(F32) for array in small_all)
    per_layer = 4 * width + hidden
    mod_all = partial[0] + bias_all[:, layers * per_layer :]
    for step in range(1, n_shard):
        mod_all = mod_all + exchange(partial[step], by_shard=step)
    mods = [mod_all[:, layer * wide : (layer + 1) * wide] for layer in range(layers)]
    biases = []
    for layer in range(layers):
        at = layer * per_layer
        cuts = (at, at + 2 * width, at + 3 * width, at + 3 * width + hidden, at + per_layer)
        biases.append([bias_all[:, cuts[part] : cuts[part + 1]] for part in range(4)])

    big = seq * width
    row = lambda kind="v": ((seq, width), F32, kind)

    def piece_args(pair):
        return [(array, "a") for array in pair[0] + pair[1]]

    qkv_sems = pltpu.SemaphoreType.DMA((3 + 2 * peers,))
    mlp_sems = pltpu.SemaphoreType.DMA((1 + hidden // width + 2 * peers,))
    out_sems = pltpu.SemaphoreType.DMA((2 * n_shard,))
    w_qkv_all = pltpu.VMEM((2, width, 2 * width), BF)
    w_mlp_all = pltpu.VMEM((2, width, hidden), BF)

    def grads_out(half_wide):
        return [((n_shard, rows, half_wide), BF, "a")] * 2

    stream = latents[0]
    saved = []
    grad_stream = None
    vec_qkv, vec_mlp = [None] * layers, [None] * layers
    raw = {}
    for layer in range(layers):
        pair, offset = qkv_pieces[layer]
        b_qv_l, b_proj_l, b_fc1_l, b_fc2_l = biases[layer]
        qkv, probs, attended, branch, middle = run(
            functools.partial(attention_forward, layer, rows, offset, peers), "attention_forward",
            [(idx, "s"), (stream, "v"), (mods[layer], "v"), (b_qv_l, "v"), (b_proj_l, "v"),
             (w_qkv, "a"), (w_proj, "a")] + piece_args(pair),
            [((seq, 3 * width), BF, "v"), ((HEADS, seq, seq), F32, "v"), ((seq, width), BF, "v"),
             row(), row()],
            [w_qkv_all, qkv_sems], flops=10 * big * width,
        )
        pair, offset = mlp_pieces[layer]
        entry = dict(stream=stream, qkv=qkv, probs=probs, attended=attended, branch=branch,
                     middle=middle)
        if layer + 1 < layers:
            act_low, slopes, mlp_out, stream = run(
                functools.partial(mlp_forward, layer, rows, offset, peers), "mlp_forward",
                [(idx, "s"), (middle, "v"), (mods[layer], "v"), (b_fc1_l, "v"), (b_fc2_l, "v"),
                 (w_fc1, "a"), (w_fc2, "a")] + piece_args(pair),
                [((seq, hidden), BF, "v"), ((seq, hidden), F32, "v"), row(), row()],
                [w_mlp_all, mlp_sems], flops=16 * big * width,
            )
            entry.update(act_low=act_low, slopes=slopes, mlp_out=mlp_out)
        else:
            x_out, d_middle, vec_mlp[layer], keep, send = run(
                functools.partial(mlp_both, layer, rows, offset, peers), "mlp_both",
                [(idx, "s"), (middle, "v"), (mods[layer], "v"), (b_fc1_l, "v"), (b_fc2_l, "v"),
                 (cotangent[0], "v"), (w_fc1, "a"), (w_fc2, "a")] + piece_args(pair),
                [((seq, width), BF, "v"), row(), ((1, 4 * width + hidden), F32, "v")]
                + grads_out(hidden),
                [w_mlp_all, w_mlp_all, pltpu.VMEM((seq, hidden), BF),
                 pltpu.VMEM((seq, hidden), F32), mlp_sems, out_sems], flops=48 * big * width,
            )
            raw["mlp", layer] = (keep, send)
        saved.append(entry)

    def reduce_group(keys):
        pairs = [raw[key] for key in keys]
        received = [exchange(send, by_core=1) for _, send in pairs]
        total_wide = sum(keep.shape[-1] for keep, _ in pairs)
        summed = run(
            functools.partial(core_sum_kernel, n_shard, len(pairs)), "core_sum",
            [(keep, "v") for keep, _ in pairs] + [(array, "v") for array in received],
            [((rows, total_wide), BF, "v")] * n_shard,
        )
        arrived = [exchange(summed[step], by_shard=step) for step in range(1, n_shard)]
        size = -(-(rows // 16) * (total_wide // 128) // levels)
        chunks = run(
            functools.partial(shard_sum_kernel, n_shard, levels), "shard_sum",
            [(idx, "s"), (summed[0], "v")] + [(array, "v") for array in arrived],
            [((size, 16, 128), BF, "v")] * levels,
            [pltpu.VMEM((size * levels, 16, 128), BF), pltpu.SemaphoreType.DMA((1,))],
        )
        arrived = [exchange(chunks[step], by_level=step) for step in range(1, levels)]
        (total,) = run(
            level_sum_kernel, "level_sum",
            [(chunks[0], "v")] + [(array, "v") for array in arrived],
            [((size, 16, 128), BF, "v")],
        )
        near = [total] + [exchange(total, by_level=step) for step in range(1, levels)]
        far = [exchange(array, by_core=1) for array in near]
        return near, far, total_wide

    plan, finals = [], []
    for layer in reversed(range(layers)):
        entry = saved[layer]
        pair, offset = mlp_pieces[layer]
        if layer + 1 < layers:
            d_middle, vec_mlp[layer], keep, send = run(
                functools.partial(mlp_backward, layer, rows, offset, peers), "mlp_backward",
                [(idx, "s"), (entry["middle"], "v"), (mods[layer], "v"), (grad_stream, "v"),
                 (entry["act_low"], "v"), (entry["slopes"], "v"), (entry["mlp_out"], "v"),
                 (w_fc1, "a"), (w_fc2, "a")] + piece_args(pair),
                [row(), ((1, 4 * width + hidden), F32, "v")] + grads_out(hidden),
                [w_mlp_all, w_mlp_all, mlp_sems, out_sems], flops=32 * big * width,
            )
            raw["mlp", layer] = (keep, send)
            keys = [("qkv", layer + 1), ("mlp", layer)]
        else:
            keys = [("mlp", layer)]
        finals.append(reduce_group(keys))
        plan.append(keys)
        pair, offset = qkv_pieces[layer]
        grad_stream, vec_qkv[layer], keep, send = run(
            functools.partial(attention_backward, layer, rows, offset, peers),
            "attention_backward",
            [(idx, "s"), (entry["stream"], "v"), (mods[layer], "v"), (d_middle, "v"),
             (entry["qkv"], "v"), (entry["probs"], "v"), (entry["attended"], "v"),
             (entry["branch"], "v"), (w_qkv, "a"), (w_proj, "a")] + piece_args(pair),
            [row(), ((1, 6 * width), F32, "v")] + grads_out(2 * width),
            [w_qkv_all, pltpu.VMEM((seq, 3 * width), BF), w_qkv_all, qkv_sems, out_sems],
            flops=28 * big * width,
        )
        raw["qkv", layer] = (keep, send)
    finals.append(reduce_group([("qkv", 0)]))
    plan.append([("qkv", 0)])

    cond_in = condition.astype(F32)
    vector = [jax.nn.silu(cond_in).astype(BF)]
    for layer in range(layers):
        vector += [vec_qkv[layer][:, : 3 * width].astype(BF), vec_mlp[layer][:, : 3 * width].astype(BF)]
    for layer in range(layers):
        vector += [vec_qkv[layer][:, 3 * width :].astype(BF), vec_mlp[layer][:, 3 * width :].astype(BF)]
    vector = jnp.concatenate(vector, axis=1)
    same_shard = [vector] + [exchange(vector, by_level=step) for step in range(1, levels)]
    group = [vector] + [exchange(vector, by_shard=step) for step in range(1, n_shard)]
    packed = jnp.concatenate(same_shard[1:], axis=0)
    packed_all = [packed] + [exchange(packed, by_shard=step) for step in range(1, n_shard)]
    half_rows = jnp.concatenate(group + packed_all, axis=0)
    gathered = jnp.concatenate([half_rows, exchange(half_rows, by_core=1)], axis=0)
    grad_ada, sums = run(
        functools.partial(ada_grad_kernel, rows, wide, factor), "ada_grad",
        [(idx, "s"), (gathered, "v")],
        [((layers, rows, wide), F32, "v"), ((1, vector.shape[1] - width), F32, "v")],
        [pltpu.VMEM((width, total_latents), F32)], flops=10**8,
    )
    d_cond = run(
        functools.partial(condition_back_kernel, n_shard), "condition_back",
        [(idx, "s"), (w_ada, "a")] + [(array, "v") for array in group],
        [((1, width), F32, "v")] * n_shard, pad_scratch, flops=10**7,
    )
    grad_cond = d_cond[0]
    for step in range(1, n_shard):
        grad_cond = grad_cond + exchange(d_cond[step], by_shard=step)
    cond_grad = jax.vjp(jax.nn.silu, cond_in)[1](grad_cond)[0]

    def own_part(parts):
        whole = jnp.concatenate(parts, axis=0)
        length = whole.shape[1] // n_shard
        return lax.dynamic_slice_in_dim(whole, shard_id * length, length, axis=1)

    base = layers * wide
    at = [base + layer * (4 * width + hidden) for layer in range(layers)]
    grad_ada_bias = own_part([sums[:, layer * wide : (layer + 1) * wide] for layer in range(layers)])
    grad_qv_bias = own_part([sums[:, a : a + 2 * width] for a in at])
    grad_proj_bias = own_part([sums[:, a + 2 * width : a + 3 * width] for a in at])
    grad_fc1_bias = own_part([sums[:, a + 3 * width : a + 3 * width + hidden] for a in at])
    grad_fc2_bias = own_part([sums[:, a + 3 * width + hidden : a + 4 * width + hidden] for a in at])

    finish_plan, finish_inputs, finish_scratch = [], [(idx, "s")], []
    for keys, (near, far, total_wide) in zip(plan, finals):
        members, skip = [], 0
        for kind, layer in keys:
            members.append((kind, layer, skip))
            skip += 2 * width if kind == "qkv" else hidden
        finish_plan.append((members, total_wide))
        finish_inputs += [(array, "v") for array in near + far]
        finish_scratch.append(pltpu.VMEM((2, near[0].shape[0] * levels, 16, 128), BF))
    grad_qkv, grad_proj, grad_fc1, grad_fc2 = run(
        functools.partial(finish_kernel, rows, levels, finish_plan, factor), "finish",
        finish_inputs,
        [(array.shape, F32, "v") for array in (w_qkv, w_proj, w_fc1, w_fc2)],
        finish_scratch,
    )
    return (
        x_out[None], grad_stream[None], cond_grad, grad_qkv, grad_qv_bias, grad_proj,
        grad_proj_bias, grad_fc1, grad_fc1_bias, grad_fc2, grad_fc2_bias, grad_ada, grad_ada_bias,
    )


def solution(mesh):
    rows3, rows2 = P(("shard", "rep"), None, None), P(("shard", "rep"), None)
    weight, bias = P(None, "shard", None), P(None, "shard")
    return jax.shard_map(
        shards,
        mesh=mesh,
        in_specs=(rows3, rows2, rows3) + (weight, bias) * 5,
        out_specs=(rows3, rows3, rows2) + (weight, bias) * 5,
        check_vma=False,
    )
```

time: 627 us -> 240 us (0.38)
  waiting for transfers between devices: 367 us -> 77.2 us
  blocking collectives: 126 us -> 0 us
  starting transfers between devices: 0.95 us -> 73.5 us
  matrix products: 59.6 us -> 0 us
  Pallas kernels: 0 us -> 51.5 us
  other arithmetic: 31.8 us -> 7.25 us
  between operations: 20 us -> 1.5 us
  local copies, waits for them, and re-layouts: 20.1 us -> 28.1 us
    reduce_scatter x10 -> x0, waiting for transfers between devices: 260 us -> none  [the longest x2 71.4 us: shards(): lax.psum_scatter(grads[8].astype(jnp.bfloat16), 'shard', scatter_dimensio...]
    ppermute x0 -> x80, waiting for transfers between devices: none -> 77.2 us  [exchange(): return lax.ppermute(array, ('shard', 'rep'), moves)]
    all_gather x6 -> x0, waiting for transfers between devices: 75.3 us -> none  [the longest x2 53.2 us: shards(): lax.all_gather(w_fc2[layer_number], 'shard', axis=0, tiled=True)]
    ppermute x0 -> x80, starting transfers between devices: none -> 73.5 us  [exchange(): return lax.ppermute(array, ('shard', 'rep'), moves)]
    all_gather x6 -> x0, blocking collectives: 67.8 us -> none  [the longest x2 28.9 us: shards(): lax.all_gather(w_qkv[layer_number], 'shard', axis=0, tiled=True)]
    dot_general x40 -> x0, matrix products: 59.6 us -> none  [the longest x8 18.1 us: weight_grad(): jnp.einsum('lsd,lse->de', left, right, preferred_element_type=jnp.float32)]
    pallas_call x0 -> x20, Pallas kernels: none -> 51.5 us  [run(): pl.pallas_call(body, out_shape=[jax.ShapeDtypeStruct(shape, dtype) for sh...]
    unnamed x2 -> x0, blocking collectives: 31.1 us -> none
  transfers between devices with their start and end apart: 17 -> 80, of which waited for: 14 -> 26; matrix products, arithmetic and copies ran while one was open for 13% -> 10% of each run, Pallas kernels for 0% -> 9%
where the time goes in v1:
time: 240 us; the launch traced here: 239 us
  waiting for transfers between devices  77.2 us (32%)
  starting transfers between devices  73.5 us (31%)
  Pallas kernels  51.5 us (21%)
  local copies, waits for them, and re-layouts  28.1 us (12%)
  other arithmetic  7.25 us (3%)
    ppermute x80, waiting for transfers between devices, exchange(): return lax.ppermute(array, ('shard', 'rep'), moves)  77.2 us
    ppermute x80, starting transfers between devices, exchange(): return lax.ppermute(array, ('shard', 'rep'), moves)  73.5 us
    pallas_call x20, Pallas kernels, run(): pl.pallas_call(body, out_shape=[jax.ShapeDtypeStruct(shape, dtype) for sh...  51.5 us
    concatenate x1, local copies, waits for them, and re-layouts, shards(): jnp.concatenate([half_rows, exchange(half_rows, by_core=1)], axis=0)  8.14 us
    concatenate x1, local copies, waits for them, and re-layouts, shards(): half_rows = jnp.concatenate(group + packed_all, axis=0)  7.54 us
    unnamed x77, local copies, waits for them, and re-layouts  6.02 us
  transfers between devices with their start and end apart: 80, of which 26 were waited for; matrix products, arithmetic and copies ran while one was open for 10% of the time, Pallas kernels for 9%

profile of v1, /device:TPU:0, one launch (start us, length us, event | category | flops | bytes accessed | tf_op | source)
XLA Modules:
  0.0 239.0 jit_solution(7693360793145357293)
XLA Ops:
  6.9 3.0 %collective-permute-start = (bf16[1,11136]{1,0:T(2,128)(2,1)S(1)}, bf16[1,11136]{1,0:T(2,128)(2,1)S(1)}, u32[]{:S(2)}, u32[]{:S(2)}) collective-permute-start(bf16[1,11136]{1,0:T(2,128)(2,1)S(1)} %constant_dynamic-update-slice_fusion.refs_2_), channel_id=1, source_target_pairs={{0,8},{1,9},{2,10},{3,11},{4,12},{5,13},{6,14},{7,15},{8,0},{9,1},... | collective-permute-start | bytes 66824 | tf_op jit(solution)/shard_map/ppermute | solution.py:516
  28.7 2.6 %collective-permute-done.6.refs_7_.refs_10_ = bf16[96,768]{1,0:T(8,128)(2,1)S(1)} collective-permute-done((bf16[96,768]{1,0:T(8,128)(2,1)S(1)}, bf16[96,768]{1,0:T(8,128)(2,1)S(1)}, u32[]{:S(2)}, u32[]{:S(2)}) %collective-permute-start.6) | collective-permute-done | bytes 147488 | tf_op jit(solution)/shard_map/ppermute | solution.py:516
  36.5 5.7 %collective-permute-done.14.refs_9_.refs_11_ = bf16[96,1536]{1,0:T(8,128)(2,1)S(1)} collective-permute-done((bf16[96,1536]{1,0:T(8,128)(2,1)S(1)}, bf16[96,1536]{1,0:T(8,128)(2,1)S(1)}, u32[]{:S(2)}, u32[]{:S(2)}) %collective-permute-start.14) | collective-permute-done | bytes 294944 | tf_op jit(solution)/shard_map/ppermute | solution.py:516
  42.2 9.5 %collective-permute-done.18.refs_7_.refs_8_.refs_10_ = bf16[96,2304]{1,0:T(8,128)(2,1)S(1)} collective-permute-done((bf16[96,2304]{1,0:T(8,128)(2,1)S(1)}, bf16[96,2304]{1,0:T(8,128)(2,1)S(1)}, u32[]{:S(2)}, u32[]{:S(2)}) %collective-permute-start.18) | collective-permute-done | bytes 442400 | tf_op jit(solution)/shard_map/ppermute | solution.py:516
  52.2 8.6 %collective-permute-done.20.refs_9_.refs_10_.refs_12_ = bf16[96,2304]{1,0:T(8,128)(2,1)S(1)} collective-permute-done((bf16[96,2304]{1,0:T(8,128)(2,1)S(1)}, bf16[96,2304]{1,0:T(8,128)(2,1)S(1)}, u32[]{:S(2)}, u32[]{:S(2)}) %collective-permute-start.20) | collective-permute-done | bytes 442400 | tf_op jit(solution)/shard_map/ppermute | solution.py:516
  61.2 4.1 %attention_forward.2 = (bf16[256,1152]{1,0:T(8,128)(2,1)S(1)}, f32[6,256,256]{2,1,0:T(8,128)S(1)}, bf16[256,384]{1,0:T(8,128)(2,1)S(1)}, f32[256,384]{1,0:T(8,128)S(1)}, f32[256,384]{1,0:T(8,128)S(1)}) custom-call(s32[3]{0:T(128)S(1)} %pad_add_fusion.refs_0_, bf16[256,384]{1,0:T(8,128)(2,1)S(1)} %bitcast.55, f32[1,2304]{1,0:T(1,128)S(1)} %get-tuple-element.192.refs_2_, ...), custom_call_target="tpu_custom_call" | custom-call | flops 377487360 | bytes 1685004 | tf_op jit(solution)/shard_map/attention_forward/pallas_call | solution.py:68
  65.4 3.7 %mlp_forward.1 = (bf16[256,1536]{1,0:T(8,128)(2,1)S(1)}, f32[256,1536]{1,0:T(8,128)S(1)}, f32[256,384]{1,0:T(8,128)S(1)}, f32[256,384]{1,0:T(8,128)S(1)}) custom-call(s32[3]{0:T(128)S(1)} %pad_add_fusion.refs_0_, f32[256,384]{1,0:T(8,128)S(1)} %get-tuple-element.86.refs_1_, f32[1,2304]{1,0:T(1,128)S(1)} %get-tuple-element.192.refs_2_, ...), custom_call_target="tpu_custom_call" | custom-call | flops 603979776 | bytes 3359244 | tf_op jit(solution)/shard_map/mlp_forward/pallas_call | solution.py:68
  69.1 3.0 %attention_forward.3 = (bf16[256,1152]{1,0:T(8,128)(2,1)S(1)}, f32[6,256,256]{2,1,0:T(8,128)S(1)}, bf16[256,384]{1,0:T(8,128)(2,1)S(1)}, f32[256,384]{1,0:T(8,128)S(1)}, f32[256,384]{1,0:T(8,128)S(1)}) custom-call(s32[3]{0:T(128)S(1)} %pad_add_fusion.refs_0_, f32[256,384]{1,0:T(8,128)S(1)} %get-tuple-element.87.refs_1_, ...), custom_call_target="tpu_custom_call" | custom-call | flops 377487360 | bytes 3651084 | tf_op jit(solution)/shard_map/attention_forward/pallas_call | solution.py:68
  72.1 7.2 %mlp_both.1 = (bf16[256,384]{1,0:T(8,128)(2,1)}, f32[256,384]{1,0:T(8,128)S(1)}, f32[1,3072]{1,0:T(1,128)S(1)}, bf16[4,96,1536]{2,1,0:T(8,128)(2,1)S(1)}, bf16[4,96,1536]{2,1,0:T(8,128)(2,1)S(1)}) custom-call(s32[3]{0:T(128)S(1)} %pad_add_fusion.refs_0_, f32[256,384]{1,0:T(8,128)S(1)} %get-tuple-element.88.refs_1_, ...), custom_call_target="tpu_custom_call" | custom-call | flops 1811939328 | bytes 4440588 | tf_op jit(solution)/shard_map/mlp_both/pallas_call | solution.py:68
  81.3 5.9 %attention_backward.2 = (f32[256,384]{1,0:T(8,128)S(1)}, f32[1,2304]{1,0:T(1,128)S(1)}, bf16[4,96,768]{2,1,0:T(8,128)(2,1)S(1)}, bf16[4,96,768]{2,1,0:T(8,128)(2,1)S(1)}) custom-call(s32[3]{0:T(128)S(1)} %pad_add_fusion.refs_0_, f32[256,384]{1,0:T(8,128)S(1)} %get-tuple-element.87.refs_1_, f32[1,2304]{1,0:T(1,128)S(1)} %get-tuple-element.191.refs_2_, ...), custom_call_target="tpu_custom_call" | custom-call | flops 1056964608 | bytes 6792204 | tf_op jit(solution)/shard_map/attention_backward/pallas_call | solution.py:68
  88.0 4.8 %mlp_backward.1 = (f32[256,384]{1,0:T(8,128)S(1)}, f32[1,3072]{1,0:T(1,128)S(1)}, bf16[4,96,1536]{2,1,0:T(8,128)(2,1)S(1)}, bf16[4,96,1536]{2,1,0:T(8,128)(2,1)S(1)}) custom-call(s32[3]{0:T(128)S(1)} %pad_add_fusion.refs_0_, f32[256,384]{1,0:T(8,128)S(1)} %get-tuple-element.86.refs_1_, f32[1,2304]{1,0:T(1,128)S(1)} %get-tuple-element.192.refs_2_, ...), custom_call_target="tpu_custom_call" | custom-call | flops 1207959552 | bytes 6497292 | tf_op jit(solution)/shard_map/mlp_backward/pallas_call | solution.py:68
  92.8 7.6 %attention_backward.3 = (f32[256,384]{1,0:T(8,128)}, f32[1,2304]{1,0:T(1,128)S(1)}, bf16[4,96,768]{2,1,0:T(8,128)(2,1)S(1)}, bf16[4,96,768]{2,1,0:T(8,128)(2,1)}) custom-call(s32[3]{0:T(128)S(1)} %pad_add_fusion.refs_0_, bf16[256,384]{1,0:T(8,128)(2,1)S(1)} %bitcast.56, f32[1,2304]{1,0:T(1,128)S(1)} %get-tuple-element.192.refs_2_, ...), custom_call_target="tpu_custom_call" | custom-call | flops 1056964608 | bytes 4826124 | tf_op jit(solution)/shard_map/attention_backward/pallas_call | solution.py:68
  102.3 2.6 %collective-permute-start.74 = (bf16[1,11136]{1,0:T(2,128)(2,1)S(1)}, bf16[1,11136]{1,0:T(2,128)(2,1)S(1)}, u32[]{:S(2)}, u32[]{:S(2)}) collective-permute-start(bf16[1,11136]{1,0:T(2,128)(2,1)S(1)} %constant_dynamic-update-slice_fusion.21.refs_2_), channel_id=1, source_target_pairs={{0,4},{1,5},{2,6},{3,7},{4,0},{5,1},{6,2},{7,3},{8,12},{9,13},{10,... | collective-permute-start | bytes 66824 | tf_op jit(solution)/shard_map/ppermute | solution.py:516
  105.7 2.4 %collective-permute-done.74 = bf16[1,11136]{1,0:T(2,128)(2,1)S(1)} collective-permute-done((bf16[1,11136]{1,0:T(2,128)(2,1)S(1)}, bf16[1,11136]{1,0:T(2,128)(2,1)S(1)}, u32[]{:S(2)}, u32[]{:S(2)}) %collective-permute-start.74) | collective-permute-done | bytes 22304 | tf_op jit(solution)/shard_map/ppermute | solution.py:516
  108.1 2.6 %collective-permute-done.75 = bf16[1,11136]{1,0:T(2,128)(2,1)S(1)} collective-permute-done((bf16[1,11136]{1,0:T(2,128)(2,1)S(1)}, bf16[1,11136]{1,0:T(2,128)(2,1)S(1)}, u32[]{:S(2)}, u32[]{:S(2)}) %collective-permute-start.75) | collective-permute-done | bytes 22304 | tf_op jit(solution)/shard_map/ppermute | solution.py:516
  115.9 3.0 %collective-permute-done.25.refs_4_ = bf16[1,11136]{1,0:T(2,128)(2,1)S(1)} collective-permute-done((bf16[1,11136]{1,0:T(2,128)(2,1)S(1)}, bf16[1,11136]{1,0:T(2,128)(2,1)S(1)}, u32[]{:S(2)}, u32[]{:S(2)}) %collective-permute-start.25) | collective-permute-done | bytes 22304 | tf_op jit(solution)/shard_map/ppermute | solution.py:516
  120.3 3.5 %collective-permute-done.26.refs_5_ = bf16[1,11136]{1,0:T(2,128)(2,1)S(1)} collective-permute-done((bf16[1,11136]{1,0:T(2,128)(2,1)S(1)}, bf16[1,11136]{1,0:T(2,128)(2,1)S(1)}, u32[]{:S(2)}, u32[]{:S(2)}) %collective-permute-start.26) | collective-permute-done | bytes 22304 | tf_op jit(solution)/shard_map/ppermute | solution.py:516
  125.1 7.5 %concatenate.95 = bf16[16,11136]{1,0:T(8,128)(2,1)} concatenate(bf16[1,11136]{1,0:T(2,128)(2,1)} %copy-done.11, bf16[1,11136]{1,0:T(2,128)(2,1)S(1)} %collective-permute-done.24.refs_3_, bf16[1,11136]{1,0:T(2,128)(2,1)S(1)} %collective-permute-done.25.refs_4_, bf16[1,11136]{1,0:T(2,128)(2,1)S(1)} %collective-permute-done.26.refs_5_, ...), dimensions={0} | concatenate | bytes 712704 | tf_op jit(solution)/shard_map/concatenate | solution.py:701
  140.7 2.2 collective-permute-start.29
  148.3 8.1 %concatenate.96.refs_1_ = bf16[32,11136]{1,0:T(8,128)(2,1)S(1)} concatenate(bf16[1,11136]{1,0:T(2,128)(2,1)} %copy-done.11, bf16[1,11136]{1,0:T(2,128)(2,1)S(1)} %copy-done.14, bf16[1,11136]{1,0:T(2,128)(2,1)S(1)} %copy-done.16, bf16[1,11136]{1,0:T(2,128)(2,1)S(1)} %copy-done.18, bf16[1,11136]{1,0:T(2,128)(2,1)} %copy-done.23, bf16[1,11136]{1,0:T(2,128)(2,1)} %copy-done.24, ...), dimensions={0} | concatenate | bytes 1425408 | tf_op jit(solution)/shard_map/concatenate | solution.py:702
  156.5 2.2 ada_grad.1
  161.2 3.1 %collective-permute-start.65 = (bf16[9,16,128]{2,1,0:T(8,128)(2,1)S(1)}, bf16[9,16,128]{2,1,0:T(8,128)(2,1)S(1)}, u32[]{:S(2)}, u32[]{:S(2)}) collective-permute-start(bf16[9,16,128]{2,1,0:T(8,128)(2,1)S(1)} %get-tuple-element.144), channel_id=1, source_target_pairs={{0,6},{1,7},{2,4},{3,5},{4,2},{5,3},{6,0},{7,1},{8,14},{9,15},{10,... | collective-permute-start | bytes 110600 | tf_op jit(solution)/shard_map/ppermute | solution.py:516
  173.2 2.7 %collective-permute-done.31.refs_2_ = bf16[96,1536]{1,0:T(8,128)(2,1)S(1)} collective-permute-done((bf16[96,1536]{1,0:T(8,128)(2,1)S(1)}, bf16[96,1536]{1,0:T(8,128)(2,1)S(1)}, u32[]{:S(2)}, u32[]{:S(2)}) %collective-permute-start.31) | collective-permute-done | bytes 294944 | tf_op jit(solution)/shard_map/ppermute | solution.py:516
  177.4 5.8 %collective-permute-done.32.refs_3_ = bf16[96,1536]{1,0:T(8,128)(2,1)S(1)} collective-permute-done((bf16[96,1536]{1,0:T(8,128)(2,1)S(1)}, bf16[96,1536]{1,0:T(8,128)(2,1)S(1)}, u32[]{:S(2)}, u32[]{:S(2)}) %collective-permute-start.32) | collective-permute-done | bytes 294944 | tf_op jit(solution)/shard_map/ppermute | solution.py:516
  188.5 3.2 %collective-permute-done.46.refs_2_ = bf16[96,2304]{1,0:T(8,128)(2,1)S(1)} collective-permute-done((bf16[96,2304]{1,0:T(8,128)(2,1)S(1)}, bf16[96,2304]{1,0:T(8,128)(2,1)S(1)}, u32[]{:S(2)}, u32[]{:S(2)}) %collective-permute-start.46) | collective-permute-done | bytes 442400 | tf_op jit(solution)/shard_map/ppermute | solution.py:516
  193.0 8.0 %collective-permute-done.48.refs_4_ = bf16[96,2304]{1,0:T(8,128)(2,1)S(1)} collective-permute-done((bf16[96,2304]{1,0:T(8,128)(2,1)S(1)}, bf16[96,2304]{1,0:T(8,128)(2,1)S(1)}, u32[]{:S(2)}, u32[]{:S(2)}) %collective-permute-start.48) | collective-permute-done | bytes 442400 | tf_op jit(solution)/shard_map/ppermute | solution.py:516
  203.6 4.1 %collective-permute-start.50 = (bf16[27,16,128]{2,1,0:T(8,128)(2,1)S(1)}, bf16[27,16,128]{2,1,0:T(8,128)(2,1)S(1)}, u32[]{:S(2)}, u32[]{:S(2)}) collective-permute-start(bf16[27,16,128]{2,1,0:T(8,128)(2,1)S(1)} %get-tuple-element.133), channel_id=1, source_target_pairs={{0,4},{1,5},{2,6},{3,7},{4,0},{5,1},{6,2},{7,3},{8,12},{9,13},{10,... | collective-permute-start | bytes 331784 | tf_op jit(solution)/shard_map/ppermute | solution.py:516
  212.9 3.6 %collective-permute-done.50.refs_2_ = bf16[27,16,128]{2,1,0:T(8,128)(2,1)S(1)} collective-permute-done((bf16[27,16,128]{2,1,0:T(8,128)(2,1)S(1)}, bf16[27,16,128]{2,1,0:T(8,128)(2,1)S(1)}, u32[]{:S(2)}, u32[]{:S(2)}) %collective-permute-start.50) | collective-permute-done | bytes 110624 | tf_op jit(solution)/shard_map/ppermute | solution.py:516
  216.5 3.8 %collective-permute-start.39 = (bf16[18,16,128]{2,1,0:T(8,128)(2,1)S(1)}, bf16[18,16,128]{2,1,0:T(8,128)(2,1)S(1)}, u32[]{:S(2)}, u32[]{:S(2)}) collective-permute-start(bf16[18,16,128]{2,1,0:T(8,128)(2,1)S(1)} %level_sum.3.refs_1_), channel_id=1, source_target_pairs={{0,6},{1,7},{2,4},{3,5},{4,2},{5,3},{6,0},{7,1},{8,14},{9,15},{10,... | collective-permute-start | bytes 221192 | tf_op jit(solution)/shard_map/ppermute | solution.py:516
  225.6 2.2 collective-permute-start.54
  230.3 4.7 %collective-permute-done.53.refs_11_ = bf16[27,16,128]{2,1,0:T(8,128)(2,1)S(1)} collective-permute-done((bf16[27,16,128]{2,1,0:T(8,128)(2,1)S(1)}, bf16[27,16,128]{2,1,0:T(8,128)(2,1)S(1)}, u32[]{:S(2)}, u32[]{:S(2)}) %collective-permute-start.53) | collective-permute-done | bytes 110624 | tf_op jit(solution)/shard_map/ppermute | solution.py:516
  236.5 2.5 %finish.1 = (f32[2,96,1152]{2,1,0:T(8,128)}, f32[2,96,384]{2,1,0:T(8,128)}, f32[2,96,1536]{2,1,0:T(8,128)}, f32[2,384,384]{2,1,0:T(8,128)}) custom-call(s32[3]{0:T(128)S(1)} %pad_add_fusion.refs_0_, bf16[18,16,128]{2,1,0:T(8,128)(2,1)S(1)} %level_sum.3.refs_1_, bf16[18,16,128]{2,1,0:T(8,128)(2,1)S(1)} %collective-permute-done.37.refs_2_, ...), custom_call_target="tpu_custom_call" | custom-call | bytes 1769484 | tf_op jit(solution)/shard_map/finish/pallas_call | solution.py:68
  (306 shorter events, 94.1 us)
Async XLA Ops:
  13.6 14.6 %collective-permute-start.7 = (bf16[96,768]{1,0:T(8,128)(2,1)S(1)}, bf16[96,768]{1,0:T(8,128)(2,1)S(1)}, u32[]{:S(2)}, u32[]{:S(2)}) collective-permute-start(bf16[96,768]{1,0:T(8,128)(2,1)S(1)} %get-tuple-element.168), channel_id=1, source_target_pairs={{0,16},{1,17},{2,18},{3,19},{4,20},{5,21},{6,22},{7,23},{8,24},{9,... | collective-permute-start | bytes 442376 | tf_op jit(solution)/shard_map/ppermute | solution.py:516
  15.6 12.6 %collective-permute-start.8 = (bf16[96,768]{1,0:T(8,128)(2,1)S(1)}, bf16[96,768]{1,0:T(8,128)(2,1)S(1)}, u32[]{:S(2)}, u32[]{:S(2)}) collective-permute-start(bf16[96,768]{1,0:T(8,128)(2,1)S(1)} %get-tuple-element.168), channel_id=1, source_target_pairs={{0,24},{1,25},{2,26},{3,27},{4,28},{5,29},{6,30},{7,31},{8,16},{9,... | collective-permute-start | bytes 442376 | tf_op jit(solution)/shard_map/ppermute | solution.py:516
  32.9 18.7 %collective-permute-start.18 = (bf16[96,2304]{1,0:T(8,128)(2,1)S(1)}, bf16[96,2304]{1,0:T(8,128)(2,1)S(1)}, u32[]{:S(2)}, u32[]{:S(2)}) collective-permute-start(bf16[96,2304]{1,0:T(8,128)(2,1)S(1)} %pad_maximum_fusion), channel_id=1, source_target_pairs={{0,8},{1,9},{2,10},{3,11},{4,12},{5,13},{6,14},{7,15},{8,0},{9,1},... | collective-permute-start | bytes 1327112 | tf_op jit(solution)/shard_map/ppermute | solution.py:516
  34.3 17.3 %collective-permute-start.19 = (bf16[96,2304]{1,0:T(8,128)(2,1)S(1)}, bf16[96,2304]{1,0:T(8,128)(2,1)S(1)}, u32[]{:S(2)}, u32[]{:S(2)}) collective-permute-start(bf16[96,2304]{1,0:T(8,128)(2,1)S(1)} %pad_maximum_fusion), channel_id=1, source_target_pairs={{0,16},{1,17},{2,18},{3,19},{4,20},{5,21},{6,22},{7,23},{8,24},{9,... | collective-permute-start | bytes 1327112 | tf_op jit(solution)/shard_map/ppermute | solution.py:516
  34.9 25.8 %collective-permute-start.20 = (bf16[96,2304]{1,0:T(8,128)(2,1)S(1)}, bf16[96,2304]{1,0:T(8,128)(2,1)S(1)}, u32[]{:S(2)}, u32[]{:S(2)}) collective-permute-start(bf16[96,2304]{1,0:T(8,128)(2,1)S(1)} %pad_maximum_fusion), channel_id=1, source_target_pairs={{0,24},{1,25},{2,26},{3,27},{4,28},{5,29},{6,30},{7,31},{8,16},{9,... | collective-permute-start | bytes 1327112 | tf_op jit(solution)/shard_map/ppermute | solution.py:516
  36.4 24.3 %collective-permute-start.15 = (bf16[96,1536]{1,0:T(8,128)(2,1)S(1)}, bf16[96,1536]{1,0:T(8,128)(2,1)S(1)}, u32[]{:S(2)}, u32[]{:S(2)}) collective-permute-start(bf16[96,1536]{1,0:T(8,128)(2,1)S(1)} %collective-permute-done.12.refs_7_.refs_9_), channel_id=1, source_target_pairs={{0,1},{1,0},{2,3},{3,2},{4,5},{5,4},{6,7},{7,6},{8,9},{9,8},{10,11... | collective-permute-start | bytes 884744 | tf_op jit(solution)/shard_map/ppermute | solution.py:516
  42.2 23.2 %collective-permute-start.16 = (bf16[96,1536]{1,0:T(8,128)(2,1)S(1)}, bf16[96,1536]{1,0:T(8,128)(2,1)S(1)}, u32[]{:S(2)}, u32[]{:S(2)}) collective-permute-start(bf16[96,1536]{1,0:T(8,128)(2,1)S(1)} %collective-permute-done.13.refs_8_.refs_10_), channel_id=1, source_target_pairs={{0,1},{1,0},{2,3},{3,2},{4,5},{5,4},{6,7},{7,6},{8,9},{9,8},{10,11... | collective-permute-start | bytes 884744 | tf_op jit(solution)/shard_map/ppermute | solution.py:516
  51.6 13.7 %collective-permute-start.17 = (bf16[96,1536]{1,0:T(8,128)(2,1)S(1)}, bf16[96,1536]{1,0:T(8,128)(2,1)S(1)}, u32[]{:S(2)}, u32[]{:S(2)}) collective-permute-start(bf16[96,1536]{1,0:T(8,128)(2,1)S(1)} %collective-permute-done.14.refs_9_.refs_11_), channel_id=1, source_target_pairs={{0,1},{1,0},{2,3},{3,2},{4,5},{5,4},{6,7},{7,6},{8,9},{9,8},{10,11... | collective-permute-start | bytes 884744 | tf_op jit(solution)/shard_map/ppermute | solution.py:516
  51.7 17.4 %collective-permute-start.21 = (bf16[96,2304]{1,0:T(8,128)(2,1)S(1)}, bf16[96,2304]{1,0:T(8,128)(2,1)S(1)}, u32[]{:S(2)}, u32[]{:S(2)}) collective-permute-start(bf16[96,2304]{1,0:T(8,128)(2,1)S(1)} %collective-permute-done.18.refs_7_.refs_8_.refs_10_), channel_id=1, source_target_pairs={{0,1},{1,0},{2,3},{3,2},{4,5},{5,4},{6,7},{7,6},{8,9},{9,8},{10,11... | collective-permute-start | bytes 1327112 | tf_op jit(solution)/shard_map/ppermute | solution.py:516
  105.7 35.0 %collective-permute-start.59 = (bf16[4,96,768]{2,1,0:T(8,128)(2,1)}, bf16[4,96,768]{2,1,0:T(8,128)(2,1)S(1)}, u32[]{:S(2)}, u32[]{:S(2)}) collective-permute-start(bf16[4,96,768]{2,1,0:T(8,128)(2,1)} %get-tuple-element.136), channel_id=1, source_target_pairs={{0,1},{1,0},{2,3},{3,2},{4,5},{5,4},{6,7},{7,6},{8,9},{9,8},{10,11... | collective-permute-start | bytes 1769480 | tf_op jit(solution)/shard_map/ppermute | solution.py:516
  110.9 12.9 %collective-permute-start.76 = (bf16[3,11136]{1,0:T(4,128)(2,1)S(1)}, bf16[3,11136]{1,0:T(4,128)(2,1)S(1)}, u32[]{:S(2)}, u32[]{:S(2)}) collective-permute-start(bf16[3,11136]{1,0:T(4,128)(2,1)S(1)} %pad_maximum_fusion.1), channel_id=1, source_target_pairs={{0,8},{1,9},{2,10},{3,11},{4,12},{5,13},{6,14},{7,15},{8,0},{9,1},... | collective-permute-start | bytes 200456 | tf_op jit(solution)/shard_map/ppermute | solution.py:516
  111.6 12.9 %collective-permute-start.77 = (bf16[3,11136]{1,0:T(4,128)(2,1)S(1)}, bf16[3,11136]{1,0:T(4,128)(2,1)S(1)}, u32[]{:S(2)}, u32[]{:S(2)}) collective-permute-start(bf16[3,11136]{1,0:T(4,128)(2,1)S(1)} %pad_maximum_fusion.1), channel_id=1, source_target_pairs={{0,16},{1,17},{2,18},{3,19},{4,20},{5,21},{6,22},{7,23},{8,24},{9,... | collective-permute-start | bytes 200456 | tf_op jit(solution)/shard_map/ppermute | solution.py:516
  112.9 12.1 %collective-permute-start.78 = (bf16[3,11136]{1,0:T(4,128)(2,1)S(1)}, bf16[3,11136]{1,0:T(4,128)(2,1)}, u32[]{:S(2)}, u32[]{:S(2)}) collective-permute-start(bf16[3,11136]{1,0:T(4,128)(2,1)S(1)} %pad_maximum_fusion.1), channel_id=1, source_target_pairs={{0,24},{1,25},{2,26},{3,27},{4,28},{5,29},{6,30},{7,31},{8,16},{9,... | collective-permute-start | bytes 200456 | tf_op jit(solution)/shard_map/ppermute | solution.py:516
  132.6 13.6 %collective-permute-start.79 = (bf16[16,11136]{1,0:T(8,128)(2,1)}, bf16[16,11136]{1,0:T(8,128)(2,1)}, u32[]{:S(2)}, u32[]{:S(2)}) collective-permute-start(bf16[16,11136]{1,0:T(8,128)(2,1)} %concatenate.95), channel_id=1, source_target_pairs={{0,1},{1,0},{2,3},{3,2},{4,5},{5,4},{6,7},{7,6},{8,9},{9,8},{10,11... | collective-permute-start | bytes 1069064 | tf_op jit(solution)/shard_map/ppermute | solution.py:516
  132.6 28.5 %collective-permute-start.30 = (bf16[4,96,1536]{2,1,0:T(8,128)(2,1)}, bf16[4,96,1536]{2,1,0:T(8,128)(2,1)}, u32[]{:S(2)}, u32[]{:S(2)}) collective-permute-start(bf16[4,96,1536]{2,1,0:T(8,128)(2,1)} %copy-done.20), channel_id=1, source_target_pairs={{0,1},{1,0},{2,3},{3,2},{4,5},{5,4},{6,7},{7,6},{8,9},{9,8},{10,11... | collective-permute-start | bytes 3538952 | tf_op jit(solution)/shard_map/ppermute | solution.py:516
  133.1 34.8 %collective-permute-start.45 = (bf16[4,96,1536]{2,1,0:T(8,128)(2,1)}, bf16[4,96,1536]{2,1,0:T(8,128)(2,1)}, u32[]{:S(2)}, u32[]{:S(2)}) collective-permute-start(bf16[4,96,1536]{2,1,0:T(8,128)(2,1)} %copy-done.19), channel_id=1, source_target_pairs={{0,1},{1,0},{2,3},{3,2},{4,5},{5,4},{6,7},{7,6},{8,9},{9,8},{10,11... | collective-permute-start | bytes 3538952 | tf_op jit(solution)/shard_map/ppermute | solution.py:516
  143.7 15.0 %collective-permute-start.60 = (bf16[96,768]{1,0:T(8,128)(2,1)}, bf16[96,768]{1,0:T(8,128)(2,1)S(1)}, u32[]{:S(2)}, u32[]{:S(2)}) collective-permute-start(bf16[96,768]{1,0:T(8,128)(2,1)} %get-tuple-element.138), channel_id=1, source_target_pairs={{0,8},{1,9},{2,10},{3,11},{4,12},{5,13},{6,14},{7,15},{8,0},{9,1},... | collective-permute-start | bytes 442376 | tf_op jit(solution)/shard_map/ppermute | solution.py:516
  145.3 13.4 %collective-permute-start.61 = (bf16[96,768]{1,0:T(8,128)(2,1)}, bf16[96,768]{1,0:T(8,128)(2,1)}, u32[]{:S(2)}, u32[]{:S(2)}) collective-permute-start(bf16[96,768]{1,0:T(8,128)(2,1)} %get-tuple-element.139), channel_id=1, source_target_pairs={{0,16},{1,17},{2,18},{3,19},{4,20},{5,21},{6,22},{7,23},{8,24},{9,... | collective-permute-start | bytes 442376 | tf_op jit(solution)/shard_map/ppermute | solution.py:516
  146.2 12.5 %collective-permute-start.62 = (bf16[96,768]{1,0:T(8,128)(2,1)}, bf16[96,768]{1,0:T(8,128)(2,1)}, u32[]{:S(2)}, u32[]{:S(2)}) collective-permute-start(bf16[96,768]{1,0:T(8,128)(2,1)} %get-tuple-element.140), channel_id=1, source_target_pairs={{0,24},{1,25},{2,26},{3,27},{4,28},{5,29},{6,30},{7,31},{8,16},{9,... | collective-permute-start | bytes 442376 | tf_op jit(solution)/shard_map/ppermute | solution.py:516
  167.0 16.2 %collective-permute-start.32 = (bf16[96,1536]{1,0:T(8,128)(2,1)S(1)}, bf16[96,1536]{1,0:T(8,128)(2,1)S(1)}, u32[]{:S(2)}, u32[]{:S(2)}) collective-permute-start(bf16[96,1536]{1,0:T(8,128)(2,1)S(1)} %get-tuple-element.117), channel_id=1, source_target_pairs={{0,16},{1,17},{2,18},{3,19},{4,20},{5,21},{6,22},{7,23},{8,24},{9,... | collective-permute-start | bytes 884744 | tf_op jit(solution)/shard_map/ppermute | solution.py:516
  168.0 15.4 %collective-permute-start.33 = (bf16[96,1536]{1,0:T(8,128)(2,1)S(1)}, bf16[96,1536]{1,0:T(8,128)(2,1)S(1)}, u32[]{:S(2)}, u32[]{:S(2)}) collective-permute-start(bf16[96,1536]{1,0:T(8,128)(2,1)S(1)} %get-tuple-element.118), channel_id=1, source_target_pairs={{0,24},{1,25},{2,26},{3,27},{4,28},{5,29},{6,30},{7,31},{8,16},{9,... | collective-permute-start | bytes 884744 | tf_op jit(solution)/shard_map/ppermute | solution.py:516
  171.2 20.6 %collective-permute-start.46 = (bf16[96,2304]{1,0:T(8,128)(2,1)S(1)}, bf16[96,2304]{1,0:T(8,128)(2,1)S(1)}, u32[]{:S(2)}, u32[]{:S(2)}) collective-permute-start(bf16[96,2304]{1,0:T(8,128)(2,1)S(1)} %get-tuple-element.128), channel_id=1, source_target_pairs={{0,8},{1,9},{2,10},{3,11},{4,12},{5,13},{6,14},{7,15},{8,0},{9,1},... | collective-permute-start | bytes 1327112 | tf_op jit(solution)/shard_map/ppermute | solution.py:516
  172.3 19.8 %collective-permute-start.47 = (bf16[96,2304]{1,0:T(8,128)(2,1)S(1)}, bf16[96,2304]{1,0:T(8,128)(2,1)S(1)}, u32[]{:S(2)}, u32[]{:S(2)}) collective-permute-start(bf16[96,2304]{1,0:T(8,128)(2,1)S(1)} %get-tuple-element.129), channel_id=1, source_target_pairs={{0,16},{1,17},{2,18},{3,19},{4,20},{5,21},{6,22},{7,23},{8,24},{9,... | collective-permute-start | bytes 1327112 | tf_op jit(solution)/shard_map/ppermute | solution.py:516
  175.9 25.1 %collective-permute-start.48 = (bf16[96,2304]{1,0:T(8,128)(2,1)S(1)}, bf16[96,2304]{1,0:T(8,128)(2,1)S(1)}, u32[]{:S(2)}, u32[]{:S(2)}) collective-permute-start(bf16[96,2304]{1,0:T(8,128)(2,1)S(1)} %get-tuple-element.130), channel_id=1, source_target_pairs={{0,24},{1,25},{2,26},{3,27},{4,28},{5,29},{6,30},{7,31},{8,16},{9,... | collective-permute-start | bytes 1327112 | tf_op jit(solution)/shard_map/ppermute | solution.py:516
  187.2 15.8 %collective-permute-start.68 = (bf16[9,16,128]{2,1,0:T(8,128)(2,1)S(1)}, bf16[9,16,128]{2,1,0:T(8,128)(2,1)S(1)}, u32[]{:S(2)}, u32[]{:S(2)}) collective-permute-start(bf16[9,16,128]{2,1,0:T(8,128)(2,1)S(1)} %level_sum.5.refs_17_), channel_id=1, source_target_pairs={{0,6},{1,7},{2,4},{3,5},{4,2},{5,3},{6,0},{7,1},{8,14},{9,15},{10,... | collective-permute-start | bytes 110600 | tf_op jit(solution)/shard_map/ppermute | solution.py:516
  188.5 14.5 %collective-permute-start.69 = (bf16[9,16,128]{2,1,0:T(8,128)(2,1)S(1)}, bf16[9,16,128]{2,1,0:T(8,128)(2,1)S(1)}, u32[]{:S(2)}, u32[]{:S(2)}) collective-permute-start(bf16[9,16,128]{2,1,0:T(8,128)(2,1)S(1)} %level_sum.5.refs_17_), channel_id=1, source_target_pairs={{0,1},{1,0},{2,3},{3,2},{4,5},{5,4},{6,7},{7,6},{8,9},{9,8},{10,11... | collective-permute-start | bytes 110600 | tf_op jit(solution)/shard_map/ppermute | solution.py:516
  191.8 11.8 %collective-permute-start.34 = (bf16[18,16,128]{2,1,0:T(8,128)(2,1)S(1)}, bf16[18,16,128]{2,1,0:T(8,128)(2,1)S(1)}, u32[]{:S(2)}, u32[]{:S(2)}) collective-permute-start(bf16[18,16,128]{2,1,0:T(8,128)(2,1)S(1)} %get-tuple-element.120), channel_id=1, source_target_pairs={{0,2},{1,3},{2,0},{3,1},{4,6},{5,7},{6,4},{7,5},{8,10},{9,11},{10,... | collective-permute-start | bytes 221192 | tf_op jit(solution)/shard_map/ppermute | solution.py:516
  203.6 13.0 %collective-permute-start.50 = (bf16[27,16,128]{2,1,0:T(8,128)(2,1)S(1)}, bf16[27,16,128]{2,1,0:T(8,128)(2,1)S(1)}, u32[]{:S(2)}, u32[]{:S(2)}) collective-permute-start(bf16[27,16,128]{2,1,0:T(8,128)(2,1)S(1)} %get-tuple-element.133), channel_id=1, source_target_pairs={{0,4},{1,5},{2,6},{3,7},{4,0},{5,1},{6,2},{7,3},{8,12},{9,13},{10,... | collective-permute-start | bytes 331784 | tf_op jit(solution)/shard_map/ppermute | solution.py:516
  207.7 12.7 %collective-permute-start.51 = (bf16[27,16,128]{2,1,0:T(8,128)(2,1)S(1)}, bf16[27,16,128]{2,1,0:T(8,128)(2,1)S(1)}, u32[]{:S(2)}, u32[]{:S(2)}) collective-permute-start(bf16[27,16,128]{2,1,0:T(8,128)(2,1)S(1)} %get-tuple-element.134), channel_id=1, source_target_pairs={{0,6},{1,7},{2,4},{3,5},{4,2},{5,3},{6,0},{7,1},{8,14},{9,15},{10,... | collective-permute-start | bytes 331784 | tf_op jit(solution)/shard_map/ppermute | solution.py:516
  208.7 14.7 %collective-permute-start.72 = (bf16[9,16,128]{2,1,0:T(8,128)(2,1)S(1)}, bf16[9,16,128]{2,1,0:T(8,128)(2,1)S(1)}, u32[]{:S(2)}, u32[]{:S(2)}) collective-permute-start(bf16[9,16,128]{2,1,0:T(8,128)(2,1)S(1)} %collective-permute-done.68.refs_20_), channel_id=1, source_target_pairs={{0,1},{1,0},{2,3},{3,2},{4,5},{5,4},{6,7},{7,6},{8,9},{9,8},{10,11... | collective-permute-start | bytes 110600 | tf_op jit(solution)/shard_map/ppermute | solution.py:516
  208.7 12.3 %collective-permute-start.37 = (bf16[18,16,128]{2,1,0:T(8,128)(2,1)S(1)}, bf16[18,16,128]{2,1,0:T(8,128)(2,1)S(1)}, u32[]{:S(2)}, u32[]{:S(2)}) collective-permute-start(bf16[18,16,128]{2,1,0:T(8,128)(2,1)S(1)} %level_sum.3.refs_1_), channel_id=1, source_target_pairs={{0,2},{1,3},{2,0},{3,1},{4,6},{5,7},{6,4},{7,5},{8,10},{9,11},{10,... | collective-permute-start | bytes 221192 | tf_op jit(solution)/shard_map/ppermute | solution.py:516
  211.2 12.2 %collective-permute-start.38 = (bf16[18,16,128]{2,1,0:T(8,128)(2,1)S(1)}, bf16[18,16,128]{2,1,0:T(8,128)(2,1)S(1)}, u32[]{:S(2)}, u32[]{:S(2)}) collective-permute-start(bf16[18,16,128]{2,1,0:T(8,128)(2,1)S(1)} %level_sum.3.refs_1_), channel_id=1, source_target_pairs={{0,4},{1,5},{2,6},{3,7},{4,0},{5,1},{6,2},{7,3},{8,12},{9,13},{10,... | collective-permute-start | bytes 221192 | tf_op jit(solution)/shard_map/ppermute | solution.py:516
  (77 other events, 750.8 us)

commit v2 on v1

v2 whole, which is shorter than its diff:
```python
import functools

import jax
import jax.numpy as jnp
from jax import lax
from jax.experimental import pallas as pl
from jax.experimental.pallas import tpu as pltpu
from jax.sharding import PartitionSpec as P

HEADS = 6
BF = jnp.bfloat16
F32 = jnp.float32
CORES = 2
VMEM_LIMIT = 40 * 1024 * 1024


def dot(left, right):
    return jnp.dot(left, right, preferred_element_type=F32)


def dot_nt(left, right):
    return lax.dot_general(left, right, (((1,), (1,)), ((), ())), preferred_element_type=F32)


def dot_tn(left, right):
    return lax.dot_general(left, right, (((0,), (0,)), ((), ())), preferred_element_type=F32)


def layer_norm(rows):
    center = rows - jnp.mean(rows, axis=-1, keepdims=True)
    inverse = lax.rsqrt(jnp.mean(center * center, axis=-1, keepdims=True) + 1e-06)
    return center * inverse, inverse


def norm_back(grad_norm, normed, inverse):
    centered = grad_norm - jnp.mean(grad_norm, axis=-1, keepdims=True)
    return inverse * (centered - normed * jnp.mean(grad_norm * normed, axis=-1, keepdims=True))


def col_sum(rows):
    return jnp.sum(rows, axis=0, keepdims=True)


def block_at(start, size):
    return pl.ds(pl.multiple_of(start, size), size)


def start_all(copies):
    for copy in copies:
        copy.start()


def wait_all(copies):
    for copy in copies:
        copy.wait()


def make_copies(pairs, sems):
    return [
        pltpu.make_async_copy(source, target, sems.at[slot])
        for slot, (source, target) in enumerate(pairs)
    ]


def run(body, name, inputs, outputs, scratch=(), flops=0):
    places = {"v": pltpu.VMEM, "a": pl.ANY, "s": pltpu.SMEM}
    moved = sum(arr.size * arr.dtype.itemsize for arr, _ in inputs)
    return pl.pallas_call(
        body,
        out_shape=[jax.ShapeDtypeStruct(shape, dtype) for shape, dtype, _ in outputs],
        in_specs=[pl.BlockSpec(memory_space=places[kind]) for _, kind in inputs],
        out_specs=[pl.BlockSpec(memory_space=places[kind]) for _, _, kind in outputs],
        scratch_shapes=list(scratch),
        compiler_params=pltpu.CompilerParams(vmem_limit_bytes=VMEM_LIMIT),
        cost_estimate=pl.CostEstimate(flops=1, bytes_accessed=1, transcendentals=0),
        name=name,
    )(*[arr for arr, _ in inputs])


def pack_kernel(plan, *refs):
    w_qkv, w_proj, w_fc1, w_fc2 = refs[:4]
    outs, sems = refs[4:-1], refs[-1]
    rows, width = w_proj.shape[1:]
    hidden = w_fc1.shape[-1]
    pairs = []
    for (layer, kinds), out in zip(plan, outs):
        at = 0
        pieces = {"qkv": [w_qkv.at[layer, :, : 2 * width]], "mlp": [w_fc1.at[layer]]}
        second = {
            "qkv": [w_qkv.at[layer, :, 2 * width :], w_proj.at[layer]],
            "mlp": [
                w_fc2.at[layer, part * rows : (part + 1) * rows]
                for part in range(hidden // width)
            ],
        }
        for half in (pieces, second):
            for kind in kinds:
                for piece in half[kind]:
                    pairs.append((piece, out.at[:, at : at + piece.shape[-1]]))
                    at += piece.shape[-1]
    copies = make_copies(pairs, sems)
    start_all(copies)
    wait_all(copies)


def piece_count(shards):
    return 2 if shards == 4 else shards - 1


def peer_order(shards, core):
    if shards != 4:
        return list(range(shards))
    return [0, 2 - core, 1 + core, 3]


def qkv_pairs(idx, layer, rows, offset, w_qkv, w_proj, near, far, w_all):
    width = w_proj.shape[-1]
    own = block_at(idx[0] * rows, rows)
    pairs = [
        (w_qkv.at[layer, :, : 2 * width], w_all.at[0, own, :]),
        (w_qkv.at[layer, :, 2 * width :], w_all.at[1, own, :width]),
        (w_proj.at[layer], w_all.at[1, own, width:]),
    ]
    return pairs + piece_pairs(idx, rows, offset, 2 * width, near, far, w_all)


def mlp_pairs(idx, layer, rows, offset, w_fc1, w_fc2, near, far, w_all):
    width = w_fc2.shape[-1]
    hidden = w_fc1.shape[-1]
    own = block_at(idx[0] * rows, rows)
    pairs = [(w_fc1.at[layer], w_all.at[0, own, :])]
    for part in range(hidden // width):
        pairs.append(
            (
                w_fc2.at[layer, part * rows : (part + 1) * rows, :],
                w_all.at[1, own, part * width : (part + 1) * width],
            )
        )
    return pairs + piece_pairs(idx, rows, offset, hidden, near, far, w_all)


def piece_pairs(idx, rows, offset, wide, near, far, w_all):
    pairs = []
    shards = w_all.shape[1] // rows
    for pieces, core in ((near, idx[2]), (far, 1 - idx[2])):
        for slot, piece in enumerate(pieces):
            if shards != 4:
                mask, halves = slot + 1, [(core, 0)]
            elif slot == 0:
                mask, halves = 1 + core, [(0, 0), (1, piece.shape[1] // 2)]
            else:
                mask, halves = 3, [(core, 0)]
            place = block_at(jnp.bitwise_xor(idx[0], mask) * rows, rows)
            for half, first in halves:
                at = first + offset
                pairs.append((piece.at[:, at : at + wide], w_all.at[half, place, :]))
    return pairs


def grad_pairs(idx, rows, shards, grad_all, keep, send):
    pairs = []
    for slot in range(shards):
        for target, core in ((keep, idx[2]), (send, 1 - idx[2])):
            mask = peer_order(shards, core)[slot]
            place = block_at(jnp.bitwise_xor(idx[0], mask) * rows, rows)
            pairs.append((grad_all.at[core, place, :], target.at[slot]))
    return pairs


def fc2_chunk(w_all, rows, chunk):
    width = w_all.shape[1]
    parts = w_all.shape[2] // width
    blocks = []
    for number in range(chunk * width // rows, (chunk + 1) * width // rows):
        at, part = number // parts, number % parts
        blocks.append(w_all[1, at * rows : (at + 1) * rows, part * width : (part + 1) * width])
    return jnp.concatenate(blocks, axis=0)


def attention_forward(layer, rows, offset, shards, *refs):
    peers = piece_count(shards)
    idx, stream, mod_all, w_qkv, w_proj = refs[:5]
    near, far = refs[5 : 5 + peers], refs[5 + peers : 5 + 2 * peers]
    qkv_out, probs_out, attended_out, branch_out, middle_out, w_all, sems = refs[5 + 2 * peers :]
    mod = mod_all.at[layer : layer + 1]
    copies = make_copies(
        qkv_pairs(idx, layer, rows, offset, w_qkv, w_proj, near, far, w_all), sems
    )
    start_all(copies)
    width = stream.shape[-1]
    head = width // HEADS
    b_qv, b_proj = mod[:, 6 * width : 8 * width], mod[:, 8 * width : 9 * width]
    values = stream[...].astype(F32)
    shift, scale, gate = (mod[:, part * width : (part + 1) * width] for part in range(3))
    normed, _ = layer_norm(values)
    h_one = (normed * (1.0 + scale) + shift).astype(BF)
    wait_all(copies)
    mixed = dot(h_one, w_all[0])
    qkv_out[:, :width] = (mixed[:, :width] + b_qv[:, :width]).astype(BF)
    qkv_out[:, width : 2 * width] = mixed[:, width:].astype(BF)
    qkv_out[:, 2 * width :] = (dot(h_one, w_all[1, :, :width]) + b_qv[:, width:]).astype(BF)
    lane = lax.broadcasted_iota(jnp.int32, (1, 2 * head), 1)
    masks = [(lane < head).astype(BF), (lane >= head).astype(BF)]
    for pair in range(HEADS // 2):
        at = pair * 2 * head
        queries = qkv_out[:, at : at + 2 * head]
        keys = qkv_out[:, width + at : width + at + 2 * head]
        vals = qkv_out[:, 2 * width + at : 2 * width + at + 2 * head]
        attended = 0.0
        for side in range(2):
            scores = dot_nt(queries, keys * masks[side]) * head ** (-0.5)
            raised = jnp.exp(scores - jnp.max(scores, axis=-1, keepdims=True))
            probs = raised * (1.0 / jnp.sum(raised, axis=-1, keepdims=True))
            probs_out[2 * pair + side] = probs
            attended = attended + dot(probs.astype(BF), vals * masks[side])
        attended_out[:, at : at + 2 * head] = attended.astype(BF)
    branch = dot(attended_out[...], w_all[1, :, width:]) + b_proj
    branch_out[...] = branch
    middle_out[...] = values + gate * branch


def attention_backward(layer, rows, offset, shards, *refs):
    peers = piece_count(shards)
    idx, stream, mod_all, d_middle_in, qkv, probs_in, attended, branch, w_qkv, w_proj = refs[:10]
    near, far = refs[10 : 10 + peers], refs[10 + peers : 10 + 2 * peers]
    d_stream, vec, keep, send, w_all, d_qkv, grad_all, sems, out_sems = refs[10 + 2 * peers :]
    mod = mod_all.at[layer : layer + 1]
    copies = make_copies(
        qkv_pairs(idx, layer, rows, offset, w_qkv, w_proj, near, far, w_all), sems
    )
    start_all(copies)
    width = stream.shape[-1]
    head = width // HEADS
    root = head ** (-0.5)
    shift, scale, gate = (mod[:, part * width : (part + 1) * width] for part in range(3))
    normed, inverse = layer_norm(stream[...].astype(F32))
    h_one = (normed * (1.0 + scale) + shift).astype(BF)
    d_middle = d_middle_in[...]
    vec[:, 2 * width : 3 * width] = col_sum(d_middle * branch[...])
    d_branch = (d_middle * gate).astype(BF)
    grad_all[1, :, width:] = dot_tn(attended[...], d_branch).astype(BF)
    vec[:, 5 * width :] = col_sum(d_branch.astype(F32))
    wait_all(copies)
    d_attended = dot_nt(d_branch, w_all[1, :, width:]).astype(BF)
    lane = lax.broadcasted_iota(jnp.int32, (1, 2 * head), 1)
    masks = [(lane < head).astype(BF), (lane >= head).astype(BF)]
    for pair in range(HEADS // 2):
        at = pair * 2 * head
        queries = qkv[:, at : at + 2 * head]
        keys = qkv[:, width + at : width + at + 2 * head]
        vals = qkv[:, 2 * width + at : 2 * width + at + 2 * head]
        d_att = d_attended[:, at : at + 2 * head]
        d_queries, d_keys, d_values = 0.0, 0.0, 0.0
        for side in range(2):
            probs = probs_in[2 * pair + side]
            d_values = d_values + dot_tn(probs.astype(BF), d_att * masks[side])
            d_probs = dot_nt(d_att, vals * masks[side])
            inner = jnp.sum(probs * d_probs, axis=-1, keepdims=True)
            d_scores = (probs * (d_probs - inner)).astype(BF)
            d_queries = d_queries + dot(d_scores, keys * masks[side])
            d_keys = d_keys + dot_tn(d_scores, queries * masks[side])
        d_qkv[:, at : at + 2 * head] = (d_queries * root).astype(BF)
        d_qkv[:, width + at : width + at + 2 * head] = (d_keys * root).astype(BF)
        d_qkv[:, 2 * width + at : 2 * width + at + 2 * head] = d_values.astype(BF)
    d_qk, d_val = d_qkv[:, : 2 * width], d_qkv[:, 2 * width :]
    grad_all[0] = dot_tn(h_one, d_qk).astype(BF)
    grad_all[1, :, :width] = dot_tn(h_one, d_val).astype(BF)
    out_copies = make_copies(grad_pairs(idx, rows, shards, grad_all, keep, send), out_sems)
    start_all(out_copies)
    vec[:, 3 * width : 4 * width] = col_sum(d_qk[:, :width].astype(F32))
    vec[:, 4 * width : 5 * width] = col_sum(d_val.astype(F32))
    d_h_one = dot_nt(d_qk, w_all[0]) + dot_nt(d_val, w_all[1, :, :width])
    vec[:, :width] = col_sum(d_h_one)
    vec[:, width : 2 * width] = col_sum(d_h_one * normed)
    d_stream[...] = d_middle + norm_back(d_h_one * (1.0 + scale), normed, inverse)
    wait_all(out_copies)


def gelu_parts(pre_act):
    root = 0.7978845608028654
    square = pre_act * pre_act
    bent = jnp.tanh(root * pre_act * (1.0 + 0.044715 * square))
    half = 0.5 * (1.0 + bent)
    slope = half + 0.5 * pre_act * (1.0 - bent * bent) * (root * (1.0 + 3 * 0.044715 * square))
    return pre_act * half, slope


def mlp_vectors(mod_all, layer, width):
    mod = mod_all.at[layer : layer + 1]
    last = mod_all.shape[-1] - width
    return mod, mod[:, 9 * width : last], mod[:, last:]


def mlp_forward_part(rows, h_two, b_fc1, b_fc2, w_all, act_low, slopes):
    width = w_all.shape[1]
    mlp_out = b_fc2
    for chunk in range(w_all.shape[2] // width):
        cols = slice(chunk * width, (chunk + 1) * width)
        act, slope = gelu_parts(dot(h_two, w_all[0, :, cols]) + b_fc1[:, cols])
        act_low[:, cols] = act.astype(BF)
        slopes[:, cols] = slope
        mlp_out = mlp_out + dot(act_low[:, cols], fc2_chunk(w_all, rows, chunk))
    return mlp_out


def mlp_backward_part(
    idx, rows, shards, grad_out, mlp_out, middle, normed, inverse, h_two, scale, gate,
    w_all, act_low, slopes, vec, d_middle_out, grad_all, keep, send, out_sems,
):
    width = w_all.shape[1]
    parts = w_all.shape[2] // width
    vec[:, 2 * width : 3 * width] = col_sum(grad_out * mlp_out)
    d_mlp = (grad_out * gate).astype(BF)
    vec[:, (3 + parts) * width :] = col_sum(d_mlp.astype(F32))
    d_h_two = 0.0
    for chunk in range(parts):
        cols = slice(chunk * width, (chunk + 1) * width)
        d_act = dot_nt(d_mlp, fc2_chunk(w_all, rows, chunk))
        d_pre = (d_act * slopes[:, cols]).astype(BF)
        vec[:, (3 + chunk) * width : (4 + chunk) * width] = col_sum(d_pre.astype(F32))
        grad_all[0, :, cols] = dot_tn(h_two, d_pre).astype(BF)
        grad_fc2 = dot_tn(act_low[:, cols], d_mlp).astype(BF)
        first = chunk * width // rows
        for number in range(first, (chunk + 1) * width // rows):
            at, part = number // parts, number % parts
            grad_all[1, at * rows : (at + 1) * rows, part * width : (part + 1) * width] = grad_fc2[
                (number - first) * rows : (number - first + 1) * rows
            ]
        d_h_two = d_h_two + dot_nt(d_pre, w_all[0, :, cols])
    out_copies = make_copies(grad_pairs(idx, rows, shards, grad_all, keep, send), out_sems)
    start_all(out_copies)
    vec[:, :width] = col_sum(d_h_two)
    vec[:, width : 2 * width] = col_sum(d_h_two * normed)
    d_middle_out[...] = grad_out + norm_back(d_h_two * (1.0 + scale), normed, inverse)
    wait_all(out_copies)


def mlp_forward(layer, rows, offset, shards, *refs):
    peers = piece_count(shards)
    idx, middle, mod_all, w_fc1, w_fc2 = refs[:5]
    near, far = refs[5 : 5 + peers], refs[5 + peers : 5 + 2 * peers]
    act_low, slopes, mlp_out, stream_out, w_all, sems = refs[5 + 2 * peers :]
    mod, b_fc1, b_fc2 = mlp_vectors(mod_all, layer, middle.shape[-1])
    copies = make_copies(mlp_pairs(idx, layer, rows, offset, w_fc1, w_fc2, near, far, w_all), sems)
    start_all(copies)
    width = middle.shape[-1]
    shift, scale, gate = (mod[:, part * width : (part + 1) * width] for part in range(3, 6))
    normed, _ = layer_norm(middle[...])
    h_two = (normed * (1.0 + scale) + shift).astype(BF)
    wait_all(copies)
    mlp_out[...] = mlp_forward_part(rows, h_two, b_fc1, b_fc2, w_all, act_low, slopes)
    stream_out[...] = middle[...] + gate * mlp_out[...]


def mlp_backward(layer, rows, offset, shards, *refs):
    peers = piece_count(shards)
    idx, middle, mod_all, grad_out, act_low, slopes, mlp_out, w_fc1, w_fc2 = refs[:9]
    near, far = refs[9 : 9 + peers], refs[9 + peers : 9 + 2 * peers]
    d_middle, vec, keep, send, w_all, grad_all, sems, out_sems = refs[9 + 2 * peers :]
    mod = mod_all.at[layer : layer + 1]
    copies = make_copies(mlp_pairs(idx, layer, rows, offset, w_fc1, w_fc2, near, far, w_all), sems)
    start_all(copies)
    width = middle.shape[-1]
    shift, scale, gate = (mod[:, part * width : (part + 1) * width] for part in range(3, 6))
    normed, inverse = layer_norm(middle[...])
    h_two = (normed * (1.0 + scale) + shift).astype(BF)
    wait_all(copies)
    mlp_backward_part(
        idx, rows, shards, grad_out[...], mlp_out[...], middle, normed, inverse, h_two, scale,
        gate, w_all, act_low, slopes, vec, d_middle, grad_all, keep, send, out_sems,
    )


def mlp_both(layer, rows, offset, shards, *refs):
    peers = piece_count(shards)
    idx, middle, mod_all, cotangent, w_fc1, w_fc2 = refs[:6]
    near, far = refs[6 : 6 + peers], refs[6 + peers : 6 + 2 * peers]
    x_out, d_middle, vec, keep, send = refs[6 + 2 * peers : 11 + 2 * peers]
    w_all, grad_all, act_low, slopes, sems, out_sems = refs[11 + 2 * peers :]
    mod, b_fc1, b_fc2 = mlp_vectors(mod_all, layer, middle.shape[-1])
    copies = make_copies(mlp_pairs(idx, layer, rows, offset, w_fc1, w_fc2, near, far, w_all), sems)
    start_all(copies)
    width = middle.shape[-1]
    shift, scale, gate = (mod[:, part * width : (part + 1) * width] for part in range(3, 6))
    normed, inverse = layer_norm(middle[...])
    h_two = (normed * (1.0 + scale) + shift).astype(BF)
    wait_all(copies)
    mlp_out = mlp_forward_part(rows, h_two, b_fc1, b_fc2, w_all, act_low, slopes)
    x_out[...] = (middle[...] + gate * mlp_out).astype(BF)
    mlp_backward_part(
        idx, rows, shards, cotangent[...].astype(F32), mlp_out, middle, normed, inverse, h_two,
        scale, gate, w_all, act_low, slopes, vec, d_middle, grad_all, keep, send, out_sems,
    )


def padded_rows(idx, w_ada, w_pad, sems):
    layers, rows, wide = w_ada.shape
    w_pad[...] = jnp.zeros(w_pad.shape, BF)
    own = block_at(idx[0] * rows, rows)
    return make_copies(
        [
            (w_ada.at[layer], w_pad.at[own, layer * wide : (layer + 1) * wide])
            for layer in range(layers)
        ],
        sems,
    )


def modulate_kernel(shards, *refs):
    idx, w_ada, b_ada = refs[:3]
    biases, conditions = refs[3:7], refs[7 : 7 + shards]
    outs = refs[7 + shards : 7 + 2 * shards]
    w_pad, sems = refs[7 + 2 * shards :]
    copies = padded_rows(idx, w_ada, w_pad, sems)
    start_all(copies)
    layers = w_ada.shape[0]
    wide = w_ada.shape[2]
    acts = []
    for ref in conditions:
        cond = ref[...].astype(F32)
        acts.append(cond / (1.0 + jnp.exp(-cond)))
    acts = jnp.concatenate(acts, axis=0).astype(BF)

    def spread(bias):
        length = bias.shape[1]
        row = lax.broadcasted_iota(jnp.int32, (length, shards * length), 0)
        col = lax.broadcasted_iota(jnp.int32, (length, shards * length), 1)
        place = jnp.where(col - row == idx[0] * length, 1.0, 0.0).astype(BF)
        return dot(bias[...], place)

    first = spread(b_ada)
    at = wide
    for bias in biases:
        full = spread(bias)
        for out in outs:
            out[:, at : at + full.shape[1]] = full
        at += full.shape[1]
    wait_all(copies)
    for layer in range(layers):
        result = dot(acts, w_pad[:, layer * wide : (layer + 1) * wide]) + first[layer : layer + 1]
        for step in range(shards):
            outs[step][layer : layer + 1, :wide] = result[step : step + 1]


def stack_kernel(first, second, out, rows_f32):
    size = first.shape[0]
    rows_f32[:size] = first[...].astype(F32)
    rows_f32[size:] = second[...].astype(F32)
    out[...] = rows_f32[...].astype(BF)


def group_kernel(idx, w_ada, first, second, keep, send, stacked, rows_f32, w_pad, sems):
    copies = padded_rows(idx, w_ada, w_pad, sems)
    start_all(copies)
    width, wide = w_pad.shape
    stack_kernel(first, second, stacked, rows_f32)
    wait_all(copies)
    result = dot_nt(stacked[:, width : width + wide], w_pad[...])
    half = keep.shape[0]
    keep[...] = result[:half]
    send[...] = result[half:]


def ada_grad_kernel(rows, wide, inverse_count, *refs):
    idx, stacks = refs[0], refs[1:-4]
    grad_ada, sums, turned, gathered_f32 = refs[-4:]
    layers = grad_ada.shape[0]
    width = turned.shape[0]
    size = stacks[0].shape[0]
    for number, stack in enumerate(stacks):
        gathered_f32[number * size : (number + 1) * size] = stack[...].astype(F32)
    gathered = gathered_f32[...].astype(BF)
    turned[...] = gathered_f32[:, :width].T
    own = turned[block_at(idx[0] * rows, rows), :].astype(BF)
    for layer in range(layers):
        at = width + layer * wide
        grad_ada[layer] = dot(own, gathered[:, at : at + wide]) * inverse_count
    sums[...] = col_sum(gathered_f32[:, width:]) * inverse_count


def core_sum_kernel(slots, count, *refs):
    keeps, recvs, outs = refs[:count], refs[count : 2 * count], refs[2 * count :]
    for (first, number), out in zip(slots, outs):
        for slot in range(number):
            at = 0
            for keep, recv in zip(keeps, recvs):
                wide = keep.shape[-1]
                total = keep[first + slot].astype(F32) + recv[first + slot].astype(F32)
                out[slot, :, at : at + wide] = total.astype(BF)
                at += wide


def split_sum_kernel(mine, other, keep, send):
    keep[...] = (mine[0].astype(F32) + other[0].astype(F32)).astype(BF)
    send[...] = (mine[1].astype(F32) + other[1].astype(F32)).astype(BF)


def row_split_kernel(*refs):
    idx, terms, keep, send, halves = refs[0], refs[1:-3], refs[-3], refs[-2], refs[-1]
    total = terms[0][...].astype(F32)
    for term in terms[1:]:
        total = total + term[...].astype(F32)
    half = halves.shape[1]
    for side in range(2):
        halves[side] = total[side * half : (side + 1) * half].astype(BF)
    mine = idx[1] % 2
    keep[...] = halves[mine]
    send[...] = halves[1 - mine]


def sum_kernel(*refs):
    total = refs[0][...].astype(F32)
    for term in refs[1:-1]:
        total = total + term[...].astype(F32)
    refs[-1][...] = total.astype(BF).reshape(refs[-1].shape)


def finish_kernel(rows, plan, factor, *refs):
    idx = refs[0]
    terms = list(refs[1 : 1 + sum(2 * parts for _, parts in plan)])
    at = 1 + len(terms)
    g_qkv, g_proj, g_fc1, g_fc2 = refs[at : at + 4]
    scratch = refs[at + 4 :]
    width = g_proj.shape[-1]
    hidden = g_fc1.shape[-1]
    for (members, parts), halves in zip(plan, scratch):
        for core in (idx[2], 1 - idx[2]):
            if parts == 1:
                halves[core] = terms.pop(0)[...]
            else:
                size = terms[0].shape[0]
                for side in (idx[1] % 2, 1 - idx[1] % 2):
                    halves[core, block_at(side * size, size), :] = terms.pop(0)[...]
        for kind, layer, skip in members:
            if kind == "qkv":
                first = halves[0, :, skip : skip + 2 * width]
                g_qkv[layer, :, : 2 * width] = first.astype(F32) * factor
                second = halves[1, :, skip : skip + 2 * width].astype(F32) * factor
                g_qkv[layer, :, 2 * width :] = second[:, :width]
                g_proj[layer] = second[:, width:]
            else:
                g_fc1[layer] = halves[0, :, skip : skip + hidden].astype(F32) * factor
                for part in range(hidden // width):
                    at = skip + part * width
                    g_fc2[layer, part * rows : (part + 1) * rows] = (
                        halves[1, :, at : at + width].astype(F32) * factor
                    )


def shards(
    latents, condition, cotangent, w_qkv, b_qv, w_proj, b_proj, w_fc1, b_fc1, w_fc2, b_fc2, w_ada,
    b_ada,
):
    layers, rows, _ = w_qkv.shape
    width = w_proj.shape[-1]
    hidden = w_fc1.shape[-1]
    wide = w_ada.shape[-1]
    seq = latents.shape[1]
    n_shard = lax.axis_size("shard")
    n_rep = lax.axis_size("rep")
    levels = n_rep // CORES
    shard_id = lax.axis_index("shard")
    rep_id = lax.axis_index("rep")
    core = rep_id % CORES
    idx = jnp.stack([shard_id, rep_id // CORES, core]).astype(jnp.int32)
    total_latents = latents.shape[0] * n_shard * n_rep
    factor = 1.0 / total_latents

    def exchange(array, by_shard=0, by_level=0, by_core=0, turn=None):
        moves = []
        for own_shard in range(n_shard):
            for own_rep in range(n_rep):
                mask = turn[own_rep % CORES] if turn else by_shard
                peer = (own_shard ^ mask) * n_rep + (own_rep ^ (by_level * CORES + by_core))
                moves.append((own_shard * n_rep + own_rep, peer))
        return lax.ppermute(array, ("shard", "rep"), moves)

    def after(array, *earlier):
        return lax.optimization_barrier((array,) + earlier)[0]

    relay = n_shard == 4
    first_turn, second_turn = (1, 2), (2, 1)

    half_wide = {"qkv": 2 * width, "mlp": hidden}
    copy_total = {"qkv": 3, "mlp": 1 + hidden // width}

    def pack(*plan):
        whole = run(
            functools.partial(pack_kernel, plan), "pack",
            [(array, "a") for array in (w_qkv, w_proj, w_fc1, w_fc2)],
            [((rows, 2 * sum(half_wide[kind] for kind in kinds)), BF, "a") for _, kinds in plan],
            [pltpu.SemaphoreType.DMA((sum(copy_total[kind] for _, ks in plan for kind in ks),))],
        )
        if relay:
            return whole
        return [
            lax.dynamic_slice_in_dim(array, core * (array.shape[1] // 2), array.shape[1] // 2, 1)
            for array in whole
        ]

    def near_first(packed):
        if relay:
            return [exchange(packed, turn=first_turn)]
        return [exchange(packed, by_shard=step) for step in range(1, n_shard)]

    def near_second(near, *earlier):
        if not relay:
            return near
        half = near[0].shape[1] // 2
        source = after(near[0], *earlier) if earlier else near[0]
        part = lax.dynamic_slice_in_dim(source, core * half, half, axis=1)
        return near + [exchange(part, turn=second_turn)]

    def far_of(near, *earlier):
        return [exchange(after(piece, *earlier) if earlier else piece, by_core=1) for piece in near]

    conditions = [condition] + [exchange(condition, by_shard=step) for step in range(1, n_shard)]
    packed_qkv, packed_mlp = pack((0, ("qkv",)), (0, ("mlp",)))
    qkv_near = near_first(packed_qkv)
    mlp_near = near_first(packed_mlp)
    pad_scratch = [pltpu.VMEM((width, layers * wide), BF), pltpu.SemaphoreType.DMA((layers,))]
    span = wide + 4 * width + hidden
    partial = run(
        functools.partial(modulate_kernel, n_shard), "modulate",
        [(idx, "s"), (w_ada, "a"), (b_ada, "v"), (b_qv, "v"), (b_proj, "v"), (b_fc1, "v"),
         (b_fc2, "v")] + [(array, "v") for array in conditions],
        [((layers, span), F32, "v")] * n_shard, pad_scratch, flops=10**7,
    )
    mod_all = partial[0]
    for step in range(1, n_shard):
        mod_all = mod_all + exchange(partial[step], by_shard=step)

    qkv_near = near_second(qkv_near)
    qkv_far = far_of(qkv_near)
    mod_all = after(mod_all, *mlp_near)
    later_near = []
    for layer in range(1, layers):
        (packed,) = pack((layer, ("qkv", "mlp")))
        later_near.append(near_first(after(packed, mod_all)))
    mlp_near = near_second(mlp_near)

    big = seq * width
    row = lambda kind="v": ((seq, width), F32, kind)
    vec_wide = {"qkv": 6 * width, "mlp": 4 * width + hidden}

    def piece_args(pair):
        return [(array, "a") for array in pair[0] + pair[1]]

    copy_count = 6 if relay else 2 * (n_shard - 1)
    qkv_sems = pltpu.SemaphoreType.DMA((3 + copy_count,))
    mlp_sems = pltpu.SemaphoreType.DMA((1 + hidden // width + copy_count,))
    out_sems = pltpu.SemaphoreType.DMA((2 * n_shard,))
    w_qkv_all = pltpu.VMEM((2, width, 2 * width), BF)
    w_mlp_all = pltpu.VMEM((2, width, hidden), BF)

    def grads_out(kind):
        return [((n_shard, rows, half_wide[kind]), BF, "a")] * 2

    stream = latents[0]
    saved = []
    vecs, raw = {}, {}
    qkv_pieces, mlp_pieces = {0: ((qkv_near, qkv_far), 0)}, {}
    for layer in range(layers):
        pair, offset = qkv_pieces[layer]
        qkv, probs, attended, branch, middle = run(
            functools.partial(attention_forward, layer, rows, offset, n_shard), "attention_forward",
            [(idx, "s"), (stream, "v"), (mod_all, "v"), (w_qkv, "a"), (w_proj, "a")]
            + piece_args(pair),
            [((seq, 3 * width), BF, "v"), ((HEADS, seq, seq), F32, "v"), ((seq, width), BF, "v"),
             row(), row()],
            [w_qkv_all, qkv_sems], flops=10 * big * width,
        )
        if layer == 0:
            mlp_pieces[0] = ((mlp_near, far_of(mlp_near, middle)), 0)
            later_near = [near_second(near, middle) for near in later_near]
        pair, offset = mlp_pieces[layer]
        entry = dict(stream=stream, qkv=qkv, probs=probs, attended=attended, branch=branch,
                     middle=middle)
        if layer + 1 < layers:
            act_low, slopes, mlp_out, stream = run(
                functools.partial(mlp_forward, layer, rows, offset, n_shard), "mlp_forward",
                [(idx, "s"), (middle, "v"), (mod_all, "v"), (w_fc1, "a"), (w_fc2, "a")]
                + piece_args(pair),
                [((seq, hidden), BF, "v"), ((seq, hidden), F32, "v"), row(), row()],
                [w_mlp_all, mlp_sems], flops=16 * big * width,
            )
            entry.update(act_low=act_low, slopes=slopes, mlp_out=mlp_out)
            near = later_near[layer]
            later_pair = (near, far_of(near, stream))
            qkv_pieces[layer + 1] = (later_pair, 0)
            mlp_pieces[layer + 1] = (later_pair, 2 * width)
        else:
            x_out, d_middle, vecs["mlp", layer], *raw["mlp", layer] = run(
                functools.partial(mlp_both, layer, rows, offset, n_shard), "mlp_both",
                [(idx, "s"), (middle, "v"), (mod_all, "v"), (cotangent[0], "v"), (w_fc1, "a"),
                 (w_fc2, "a")] + piece_args(pair),
                [((seq, width), BF, "v"), row(), ((1, vec_wide["mlp"]), F32, "v")]
                + grads_out("mlp"),
                [w_mlp_all, w_mlp_all, pltpu.VMEM((seq, hidden), BF),
                 pltpu.VMEM((seq, hidden), F32), mlp_sems, out_sems], flops=48 * big * width,
            )
        saved.append(entry)

    def core_sum(keys, *earlier):
        keeps = [raw[key][0] for key in keys]
        received = [exchange(raw[key][1], by_core=1) for key in keys]
        if earlier:
            keeps[0] = after(keeps[0], *earlier)
        total_wide = sum(keep.shape[-1] for keep in keeps)
        slots = [(0, 2), (2, 2)] if relay else [(slot, 1) for slot in range(n_shard)]
        return run(
            functools.partial(core_sum_kernel, slots, len(keys)), "core_sum",
            [(array, "v") for array in keeps + received],
            [((number, rows, total_wide), BF, "v") for _, number in slots],
        )

    def shard_send(summed):
        if relay:
            return [exchange(summed[1], turn=first_turn)]
        return [exchange(summed[step], by_shard=step) for step in range(1, n_shard)]

    def add(terms, shape):
        return run(sum_kernel, "add", [(array, "v") for array in terms], [(shape, BF, "v")])[0]

    def shard_second(summed, arrived, *earlier):
        shape = summed[0].shape[1:]
        mine = after(summed[0], *earlier) if earlier else summed[0]
        if not relay:
            return [mine.reshape(shape)] + [array.reshape(shape) for array in arrived]
        keep, send = run(
            split_sum_kernel, "split_sum", [(mine, "v"), (arrived[0], "v")], [(shape, BF, "v")] * 2
        )
        return [keep, exchange(send, turn=second_turn)]

    def level_first(terms, halve, *earlier):
        shape = terms[0].shape
        if earlier:
            terms = [after(terms[0], *earlier)] + terms[1:]
        if not halve or shape[0] % 32:
            total = add(terms, shape)
            return False, total, exchange(total, by_level=1)
        part = (shape[0] // 2, shape[1])
        keep, send = run(
            row_split_kernel, "row_split",
            [(idx, "s")] + [(array, "v") for array in terms],
            [(part, BF, "v")] * 2, [pltpu.VMEM((2,) + part, BF)],
        )
        return True, keep, exchange(send, by_level=1)

    def level_second(first, *earlier):
        halved, kept, arriving = first
        if earlier:
            kept = after(kept, *earlier)
        return halved, add([kept, arriving], kept.shape)

    def level_last(halved, total):
        step = 2
        while step < levels:
            total = add([total, exchange(total, by_level=step)], total.shape)
            step *= 2
        near = [total, exchange(total, by_level=1)] if halved else [total]
        return near + far_of(near)

    waiting = []
    for layer in reversed(range(layers)):
        entry = saved[layer]
        pair, offset = mlp_pieces[layer]
        if layer + 1 < layers:
            keys = [("qkv", layer + 1), ("mlp", layer + 1)]
            summed = core_sum(keys, grad_stream)
            waiting.append((keys, summed, shard_send(summed)))
            grad_stream = after(grad_stream, summed[0])
            d_middle, vecs["mlp", layer], *raw["mlp", layer] = run(
                functools.partial(mlp_backward, layer, rows, offset, n_shard), "mlp_backward",
                [(idx, "s"), (entry["middle"], "v"), (mod_all, "v"), (grad_stream, "v"),
                 (entry["act_low"], "v"), (entry["slopes"], "v"), (entry["mlp_out"], "v"),
                 (w_fc1, "a"), (w_fc2, "a")] + piece_args(pair),
                [row(), ((1, vec_wide["mlp"]), F32, "v")] + grads_out("mlp"),
                [w_mlp_all, w_mlp_all, mlp_sems, out_sems], flops=32 * big * width,
            )
        pair, offset = qkv_pieces[layer]
        grad_stream, vecs["qkv", layer], *raw["qkv", layer] = run(
            functools.partial(attention_backward, layer, rows, offset, n_shard),
            "attention_backward",
            [(idx, "s"), (entry["stream"], "v"), (mod_all, "v"), (d_middle, "v"),
             (entry["qkv"], "v"), (entry["probs"], "v"), (entry["attended"], "v"),
             (entry["branch"], "v"), (w_qkv, "a"), (w_proj, "a")] + piece_args(pair),
            [row(), ((1, vec_wide["qkv"]), F32, "v")] + grads_out("qkv"),
            [w_qkv_all, pltpu.VMEM((seq, 3 * width), BF), w_qkv_all, qkv_sems, out_sems],
            flops=28 * big * width,
        )
    (keys_first, summed, arrived), = waiting
    terms_first = shard_second(summed, arrived, grad_stream)
    core_mlp = core_sum([("mlp", 0)], terms_first[0])
    sent_mlp = shard_send(core_mlp)
    level_a = level_first(terms_first, True, core_mlp[0])
    core_qkv = core_sum([("qkv", 0)], level_a[1])
    sent_qkv = shard_send(core_qkv)
    terms_mlp = shard_second(core_mlp, sent_mlp, core_qkv[0])
    terms_qkv = shard_second(core_qkv, sent_qkv, terms_mlp[0])

    cond_in = condition.astype(F32)
    vector = [jax.nn.silu(cond_in).astype(BF)]
    for layer in range(layers):
        vector += [vecs[kind, layer][:, : 3 * width].astype(BF) for kind in ("qkv", "mlp")]
    for layer in range(layers):
        vector += [vecs[kind, layer][:, 3 * width :].astype(BF) for kind in ("qkv", "mlp")]
    vector = after(jnp.concatenate(vector, axis=1), terms_qkv[0])
    length = vector.shape[1]
    masks = [first_turn, second_turn] if relay else []
    while not relay and 2 ** len(masks) < n_shard:
        masks.append((2 ** len(masks),) * 2)

    def stack(first, second):
        shape = (2 * first.shape[0], length)
        return run(
            stack_kernel, "stack", [(first, "v"), (second, "v")], [(shape, BF, "v")],
            [pltpu.VMEM(shape, F32)],
        )[0]

    total_a = level_second(level_a, vector)
    level_b = level_first(terms_mlp, True, total_a[1])
    level_c = level_first(terms_qkv, False, level_b[1])
    plan = [keys_first, [("mlp", 0)], [("qkv", 0)]]
    finals = [level_last(*total_a), level_last(*level_second(level_b)),
              level_last(*level_second(level_c))]
    for mask in masks[:-1]:
        vector = stack(vector, exchange(vector, turn=mask))
    grad_cond, passed, stacked = run(
        group_kernel, "group",
        [(idx, "s"), (w_ada, "a"), (vector, "v"), (exchange(vector, turn=masks[-1]), "v")],
        [((n_shard // 2, width), F32, "v")] * 2 + [((n_shard, length), BF, "v")],
        [pltpu.VMEM((n_shard, length), F32)] + pad_scratch, flops=10**7,
    )
    grad_cond = grad_cond + exchange(passed, turn=masks[-1])
    for mask in masks[-2::-1]:
        half = grad_cond.shape[0] // 2
        grad_cond = grad_cond[:half] + exchange(grad_cond[half:], turn=mask)
    cond_grad = jax.vjp(jax.nn.silu, cond_in)[1](grad_cond)[0]
    step = 1
    while 2 * step < levels:
        stacked = stack(stacked, exchange(stacked, by_level=step))
        step *= 2
    stacks = [stacked, exchange(stacked, by_level=step)]
    stacks = stacks + far_of(stacks)
    grad_ada, sums = run(
        functools.partial(ada_grad_kernel, rows, wide, factor), "ada_grad",
        [(idx, "s")] + [(array, "v") for array in stacks],
        [((layers, rows, wide), F32, "v"), ((1, length - width), F32, "v")],
        [pltpu.VMEM((width, total_latents), F32), pltpu.VMEM((total_latents, length), F32)],
        flops=10**8,
    )

    def own_part(parts):
        whole = jnp.concatenate(parts, axis=0)
        length = whole.shape[1] // n_shard
        return lax.dynamic_slice_in_dim(whole, shard_id * length, length, axis=1)

    base = layers * wide
    at = [base + layer * (4 * width + hidden) for layer in range(layers)]
    grad_ada_bias = own_part([sums[:, layer * wide : (layer + 1) * wide] for layer in range(layers)])
    grad_qv_bias = own_part([sums[:, a : a + 2 * width] for a in at])
    grad_proj_bias = own_part([sums[:, a + 2 * width : a + 3 * width] for a in at])
    grad_fc1_bias = own_part([sums[:, a + 3 * width : a + 3 * width + hidden] for a in at])
    grad_fc2_bias = own_part([sums[:, a + 3 * width + hidden : a + 4 * width + hidden] for a in at])

    finish_plan, finish_inputs, finish_scratch = [], [(idx, "s")], []
    for keys, parts in zip(plan, finals):
        members, skip = [], 0
        for kind, layer in keys:
            members.append((kind, layer, skip))
            skip += half_wide[kind]
        finish_plan.append((members, len(parts) // 2))
        finish_inputs += [(array, "v") for array in parts]
        finish_scratch.append(pltpu.VMEM((2, rows, skip), BF))
    grad_qkv, grad_proj, grad_fc1, grad_fc2 = run(
        functools.partial(finish_kernel, rows, finish_plan, factor), "finish",
        finish_inputs,
        [(array.shape, F32, "v") for array in (w_qkv, w_proj, w_fc1, w_fc2)],
        finish_scratch,
    )
    return (
        x_out[None], grad_stream[None], cond_grad, grad_qkv, grad_qv_bias, grad_proj,
        grad_proj_bias, grad_fc1, grad_fc1_bias, grad_fc2, grad_fc2_bias, grad_ada, grad_ada_bias,
    )


def solution(mesh):
    rows3, rows2 = P(("shard", "rep"), None, None), P(("shard", "rep"), None)
    weight, bias = P(None, "shard", None), P(None, "shard")
    return jax.shard_map(
        shards,
        mesh=mesh,
        in_specs=(rows3, rows2, rows3) + (weight, bias) * 5,
        out_specs=(rows3, rows3, rows2) + (weight, bias) * 5,
        check_vma=False,
    )
```

time: 240 us -> 179 us (0.75)
  starting transfers between devices: 73.5 us -> 42.1 us
  local copies, waits for them, and re-layouts: 28.1 us -> 11 us
  waiting for transfers between devices: 77.2 us -> 68.9 us
  other arithmetic: 7.25 us -> 3.39 us
    ppermute x80 -> x49, starting transfers between devices: 73.5 us -> 42.1 us  [exchange(): return lax.ppermute(array, ('shard', 'rep'), moves)]
    concatenate x4 -> x1, local copies, waits for them, and re-layouts: 15.7 us -> 0.01 us  [shards(): vector = after(jnp.concatenate(vector, axis=1), terms_qkv[0])]
    ppermute x80 -> x49, waiting for transfers between devices: 77.2 us -> 68.9 us  [exchange(): return lax.ppermute(array, ('shard', 'rep'), moves)]
    unnamed x77 -> x69, local copies, waits for them, and re-layouts: 6.02 us -> 9.35 us
    another operation x30 -> x0, local copies, waits for them, and re-layouts: 2.94 us -> none  [spread(): jnp.tile(bias[None, :], (1, n_shard))]
    pallas_call x20 -> x30, Pallas kernels: 51.5 us -> 51.9 us  [run(): pl.pallas_call(body, out_shape=[jax.ShapeDtypeStruct(shape, dtype) for sh...]
  transfers between devices with their start and end apart: 80 -> 49, of which waited for: 26 -> 21; matrix products, arithmetic and copies ran while one was open for 10% -> 3% of each run, Pallas kernels for 9% -> 21%
where the time goes in v2:
time: 179 us
  waiting for transfers between devices  68.9 us (38%)
  Pallas kernels  51.9 us (29%)
  starting transfers between devices  42.1 us (24%)
  local copies, waits for them, and re-layouts  11 us (6%)
  other arithmetic  3.39 us (2%)
    ppermute x49, waiting for transfers between devices, exchange(): return lax.ppermute(array, ('shard', 'rep'), moves)  68.9 us
    pallas_call x30, Pallas kernels, run(): pl.pallas_call(body, out_shape=[jax.ShapeDtypeStruct(shape, dtype) for sh...  51.9 us
    ppermute x49, starting transfers between devices, exchange(): return lax.ppermute(array, ('shard', 'rep'), moves)  42.1 us
    unnamed x69, local copies, waits for them, and re-layouts  9.35 us
  transfers between devices with their start and end apart: 49, of which 21 were waited for; matrix products, arithmetic and copies ran while one was open for 3% of the time, Pallas kernels for 21%

profile of v2, /device:TPU:0, one launch (start us, length us, event | category | flops | bytes accessed | tf_op | source)
XLA Modules:
  0.0 178.7 jit_solution(4436087480642678999)
XLA Ops:
  5.7 3.0 %collective-permute-start.7 = (bf16[96,1536]{1,0:T(8,128)(2,1)}, bf16[96,1536]{1,0:T(8,128)(2,1)}, u32[]{:S(2)}, u32[]{:S(2)}) collective-permute-start(bf16[96,1536]{1,0:T(8,128)(2,1)} %get-tuple-element.100), channel_id=1, source_target_pairs={{0,8},{1,17},{2,10},{3,19},{4,12},{5,21},{6,14},{7,23},{8,0},{9,25... | collective-permute-start | bytes 884744 | tf_op jit(solution)/shard_map/ppermute | solution.py:576
  8.8 2.0 %collective-permute-start.1 = (bf16[1,384]{1,0:T(2,128)(2,1)S(1)}, bf16[1,384]{1,0:T(2,128)(2,1)S(1)}, u32[]{:S(2)}, u32[]{:S(2)}) collective-permute-start(bf16[1,384]{1,0:T(2,128)(2,1)S(1)} %copy-done.25), channel_id=1, source_target_pairs={{0,16},{1,17},{2,18},{3,19},{4,20},{5,21},{6,22},{7,23},{8,24},{9,... | collective-permute-start | bytes 2312 | tf_op jit(solution)/shard_map/ppermute | solution.py:576
  15.4 2.4 %modulate.1 = (f32[2,5376]{1,0:T(2,128)S(1)}, f32[2,5376]{1,0:T(2,128)S(1)}, f32[2,5376]{1,0:T(2,128)S(1)}, f32[2,5376]{1,0:T(2,128)S(1)}) custom-call(s32[3]{0:T(128)S(1)} %pad_add_fusion.refs_0_.idx, bf16[2,96,2304]{2,1,0:T(8,128)(2,1)S(1)} %copy-done.8, bf16[2,576]{1,0:T(2,128)(2,1)S(1)} %copy-done.26, bf16[2,192]{1,0:T(2,128)(2,1)S(1)} %copy-done.28, ...), custom_call_target="tpu_custom_call" | custom-call | flops 1 | bytes 1 | tf_op jit(solution)/shard_map/modulate/pallas_call | solution.py:68
  26.5 2.2 %collective-permute-done.8.refs_6_.refs_11_ = bf16[96,768]{1,0:T(8,128)(2,1)} collective-permute-done((bf16[96,768]{1,0:T(8,128)(2,1)}, bf16[96,768]{1,0:T(8,128)(2,1)}, u32[]{:S(2)}, u32[]{:S(2)}) %collective-permute-start.8) | collective-permute-done | bytes 147488 | tf_op jit(solution)/shard_map/ppermute | solution.py:576
  30.2 3.9 %attention_forward.2 = (bf16[256,1152]{1,0:T(8,128)(2,1)S(1)}, f32[6,256,256]{2,1,0:T(8,128)S(1)}, bf16[256,384]{1,0:T(8,128)(2,1)S(1)}, f32[256,384]{1,0:T(8,128)S(1)}, f32[256,384]{1,0:T(8,128)S(1)}) custom-call(s32[3]{0:T(128)S(1)} %pad_add_fusion.refs_0_.idx, bf16[256,384]{1,0:T(8,128)(2,1)S(1)} %bitcast.7, f32[2,5376]{1,0:T(2,128)S(1)} %add_add_fusion.refs_2_, ...), custom_call_target="tpu_custom_call" | custom-call | flops 1 | bytes 1 | tf_op jit(solution)/shard_map/attention_forward/pallas_call | solution.py:68
  39.7 2.3 %collective-permute-done.13.refs_8_.refs_12_ = bf16[96,1536]{1,0:T(8,128)(2,1)} collective-permute-done((bf16[96,1536]{1,0:T(8,128)(2,1)}, bf16[96,1536]{1,0:T(8,128)(2,1)}, u32[]{:S(2)}, u32[]{:S(2)}) %collective-permute-start.13) | collective-permute-done | bytes 294944 | tf_op jit(solution)/shard_map/ppermute | solution.py:576
  42.9 4.4 %mlp_forward.1 = (bf16[256,1536]{1,0:T(8,128)(2,1)S(1)}, f32[256,1536]{1,0:T(8,128)S(1)}, f32[256,384]{1,0:T(8,128)S(1)}, f32[256,384]{1,0:T(8,128)S(1)}) custom-call(s32[3]{0:T(128)S(1)} %pad_add_fusion.refs_0_.idx, f32[256,384]{1,0:T(8,128)S(1)} %copy-done.11, f32[2,5376]{1,0:T(2,128)S(1)} %add_add_fusion.refs_2_, bf16[2,96,1536]{2,1,0:T(8,128)(2,1)S(1)} %copy-done.3, ...), custom_call_target="tpu_custom_call" | custom-call | flops 1 | bytes 1 | tf_op jit(solution)/shard_map/mlp_forward/pallas_call | solution.py:68
  49.1 6.7 %collective-permute-done.15.refs_6_.refs_7_.refs_11_ = bf16[96,2304]{1,0:T(8,128)(2,1)S(1)} collective-permute-done((bf16[96,2304]{1,0:T(8,128)(2,1)S(1)}, bf16[96,2304]{1,0:T(8,128)(2,1)S(1)}, u32[]{:S(2)}, u32[]{:S(2)}) %collective-permute-start.15) | collective-permute-done | bytes 442400 | tf_op jit(solution)/shard_map/ppermute | solution.py:576
  57.6 3.0 %attention_forward.3 = (bf16[256,1152]{1,0:T(8,128)(2,1)S(1)}, f32[6,256,256]{2,1,0:T(8,128)S(1)}, bf16[256,384]{1,0:T(8,128)(2,1)S(1)}, f32[256,384]{1,0:T(8,128)S(1)}, f32[256,384]{1,0:T(8,128)S(1)}) custom-call(s32[3]{0:T(128)S(1)} %pad_add_fusion.refs_0_.idx, f32[256,384]{1,0:T(8,128)S(1)} %get-tuple-element.104.refs_1_, ...), custom_call_target="tpu_custom_call" | custom-call | flops 1 | bytes 1 | tf_op jit(solution)/shard_map/attention_forward/pallas_call | solution.py:68
  60.6 7.1 %mlp_both.1 = (bf16[256,384]{1,0:T(8,128)(2,1)}, f32[256,384]{1,0:T(8,128)S(1)}, f32[1,3072]{1,0:T(1,128)S(1)}, bf16[4,96,1536]{2,1,0:T(8,128)(2,1)S(1)}, bf16[4,96,1536]{2,1,0:T(8,128)(2,1)S(1)}) custom-call(s32[3]{0:T(128)S(1)} %pad_add_fusion.refs_0_.idx, f32[256,384]{1,0:T(8,128)S(1)} %get-tuple-element.109.refs_1_, f32[2,5376]{1,0:T(2,128)S(1)} %add_add_fusion.refs_2_, ...), custom_call_target="tpu_custom_call" | custom-call | flops 1 | bytes 1 | tf_op jit(solution)/shard_map/mlp_both/pallas_call | solution.py:68
  67.9 5.9 %attention_backward.2 = (f32[256,384]{1,0:T(8,128)S(1)}, f32[1,2304]{1,0:T(1,128)S(1)}, bf16[4,96,768]{2,1,0:T(8,128)(2,1)S(1)}, bf16[4,96,768]{2,1,0:T(8,128)(2,1)S(1)}) custom-call(s32[3]{0:T(128)S(1)} %pad_add_fusion.refs_0_.idx, f32[256,384]{1,0:T(8,128)S(1)} %get-tuple-element.104.refs_1_, f32[2,5376]{1,0:T(2,128)S(1)} %add_add_fusion.refs_2_, ...), custom_call_target="tpu_custom_call" | custom-call | flops 1 | bytes 1 | tf_op jit(solution)/shard_map/attention_backward/pallas_call | solution.py:68
  78.2 5.6 %mlp_backward.1 = (f32[256,384]{1,0:T(8,128)S(1)}, f32[1,3072]{1,0:T(1,128)S(1)}, bf16[4,96,1536]{2,1,0:T(8,128)(2,1)S(1)}, bf16[4,96,1536]{2,1,0:T(8,128)(2,1)S(1)}) custom-call(s32[3]{0:T(128)S(1)} %pad_add_fusion.refs_0_.idx, f32[256,384]{1,0:T(8,128)S(1)} %copy-done.12, f32[2,5376]{1,0:T(2,128)S(1)} %add_add_fusion.refs_2_, ...), custom_call_target="tpu_custom_call" | custom-call | flops 1 | bytes 1 | tf_op jit(solution)/shard_map/mlp_backward/pallas_call | solution.py:68
  83.9 7.6 %attention_backward.3 = (f32[256,384]{1,0:T(8,128)}, f32[1,2304]{1,0:T(1,128)S(1)}, bf16[4,96,768]{2,1,0:T(8,128)(2,1)S(1)}, bf16[4,96,768]{2,1,0:T(8,128)(2,1)S(1)}) custom-call(s32[3]{0:T(128)S(1)} %pad_add_fusion.refs_0_.idx, bf16[256,384]{1,0:T(8,128)(2,1)S(1)} %bitcast.8, f32[2,5376]{1,0:T(2,128)S(1)} %add_add_fusion.refs_2_, ...), custom_call_target="tpu_custom_call" | custom-call | flops 1 | bytes 1 | tf_op jit(solution)/shard_map/attention_backward/pallas_call | solution.py:68
  94.5 11.0 %collective-permute-done.22.refs_2_ = bf16[96,2304]{1,0:T(8,128)(2,1)S(1)} collective-permute-done((bf16[96,2304]{1,0:T(8,128)(2,1)S(1)}, bf16[96,2304]{1,0:T(8,128)(2,1)S(1)}, u32[]{:S(2)}, u32[]{:S(2)}) %collective-permute-start.22) | collective-permute-done | bytes 442400 | tf_op jit(solution)/shard_map/ppermute | solution.py:576
  108.4 4.9 %collective-permute-done.25.other = bf16[2,96,768]{2,1,0:T(8,128)(2,1)S(1)} collective-permute-done((bf16[2,96,768]{2,1,0:T(8,128)(2,1)S(1)}, bf16[2,96,768]{2,1,0:T(8,128)(2,1)S(1)}, u32[]{:S(2)}, u32[]{:S(2)}) %collective-permute-start.25) | collective-permute-done | bytes 294944 | tf_op jit(solution)/shard_map/ppermute | solution.py:576
  113.4 4.5 %collective-permute-done.26.second = bf16[1,11136]{1,0:T(2,128)(2,1)S(1)} collective-permute-done((bf16[1,11136]{1,0:T(2,128)(2,1)S(1)}, bf16[1,11136]{1,0:T(2,128)(2,1)S(1)}, u32[]{:S(2)}, u32[]{:S(2)}) %collective-permute-start.26) | collective-permute-done | bytes 22304 | tf_op jit(solution)/shard_map/ppermute | solution.py:576
  118.1 2.0 %collective-permute-start.35 = (bf16[96,1536]{1,0:T(8,128)(2,1)S(1)}, bf16[96,1536]{1,0:T(8,128)(2,1)S(1)}, u32[]{:S(2)}, u32[]{:S(2)}) collective-permute-start(bf16[96,1536]{1,0:T(8,128)(2,1)S(1)} %get-tuple-element.163), channel_id=1, source_target_pairs={{0,16},{1,9},{2,18},{3,11},{4,20},{5,13},{6,22},{7,15},{8,24},{9,1... | collective-permute-start | bytes 884744 | tf_op jit(solution)/shard_map/ppermute | solution.py:576
  120.1 2.0 %collective-permute-done.27.second = bf16[2,11136]{1,0:T(2,128)(2,1)S(1)} collective-permute-done((bf16[2,11136]{1,0:T(2,128)(2,1)S(1)}, bf16[2,11136]{1,0:T(2,128)(2,1)S(1)}, u32[]{:S(2)}, u32[]{:S(2)}) %collective-permute-start.27) | collective-permute-done | bytes 44576 | tf_op jit(solution)/shard_map/ppermute | solution.py:576
  122.1 2.0 %group.1 = (f32[2,384]{1,0:T(2,128)S(1)}, f32[2,384]{1,0:T(2,128)S(1)}, bf16[4,11136]{1,0:T(4,128)(2,1)S(1)}) custom-call(s32[3]{0:T(128)S(1)} %pad_add_fusion.refs_0_.idx, bf16[2,96,2304]{2,1,0:T(8,128)(2,1)S(1)} %copy-done.9, bf16[2,11136]{1,0:T(2,128)(2,1)S(1)} %stack.18.first, bf16[2,11136]{1,0:T(2,128)(2,1)S(1)} %collective-permute-done.27.second), custom_call_target="tpu_custom_call" | custom-call | flops 1 | bytes 1 | tf_op jit(solution)/shard_map/group/pallas_call | solution.py:68
  125.8 2.7 %collective-permute-start.31 = (bf16[48,2304]{1,0:T(8,128)(2,1)S(1)}, bf16[48,2304]{1,0:T(8,128)(2,1)S(1)}, u32[]{:S(2)}, u32[]{:S(2)}) collective-permute-start(bf16[48,2304]{1,0:T(8,128)(2,1)S(1)} %add.84.refs_0_), channel_id=1, source_target_pairs={{0,4},{1,5},{2,6},{3,7},{4,0},{5,1},{6,2},{7,3},{8,12},{9,13},{10,... | collective-permute-start | bytes 663560 | tf_op jit(solution)/shard_map/ppermute | solution.py:576
  128.7 4.3 %collective-permute-start.46 = (bf16[8,11136]{1,0:T(8,128)(2,1)S(1)}, bf16[8,11136]{1,0:T(8,128)(2,1)S(1)}, u32[]{:S(2)}, u32[]{:S(2)}) collective-permute-start(bf16[8,11136]{1,0:T(8,128)(2,1)S(1)} %stack.19.refs_1_), channel_id=1, source_target_pairs={{0,4},{1,5},{2,6},{3,7},{4,0},{5,1},{6,2},{7,3},{8,12},{9,13},{10,... | collective-permute-start | bytes 534536 | tf_op jit(solution)/shard_map/ppermute | solution.py:576
  133.0 2.0 %collective-permute-start.28 = (f32[2,384]{1,0:T(2,128)S(1)}, f32[2,384]{1,0:T(2,128)S(1)}, u32[]{:S(2)}, u32[]{:S(2)}) collective-permute-start(f32[2,384]{1,0:T(2,128)S(1)} %get-tuple-element.159), channel_id=1, source_target_pairs={{0,16},{1,9},{2,18},{3,11},{4,20},{5,13},{6,22},{7,15},{8,24},{9,1... | collective-permute-start | bytes 9224 | tf_op jit(solution)/shard_map/ppermute | solution.py:576
  135.1 3.1 %collective-permute-done.28 = f32[2,384]{1,0:T(2,128)S(1)} collective-permute-done((f32[2,384]{1,0:T(2,128)S(1)}, f32[2,384]{1,0:T(2,128)S(1)}, u32[]{:S(2)}, u32[]{:S(2)}) %collective-permute-start.28) | collective-permute-done | bytes 3104 | tf_op jit(solution)/shard_map/ppermute | solution.py:576
  138.7 2.4 %collective-permute-start.32 = (bf16[48,2304]{1,0:T(8,128)(2,1)S(1)}, bf16[48,2304]{1,0:T(8,128)(2,1)S(1)}, u32[]{:S(2)}, u32[]{:S(2)}) collective-permute-start(bf16[48,2304]{1,0:T(8,128)(2,1)S(1)} %add.85.refs_1_), channel_id=1, source_target_pairs={{0,2},{1,3},{2,0},{3,1},{4,6},{5,7},{6,4},{7,5},{8,10},{9,11},{10,... | collective-permute-start | bytes 663560 | tf_op jit(solution)/shard_map/ppermute | solution.py:576
  141.9 2.5 %collective-permute-start.36 = (bf16[48,1536]{1,0:T(8,128)(2,1)S(1)}, bf16[48,1536]{1,0:T(8,128)(2,1)S(1)}, u32[]{:S(2)}, u32[]{:S(2)}) collective-permute-start(bf16[48,1536]{1,0:T(8,128)(2,1)S(1)} %get-tuple-element.165), channel_id=1, source_target_pairs={{0,2},{1,3},{2,0},{3,1},{4,6},{5,7},{6,4},{7,5},{8,10},{9,11},{10,... | collective-permute-start | bytes 442376 | tf_op jit(solution)/shard_map/ppermute | solution.py:576
  144.9 5.5 %collective-permute-done.42.refs_1_ = bf16[96,768]{1,0:T(8,128)(2,1)S(1)} collective-permute-done((bf16[96,768]{1,0:T(8,128)(2,1)S(1)}, bf16[96,768]{1,0:T(8,128)(2,1)S(1)}, u32[]{:S(2)}, u32[]{:S(2)}) %collective-permute-start.42) | collective-permute-done | bytes 147488 | tf_op jit(solution)/shard_map/ppermute | solution.py:576
  150.5 2.9 %collective-permute-done.36.refs_1_ = bf16[48,1536]{1,0:T(8,128)(2,1)S(1)} collective-permute-done((bf16[48,1536]{1,0:T(8,128)(2,1)S(1)}, bf16[48,1536]{1,0:T(8,128)(2,1)S(1)}, u32[]{:S(2)}, u32[]{:S(2)}) %collective-permute-start.36) | collective-permute-done | bytes 147488 | tf_op jit(solution)/shard_map/ppermute | solution.py:576
  154.3 2.2 %collective-permute-start.37 = (bf16[48,1536]{1,0:T(8,128)(2,1)S(1)}, bf16[48,1536]{1,0:T(8,128)(2,1)S(1)}, u32[]{:S(2)}, u32[]{:S(2)}) collective-permute-start(bf16[48,1536]{1,0:T(8,128)(2,1)S(1)} %add.86.refs_0_), channel_id=1, source_target_pairs={{0,4},{1,5},{2,6},{3,7},{4,0},{5,1},{6,2},{7,3},{8,12},{9,13},{10,... | collective-permute-start | bytes 442376 | tf_op jit(solution)/shard_map/ppermute | solution.py:576
  156.5 2.3 %ada_grad.1 = (f32[2,96,2304]{2,1,0:T(8,128)}, f32[1,10752]{1,0:T(1,128)S(1)}) custom-call(s32[3]{0:T(128)S(1)} %pad_add_fusion.refs_0_.idx, bf16[8,11136]{1,0:T(8,128)(2,1)S(1)} %stack.19.refs_1_, bf16[8,11136]{1,0:T(8,128)(2,1)S(1)} %collective-permute-done.46.refs_2_, bf16[8,11136]{1,0:T(8,128)(2,1)S(1)} %collective-permute-done.47.refs_3_, ...), custom_call_target="tpu_custom_call" | custom-call | flops 1 | bytes 1 | tf_op jit(solution)/shard_map/ada_grad/pallas_call | solution.py:68
  158.8 10.6 %collective-permute-done.37.refs_1_ = bf16[48,1536]{1,0:T(8,128)(2,1)S(1)} collective-permute-done((bf16[48,1536]{1,0:T(8,128)(2,1)S(1)}, bf16[48,1536]{1,0:T(8,128)(2,1)S(1)}, u32[]{:S(2)}, u32[]{:S(2)}) %collective-permute-start.37) | collective-permute-done | bytes 147488 | tf_op jit(solution)/shard_map/ppermute | solution.py:576
  171.5 3.2 %collective-permute-done.38.refs_6_ = bf16[48,1536]{1,0:T(8,128)(2,1)S(1)} collective-permute-done((bf16[48,1536]{1,0:T(8,128)(2,1)S(1)}, bf16[48,1536]{1,0:T(8,128)(2,1)S(1)}, u32[]{:S(2)}, u32[]{:S(2)}) %collective-permute-start.38) | collective-permute-done | bytes 147488 | tf_op jit(solution)/shard_map/ppermute | solution.py:576
  176.1 2.6 %finish.1 = (f32[2,96,1152]{2,1,0:T(8,128)}, f32[2,96,384]{2,1,0:T(8,128)}, f32[2,96,1536]{2,1,0:T(8,128)}, f32[2,384,384]{2,1,0:T(8,128)}) custom-call(s32[3]{0:T(128)S(1)} %pad_add_fusion.refs_0_.idx, bf16[48,2304]{1,0:T(8,128)(2,1)S(1)} %add.85.refs_1_, bf16[48,2304]{1,0:T(8,128)(2,1)S(1)} %collective-permute-done.32.refs_2_, ...), custom_call_target="tpu_custom_call" | custom-call | flops 1 | bytes 1 | tf_op jit(solution)/shard_map/finish/pallas_call | solution.py:68
  (187 shorter events, 48.6 us)
Async XLA Ops:
  5.7 15.7 %collective-permute-start.7 = (bf16[96,1536]{1,0:T(8,128)(2,1)}, bf16[96,1536]{1,0:T(8,128)(2,1)}, u32[]{:S(2)}, u32[]{:S(2)}) collective-permute-start(bf16[96,1536]{1,0:T(8,128)(2,1)} %get-tuple-element.100), channel_id=1, source_target_pairs={{0,8},{1,17},{2,10},{3,19},{4,12},{5,21},{6,14},{7,23},{8,0},{9,25... | collective-permute-start | bytes 884744 | tf_op jit(solution)/shard_map/ppermute | solution.py:576
  12.2 14.2 %collective-permute-start.6 = (bf16[96,3072]{1,0:T(8,128)(2,1)}, bf16[96,3072]{1,0:T(8,128)(2,1)S(1)}, u32[]{:S(2)}, u32[]{:S(2)}) collective-permute-start(bf16[96,3072]{1,0:T(8,128)(2,1)} %get-tuple-element.98), channel_id=1, source_target_pairs={{0,8},{1,17},{2,10},{3,19},{4,12},{5,21},{6,14},{7,23},{8,0},{9,25... | collective-permute-start | bytes 1769480 | tf_op jit(solution)/shard_map/ppermute | solution.py:576
  17.8 6.8 %collective-permute-start.3 = (f32[2,5376]{1,0:T(2,128)S(1)}, f32[2,5376]{1,0:T(2,128)S(1)}, u32[]{:S(2)}, u32[]{:S(2)}) collective-permute-start(f32[2,5376]{1,0:T(2,128)S(1)} %get-tuple-element.95), channel_id=1, source_target_pairs={{0,8},{1,9},{2,10},{3,11},{4,12},{5,13},{6,14},{7,15},{8,0},{9,1},... | collective-permute-start | bytes 129032 | tf_op jit(solution)/shard_map/ppermute | solution.py:576
  19.4 5.2 %collective-permute-start.4 = (f32[2,5376]{1,0:T(2,128)S(1)}, f32[2,5376]{1,0:T(2,128)S(1)}, u32[]{:S(2)}, u32[]{:S(2)}) collective-permute-start(f32[2,5376]{1,0:T(2,128)S(1)} %get-tuple-element.96), channel_id=1, source_target_pairs={{0,16},{1,17},{2,18},{3,19},{4,20},{5,21},{6,22},{7,23},{8,24},{9,... | collective-permute-start | bytes 129032 | tf_op jit(solution)/shard_map/ppermute | solution.py:576
  19.9 6.4 %collective-permute-start.5 = (f32[2,5376]{1,0:T(2,128)S(1)}, f32[2,5376]{1,0:T(2,128)S(1)}, u32[]{:S(2)}, u32[]{:S(2)}) collective-permute-start(f32[2,5376]{1,0:T(2,128)S(1)} %get-tuple-element.97), channel_id=1, source_target_pairs={{0,24},{1,25},{2,26},{3,27},{4,28},{5,29},{6,30},{7,31},{8,16},{9,... | collective-permute-start | bytes 129032 | tf_op jit(solution)/shard_map/ppermute | solution.py:576
  23.0 5.7 %collective-permute-start.8 = (bf16[96,768]{1,0:T(8,128)(2,1)}, bf16[96,768]{1,0:T(8,128)(2,1)}, u32[]{:S(2)}, u32[]{:S(2)}) collective-permute-start(bf16[96,768]{1,0:T(8,128)(2,1)} %constant_dynamic-slice_fusion.6), channel_id=1, source_target_pairs={{0,16},{1,9},{2,18},{3,11},{4,20},{5,13},{6,22},{7,15},{8,24},{9,1... | collective-permute-start | bytes 442376 | tf_op jit(solution)/shard_map/ppermute | solution.py:576
  24.6 5.6 %collective-permute-start.9 = (bf16[96,1536]{1,0:T(8,128)(2,1)}, bf16[96,1536]{1,0:T(8,128)(2,1)}, u32[]{:S(2)}, u32[]{:S(2)}) collective-permute-start(bf16[96,1536]{1,0:T(8,128)(2,1)} %collective-permute-done.7.refs_5_.refs_10_), channel_id=1, source_target_pairs={{0,1},{1,0},{2,3},{3,2},{4,5},{5,4},{6,7},{7,6},{8,9},{9,8},{10,11... | collective-permute-start | bytes 884744 | tf_op jit(solution)/shard_map/ppermute | solution.py:576
  26.4 21.0 %collective-permute-start.14 = (bf16[96,4608]{1,0:T(8,128)(2,1)}, bf16[96,4608]{1,0:T(8,128)(2,1)S(1)}, u32[]{:S(2)}, u32[]{:S(2)}) collective-permute-start(bf16[96,4608]{1,0:T(8,128)(2,1)} %pack.3), channel_id=1, source_target_pairs={{0,8},{1,17},{2,10},{3,19},{4,12},{5,21},{6,14},{7,23},{8,0},{9,25... | collective-permute-start | bytes 2654216 | tf_op jit(solution)/shard_map/ppermute | solution.py:576
  28.7 11.0 %collective-permute-start.11 = (bf16[96,1536]{1,0:T(8,128)(2,1)S(1)}, bf16[96,1536]{1,0:T(8,128)(2,1)}, u32[]{:S(2)}, u32[]{:S(2)}) collective-permute-start(bf16[96,1536]{1,0:T(8,128)(2,1)S(1)} %constant_dynamic-slice_fusion.5), channel_id=1, source_target_pairs={{0,16},{1,9},{2,18},{3,11},{4,20},{5,13},{6,22},{7,15},{8,24},{9,1... | collective-permute-start | bytes 884744 | tf_op jit(solution)/shard_map/ppermute | solution.py:576
  47.4 8.4 %collective-permute-start.15 = (bf16[96,2304]{1,0:T(8,128)(2,1)S(1)}, bf16[96,2304]{1,0:T(8,128)(2,1)S(1)}, u32[]{:S(2)}, u32[]{:S(2)}) collective-permute-start(bf16[96,2304]{1,0:T(8,128)(2,1)S(1)} %constant_dynamic-slice_fusion.4), channel_id=1, source_target_pairs={{0,16},{1,9},{2,18},{3,11},{4,20},{5,13},{6,22},{7,15},{8,24},{9,1... | collective-permute-start | bytes 1327112 | tf_op jit(solution)/shard_map/ppermute | solution.py:576
  47.5 10.1 %collective-permute-start.16 = (bf16[96,4608]{1,0:T(8,128)(2,1)S(1)}, bf16[96,4608]{1,0:T(8,128)(2,1)S(1)}, u32[]{:S(2)}, u32[]{:S(2)}) collective-permute-start(bf16[96,4608]{1,0:T(8,128)(2,1)S(1)} %collective-permute-done.14.refs_5_.refs_6_.refs_10_), channel_id=1, source_target_pairs={{0,1},{1,0},{2,3},{3,2},{4,5},{5,4},{6,7},{7,6},{8,9},{9,8},{10,11... | collective-permute-start | bytes 2654216 | tf_op jit(solution)/shard_map/ppermute | solution.py:576
  67.7 8.2 %collective-permute-start.19 = (bf16[4,96,1536]{2,1,0:T(8,128)(2,1)S(1)}, bf16[4,96,1536]{2,1,0:T(8,128)(2,1)S(1)}, u32[]{:S(2)}, u32[]{:S(2)}) collective-permute-start(bf16[4,96,1536]{2,1,0:T(8,128)(2,1)S(1)} %get-tuple-element.121), channel_id=1, source_target_pairs={{0,1},{1,0},{2,3},{3,2},{4,5},{5,4},{6,7},{7,6},{8,9},{9,8},{10,11... | collective-permute-start | bytes 3538952 | tf_op jit(solution)/shard_map/ppermute | solution.py:576
  76.3 15.8 %collective-permute-start.20 = (bf16[2,96,2304]{2,1,0:T(8,128)(2,1)S(1)}, bf16[2,96,2304]{2,1,0:T(8,128)(2,1)S(1)}, u32[]{:S(2)}, u32[]{:S(2)}) collective-permute-start(bf16[2,96,2304]{2,1,0:T(8,128)(2,1)S(1)} %get-tuple-element.139), channel_id=1, source_target_pairs={{0,8},{1,17},{2,10},{3,19},{4,12},{5,21},{6,14},{7,23},{8,0},{9,25... | collective-permute-start | bytes 2654216 | tf_op jit(solution)/shard_map/ppermute | solution.py:576
  83.8 9.0 %collective-permute-start.21 = (bf16[4,96,1536]{2,1,0:T(8,128)(2,1)S(1)}, bf16[4,96,1536]{2,1,0:T(8,128)(2,1)S(1)}, u32[]{:S(2)}, u32[]{:S(2)}) collective-permute-start(bf16[4,96,1536]{2,1,0:T(8,128)(2,1)S(1)} %get-tuple-element.143), channel_id=1, source_target_pairs={{0,1},{1,0},{2,3},{3,2},{4,5},{5,4},{6,7},{7,6},{8,9},{9,8},{10,11... | collective-permute-start | bytes 3538952 | tf_op jit(solution)/shard_map/ppermute | solution.py:576
  91.5 14.8 %collective-permute-start.23 = (bf16[4,96,768]{2,1,0:T(8,128)(2,1)S(1)}, bf16[4,96,768]{2,1,0:T(8,128)(2,1)S(1)}, u32[]{:S(2)}, u32[]{:S(2)}) collective-permute-start(bf16[4,96,768]{2,1,0:T(8,128)(2,1)S(1)} %get-tuple-element.149), channel_id=1, source_target_pairs={{0,1},{1,0},{2,3},{3,2},{4,5},{5,4},{6,7},{7,6},{8,9},{9,8},{10,11... | collective-permute-start | bytes 1769480 | tf_op jit(solution)/shard_map/ppermute | solution.py:576
  92.4 13.1 %collective-permute-start.22 = (bf16[96,2304]{1,0:T(8,128)(2,1)S(1)}, bf16[96,2304]{1,0:T(8,128)(2,1)S(1)}, u32[]{:S(2)}, u32[]{:S(2)}) collective-permute-start(bf16[96,2304]{1,0:T(8,128)(2,1)S(1)} %get-tuple-element.146), channel_id=1, source_target_pairs={{0,16},{1,9},{2,18},{3,11},{4,20},{5,13},{6,22},{7,15},{8,24},{9,1... | collective-permute-start | bytes 1327112 | tf_op jit(solution)/shard_map/ppermute | solution.py:576
  93.1 15.1 %collective-permute-start.24 = (bf16[2,96,1536]{2,1,0:T(8,128)(2,1)S(1)}, bf16[2,96,1536]{2,1,0:T(8,128)(2,1)S(1)}, u32[]{:S(2)}, u32[]{:S(2)}) collective-permute-start(bf16[2,96,1536]{2,1,0:T(8,128)(2,1)S(1)} %get-tuple-element.152), channel_id=1, source_target_pairs={{0,8},{1,17},{2,10},{3,19},{4,12},{5,21},{6,14},{7,23},{8,0},{9,25... | collective-permute-start | bytes 1769480 | tf_op jit(solution)/shard_map/ppermute | solution.py:576
  106.5 6.8 %collective-permute-start.25 = (bf16[2,96,768]{2,1,0:T(8,128)(2,1)S(1)}, bf16[2,96,768]{2,1,0:T(8,128)(2,1)S(1)}, u32[]{:S(2)}, u32[]{:S(2)}) collective-permute-start(bf16[2,96,768]{2,1,0:T(8,128)(2,1)S(1)} %get-tuple-element.155), channel_id=1, source_target_pairs={{0,8},{1,17},{2,10},{3,19},{4,12},{5,21},{6,14},{7,23},{8,0},{9,25... | collective-permute-start | bytes 884744 | tf_op jit(solution)/shard_map/ppermute | solution.py:576
  106.6 19.2 %collective-permute-start.30 = (bf16[48,2304]{1,0:T(8,128)(2,1)S(1)}, bf16[48,2304]{1,0:T(8,128)(2,1)S(1)}, u32[]{:S(2)}, u32[]{:S(2)}) collective-permute-start(bf16[48,2304]{1,0:T(8,128)(2,1)S(1)} %get-tuple-element.161), channel_id=1, source_target_pairs={{0,2},{1,3},{2,0},{3,1},{4,6},{5,7},{6,4},{7,5},{8,10},{9,11},{10,... | collective-permute-start | bytes 663560 | tf_op jit(solution)/shard_map/ppermute | solution.py:576
  118.1 20.6 %collective-permute-start.35 = (bf16[96,1536]{1,0:T(8,128)(2,1)S(1)}, bf16[96,1536]{1,0:T(8,128)(2,1)S(1)}, u32[]{:S(2)}, u32[]{:S(2)}) collective-permute-start(bf16[96,1536]{1,0:T(8,128)(2,1)S(1)} %get-tuple-element.163), channel_id=1, source_target_pairs={{0,16},{1,9},{2,18},{3,11},{4,20},{5,13},{6,22},{7,15},{8,24},{9,1... | collective-permute-start | bytes 884744 | tf_op jit(solution)/shard_map/ppermute | solution.py:576
  125.8 12.8 %collective-permute-start.31 = (bf16[48,2304]{1,0:T(8,128)(2,1)S(1)}, bf16[48,2304]{1,0:T(8,128)(2,1)S(1)}, u32[]{:S(2)}, u32[]{:S(2)}) collective-permute-start(bf16[48,2304]{1,0:T(8,128)(2,1)S(1)} %add.84.refs_0_), channel_id=1, source_target_pairs={{0,4},{1,5},{2,6},{3,7},{4,0},{5,1},{6,2},{7,3},{8,12},{9,13},{10,... | collective-permute-start | bytes 663560 | tf_op jit(solution)/shard_map/ppermute | solution.py:576
  128.7 15.6 %collective-permute-start.46 = (bf16[8,11136]{1,0:T(8,128)(2,1)S(1)}, bf16[8,11136]{1,0:T(8,128)(2,1)S(1)}, u32[]{:S(2)}, u32[]{:S(2)}) collective-permute-start(bf16[8,11136]{1,0:T(8,128)(2,1)S(1)} %stack.19.refs_1_), channel_id=1, source_target_pairs={{0,4},{1,5},{2,6},{3,7},{4,0},{5,1},{6,2},{7,3},{8,12},{9,13},{10,... | collective-permute-start | bytes 534536 | tf_op jit(solution)/shard_map/ppermute | solution.py:576
  133.0 8.7 %collective-permute-start.41 = (bf16[96,768]{1,0:T(8,128)(2,1)S(1)}, bf16[96,768]{1,0:T(8,128)(2,1)S(1)}, u32[]{:S(2)}, u32[]{:S(2)}) collective-permute-start(bf16[96,768]{1,0:T(8,128)(2,1)S(1)} %get-tuple-element.167), channel_id=1, source_target_pairs={{0,16},{1,9},{2,18},{3,11},{4,20},{5,13},{6,22},{7,15},{8,24},{9,1... | collective-permute-start | bytes 442376 | tf_op jit(solution)/shard_map/ppermute | solution.py:576
  138.6 15.7 %collective-permute-start.47 = (bf16[8,11136]{1,0:T(8,128)(2,1)S(1)}, bf16[8,11136]{1,0:T(8,128)(2,1)S(1)}, u32[]{:S(2)}, u32[]{:S(2)}) collective-permute-start(bf16[8,11136]{1,0:T(8,128)(2,1)S(1)} %stack.19.refs_1_), channel_id=1, source_target_pairs={{0,1},{1,0},{2,3},{3,2},{4,5},{5,4},{6,7},{7,6},{8,9},{9,8},{10,11... | collective-permute-start | bytes 534536 | tf_op jit(solution)/shard_map/ppermute | solution.py:576
  138.7 17.8 %collective-permute-start.32 = (bf16[48,2304]{1,0:T(8,128)(2,1)S(1)}, bf16[48,2304]{1,0:T(8,128)(2,1)S(1)}, u32[]{:S(2)}, u32[]{:S(2)}) collective-permute-start(bf16[48,2304]{1,0:T(8,128)(2,1)S(1)} %add.85.refs_1_), channel_id=1, source_target_pairs={{0,2},{1,3},{2,0},{3,1},{4,6},{5,7},{6,4},{7,5},{8,10},{9,11},{10,... | collective-permute-start | bytes 663560 | tf_op jit(solution)/shard_map/ppermute | solution.py:576
  141.8 8.7 %collective-permute-start.42 = (bf16[96,768]{1,0:T(8,128)(2,1)S(1)}, bf16[96,768]{1,0:T(8,128)(2,1)S(1)}, u32[]{:S(2)}, u32[]{:S(2)}) collective-permute-start(bf16[96,768]{1,0:T(8,128)(2,1)S(1)} %add.88.refs_0_), channel_id=1, source_target_pairs={{0,2},{1,3},{2,0},{3,1},{4,6},{5,7},{6,4},{7,5},{8,10},{9,11},{10,... | collective-permute-start | bytes 442376 | tf_op jit(solution)/shard_map/ppermute | solution.py:576
  141.9 11.5 %collective-permute-start.36 = (bf16[48,1536]{1,0:T(8,128)(2,1)S(1)}, bf16[48,1536]{1,0:T(8,128)(2,1)S(1)}, u32[]{:S(2)}, u32[]{:S(2)}) collective-permute-start(bf16[48,1536]{1,0:T(8,128)(2,1)S(1)} %get-tuple-element.165), channel_id=1, source_target_pairs={{0,2},{1,3},{2,0},{3,1},{4,6},{5,7},{6,4},{7,5},{8,10},{9,11},{10,... | collective-permute-start | bytes 442376 | tf_op jit(solution)/shard_map/ppermute | solution.py:576
  144.4 12.1 %collective-permute-start.48 = (bf16[8,11136]{1,0:T(8,128)(2,1)S(1)}, bf16[8,11136]{1,0:T(8,128)(2,1)S(1)}, u32[]{:S(2)}, u32[]{:S(2)}) collective-permute-start(bf16[8,11136]{1,0:T(8,128)(2,1)S(1)} %collective-permute-done.46.refs_2_), channel_id=1, source_target_pairs={{0,1},{1,0},{2,3},{3,2},{4,5},{5,4},{6,7},{7,6},{8,9},{9,8},{10,11... | collective-permute-start | bytes 534536 | tf_op jit(solution)/shard_map/ppermute | solution.py:576
  150.5 25.6 %collective-permute-start.33 = (bf16[48,2304]{1,0:T(8,128)(2,1)S(1)}, bf16[48,2304]{1,0:T(8,128)(2,1)S(1)}, u32[]{:S(2)}, u32[]{:S(2)}) collective-permute-start(bf16[48,2304]{1,0:T(8,128)(2,1)S(1)} %add.85.refs_1_), channel_id=1, source_target_pairs={{0,1},{1,0},{2,3},{3,2},{4,5},{5,4},{6,7},{7,6},{8,9},{9,8},{10,11... | collective-permute-start | bytes 663560 | tf_op jit(solution)/shard_map/ppermute | solution.py:576
  153.4 17.5 %collective-permute-start.43 = (bf16[96,768]{1,0:T(8,128)(2,1)S(1)}, bf16[96,768]{1,0:T(8,128)(2,1)S(1)}, u32[]{:S(2)}, u32[]{:S(2)}) collective-permute-start(bf16[96,768]{1,0:T(8,128)(2,1)S(1)} %add.89.refs_0_), channel_id=1, source_target_pairs={{0,4},{1,5},{2,6},{3,7},{4,0},{5,1},{6,2},{7,3},{8,12},{9,13},{10,... | collective-permute-start | bytes 442376 | tf_op jit(solution)/shard_map/ppermute | solution.py:576
  154.3 15.2 %collective-permute-start.37 = (bf16[48,1536]{1,0:T(8,128)(2,1)S(1)}, bf16[48,1536]{1,0:T(8,128)(2,1)S(1)}, u32[]{:S(2)}, u32[]{:S(2)}) collective-permute-start(bf16[48,1536]{1,0:T(8,128)(2,1)S(1)} %add.86.refs_0_), channel_id=1, source_target_pairs={{0,4},{1,5},{2,6},{3,7},{4,0},{5,1},{6,2},{7,3},{8,12},{9,13},{10,... | collective-permute-start | bytes 442376 | tf_op jit(solution)/shard_map/ppermute | solution.py:576
  156.5 19.6 %collective-permute-start.34 = (bf16[48,2304]{1,0:T(8,128)(2,1)S(1)}, bf16[48,2304]{1,0:T(8,128)(2,1)S(1)}, u32[]{:S(2)}, u32[]{:S(2)}) collective-permute-start(bf16[48,2304]{1,0:T(8,128)(2,1)S(1)} %collective-permute-done.32.refs_2_), channel_id=1, source_target_pairs={{0,1},{1,0},{2,3},{3,2},{4,5},{5,4},{6,7},{7,6},{8,9},{9,8},{10,11... | collective-permute-start | bytes 663560 | tf_op jit(solution)/shard_map/ppermute | solution.py:576
  (48 other events, 206.8 us)

commit v3 on v2

--- a/solution.py
+++ b/solution.py
@@ -63,18 +63,24 @@
 
 
 def run(body, name, inputs, outputs, scratch=(), flops=0):
-    places = {"v": pltpu.VMEM, "a": pl.ANY, "s": pltpu.SMEM}
-    moved = sum(arr.size * arr.dtype.itemsize for arr, _ in inputs)
+    places = {"v": pltpu.VMEM, "k": pltpu.VMEM, "a": pl.ANY, "h": pl.ANY, "s": pltpu.SMEM}
+    arrays = [
+        pltpu.with_memory_space_constraint(arr, pltpu.HBM) if kind in "hk" else arr
+        for arr, kind in inputs
+    ]
     return pl.pallas_call(
         body,
-        out_shape=[jax.ShapeDtypeStruct(shape, dtype) for shape, dtype, _ in outputs],
+        out_shape=[
+            pltpu.HBM(shape, dtype) if kind in "hk" else jax.ShapeDtypeStruct(shape, dtype)
+            for shape, dtype, kind in outputs
+        ],
         in_specs=[pl.BlockSpec(memory_space=places[kind]) for _, kind in inputs],
         out_specs=[pl.BlockSpec(memory_space=places[kind]) for _, _, kind in outputs],
         scratch_shapes=list(scratch),
         compiler_params=pltpu.CompilerParams(vmem_limit_bytes=VMEM_LIMIT),
         cost_estimate=pl.CostEstimate(flops=1, bytes_accessed=1, transcendentals=0),
         name=name,
-    )(*[arr for arr, _ in inputs])
+    )(*arrays)
 
 
 def pack_kernel(plan, *refs):
@@ -99,6 +105,13 @@
                     pairs.append((piece, out.at[:, at : at + piece.shape[-1]]))
                     at += piece.shape[-1]
     copies = make_copies(pairs, sems)
+    start_all(copies)
+    wait_all(copies)
+
+
+def half_kernel(idx, whole, out, sems):
+    half = out.shape[1]
+    copies = make_copies([(whole.at[:, block_at(idx[2] * half, half)], out)], sems)
     start_all(copies)
     wait_all(copies)
 
@@ -587,8 +600,8 @@
     def pack(*plan):
         whole = run(
             functools.partial(pack_kernel, plan), "pack",
-            [(array, "a") for array in (w_qkv, w_proj, w_fc1, w_fc2)],
-            [((rows, 2 * sum(half_wide[kind] for kind in kinds)), BF, "a") for _, kinds in plan],
+            [(array, "h") for array in (w_qkv, w_proj, w_fc1, w_fc2)],
+            [((rows, 2 * sum(half_wide[kind] for kind in kinds)), BF, "v") for _, kinds in plan],
             [pltpu.SemaphoreType.DMA((sum(copy_total[kind] for _, ks in plan for kind in ks),))],
         )
         if relay:
@@ -603,21 +616,25 @@
             return [exchange(packed, turn=first_turn)]
         return [exchange(packed, by_shard=step) for step in range(1, n_shard)]
 
-    def near_second(near, *earlier):
+    def near_half(near, *earlier):
+        source = after(near[0], *earlier) if earlier else near[0]
         if not relay:
-            return near
-        half = near[0].shape[1] // 2
-        source = after(near[0], *earlier) if earlier else near[0]
-        part = lax.dynamic_slice_in_dim(source, core * half, half, axis=1)
-        return near + [exchange(part, turn=second_turn)]
+            return source
+        half = source.shape[1] // 2
+        return run(
+            half_kernel, "half", [(idx, "s"), (source, "a")],
+            [((source.shape[0], half), BF, "a")], [pltpu.SemaphoreType.DMA((1,))],
+        )[0]
+
+    def near_second(near, part):
+        return near + [exchange(part, turn=second_turn)] if relay else near
 
     def far_of(near, *earlier):
         return [exchange(after(piece, *earlier) if earlier else piece, by_core=1) for piece in near]
 
     conditions = [condition] + [exchange(condition, by_shard=step) for step in range(1, n_shard)]
-    packed_qkv, packed_mlp = pack((0, ("qkv",)), (0, ("mlp",)))
-    qkv_near = near_first(packed_qkv)
-    mlp_near = near_first(packed_mlp)
+    packed = [pack((layer, ("qkv", "mlp")))[0] for layer in range(layers)]
+    near = [near_first(own) for own in packed]
     pad_scratch = [pltpu.VMEM((width, layers * wide), BF), pltpu.SemaphoreType.DMA((layers,))]
     span = wide + 4 * width + hidden
     partial = run(
@@ -626,18 +643,14 @@
          (b_fc2, "v")] + [(array, "v") for array in conditions],
         [((layers, span), F32, "v")] * n_shard, pad_scratch, flops=10**7,
     )
+    parts = [near_half(near[0], partial[0])]
+    for own in near[1:]:
+        parts.append(near_half(own, parts[-1]))
+    near = [near_second(own, part) for own, part in zip(near, parts)]
     mod_all = partial[0]
     for step in range(1, n_shard):
-        mod_all = mod_all + exchange(partial[step], by_shard=step)
-
-    qkv_near = near_second(qkv_near)
-    qkv_far = far_of(qkv_near)
-    mod_all = after(mod_all, *mlp_near)
-    later_near = []
-    for layer in range(1, layers):
-        (packed,) = pack((layer, ("qkv", "mlp")))
-        later_near.append(near_first(after(packed, mod_all)))
-    mlp_near = near_second(mlp_near)
+        mod_all = mod_all + exchange(after(partial[step], *parts[1:]), by_shard=step)
+    pieces = {0: (near[0], far_of(near[0]))}
 
     big = seq * width
     row = lambda kind="v": ((seq, width), F32, kind)
@@ -659,21 +672,18 @@
     stream = latents[0]
     saved = []
     vecs, raw = {}, {}
-    qkv_pieces, mlp_pieces = {0: ((qkv_near, qkv_far), 0)}, {}
     for layer in range(layers):
-        pair, offset = qkv_pieces[layer]
+        pair, offset = pieces[layer], 0
+        keep_in = "v" if layer + 1 == layers else "k"
         qkv, probs, attended, branch, middle = run(
             functools.partial(attention_forward, layer, rows, offset, n_shard), "attention_forward",
             [(idx, "s"), (stream, "v"), (mod_all, "v"), (w_qkv, "a"), (w_proj, "a")]
             + piece_args(pair),
-            [((seq, 3 * width), BF, "v"), ((HEADS, seq, seq), F32, "v"), ((seq, width), BF, "v"),
-             row(), row()],
+            [((seq, 3 * width), BF, keep_in), ((HEADS, seq, seq), F32, keep_in),
+             ((seq, width), BF, keep_in), row(keep_in), row()],
             [w_qkv_all, qkv_sems], flops=10 * big * width,
         )
-        if layer == 0:
-            mlp_pieces[0] = ((mlp_near, far_of(mlp_near, middle)), 0)
-            later_near = [near_second(near, middle) for near in later_near]
-        pair, offset = mlp_pieces[layer]
+        pair, offset = pieces[layer], 2 * width
         entry = dict(stream=stream, qkv=qkv, probs=probs, attended=attended, branch=branch,
                      middle=middle)
         if layer + 1 < layers:
@@ -681,14 +691,11 @@
                 functools.partial(mlp_forward, layer, rows, offset, n_shard), "mlp_forward",
                 [(idx, "s"), (middle, "v"), (mod_all, "v"), (w_fc1, "a"), (w_fc2, "a")]
                 + piece_args(pair),
-                [((seq, hidden), BF, "v"), ((seq, hidden), F32, "v"), row(), row()],
+                [((seq, hidden), BF, keep_in), ((seq, hidden), F32, keep_in), row(keep_in), row()],
                 [w_mlp_all, mlp_sems], flops=16 * big * width,
             )
             entry.update(act_low=act_low, slopes=slopes, mlp_out=mlp_out)
-            near = later_near[layer]
-            later_pair = (near, far_of(near, stream))
-            qkv_pieces[layer + 1] = (later_pair, 0)
-            mlp_pieces[layer + 1] = (later_pair, 2 * width)
+            pieces[layer + 1] = (near[layer + 1], far_of(near[layer + 1], middle))
         else:
             x_out, d_middle, vecs["mlp", layer], *raw["mlp", layer] = run(
                 functools.partial(mlp_both, layer, rows, offset, n_shard), "mlp_both",
@@ -753,8 +760,7 @@
             kept = after(kept, *earlier)
         return halved, add([kept, arriving], kept.shape)
 
-    def level_last(halved, total):
-        step = 2
+    def level_last(halved, total, step):
         while step < levels:
             total = add([total, exchange(total, by_level=step)], total.shape)
             step *= 2
@@ -764,7 +770,7 @@
     waiting = []
     for layer in reversed(range(layers)):
         entry = saved[layer]
-        pair, offset = mlp_pieces[layer]
+        pair, offset = pieces[layer], 2 * width
         if layer + 1 < layers:
             keys = [("qkv", layer + 1), ("mlp", layer + 1)]
             summed = core_sum(keys, grad_stream)
@@ -778,7 +784,10 @@
                 [row(), ((1, vec_wide["mlp"]), F32, "v")] + grads_out("mlp"),
                 [w_mlp_all, w_mlp_all, mlp_sems, out_sems], flops=32 * big * width,
             )
-        pair, offset = qkv_pieces[layer]
+            core_mlp = core_sum([("mlp", layer)], d_middle)
+            sent_mlp = shard_send(core_mlp)
+            d_middle = after(d_middle, core_mlp[0])
+        pair, offset = pieces[layer], 0
         grad_stream, vecs["qkv", layer], *raw["qkv", layer] = run(
             functools.partial(attention_backward, layer, rows, offset, n_shard),
             "attention_backward",
@@ -789,23 +798,13 @@
             [w_qkv_all, pltpu.VMEM((seq, 3 * width), BF), w_qkv_all, qkv_sems, out_sems],
             flops=28 * big * width,
         )
-    (keys_first, summed, arrived), = waiting
-    terms_first = shard_second(summed, arrived, grad_stream)
-    core_mlp = core_sum([("mlp", 0)], terms_first[0])
-    sent_mlp = shard_send(core_mlp)
-    level_a = level_first(terms_first, True, core_mlp[0])
-    core_qkv = core_sum([("qkv", 0)], level_a[1])
-    sent_qkv = shard_send(core_qkv)
-    terms_mlp = shard_second(core_mlp, sent_mlp, core_qkv[0])
-    terms_qkv = shard_second(core_qkv, sent_qkv, terms_mlp[0])
-
     cond_in = condition.astype(F32)
     vector = [jax.nn.silu(cond_in).astype(BF)]
     for layer in range(layers):
         vector += [vecs[kind, layer][:, : 3 * width].astype(BF) for kind in ("qkv", "mlp")]
     for layer in range(layers):
         vector += [vecs[kind, layer][:, 3 * width :].astype(BF) for kind in ("qkv", "mlp")]
-    vector = after(jnp.concatenate(vector, axis=1), terms_qkv[0])
+    vector = jnp.concatenate(vector, axis=1)
     length = vector.shape[1]
     masks = [first_turn, second_turn] if relay else []
     while not relay and 2 ** len(masks) < n_shard:
@@ -818,30 +817,50 @@
             [pltpu.VMEM(shape, F32)],
         )[0]
 
-    total_a = level_second(level_a, vector)
-    level_b = level_first(terms_mlp, True, total_a[1])
-    level_c = level_first(terms_qkv, False, level_b[1])
+    (keys_first, core_first, sent_first), = waiting
     plan = [keys_first, [("mlp", 0)], [("qkv", 0)]]
-    finals = [level_last(*total_a), level_last(*level_second(level_b)),
-              level_last(*level_second(level_c))]
-    for mask in masks[:-1]:
+    a = shard_second(core_first, sent_first, grad_stream)
+    vector = after(vector, a[0])
+    for mask in masks[:-2]:
         vector = stack(vector, exchange(vector, turn=mask))
+    arriving = exchange(vector, turn=masks[-2])
+    core_qkv = core_sum(plan[2], vector)
+    sent_qkv = shard_send(core_qkv)
+    b = shard_second(core_mlp, sent_mlp, core_qkv[0])
+    vector = after(vector, b[0])
+    vector = stack(after(vector, core_qkv[0]), arriving)
+    arriving = exchange(vector, turn=masks[-1])
+    a = level_first(a, True, vector)
     grad_cond, passed, stacked = run(
         group_kernel, "group",
-        [(idx, "s"), (w_ada, "a"), (vector, "v"), (exchange(vector, turn=masks[-1]), "v")],
+        [(idx, "s"), (w_ada, "a"), (after(vector, a[1]), "v"), (arriving, "v")],
         [((n_shard // 2, width), F32, "v")] * 2 + [((n_shard, length), BF, "v")],
         [pltpu.VMEM((n_shard, length), F32)] + pad_scratch, flops=10**7,
     )
+    arriving = exchange(stacked, by_level=1)
+    c = shard_second(core_qkv, sent_qkv, stacked)
+    a = level_second(a, c[0])
+    a_moving = exchange(a[1], by_level=2)
+    b = level_first(b, True, a[1])
+    stacked = stack(after(stacked, b[1]), arriving)
+    step = 2
+    while 2 * step < levels:
+        stacked = stack(stacked, exchange(stacked, by_level=step))
+        step *= 2
+    arriving = exchange(stacked, by_level=step)
+    c = level_first(c, False, stacked)
+    a = (a[0], add([after(a[1], c[1]), a_moving], a[1].shape))
+    a_parts = level_last(*a, 4)
+    b = level_second(b, a[1])
+    b_moving = exchange(b[1], by_level=2)
+    c = level_second(c, b[1])
+    c_moving = exchange(c[1], by_level=2)
     grad_cond = grad_cond + exchange(passed, turn=masks[-1])
     for mask in masks[-2::-1]:
         half = grad_cond.shape[0] // 2
         grad_cond = grad_cond[:half] + exchange(grad_cond[half:], turn=mask)
     cond_grad = jax.vjp(jax.nn.silu, cond_in)[1](grad_cond)[0]
-    step = 1
-    while 2 * step < levels:
-        stacked = stack(stacked, exchange(stacked, by_level=step))
-        step *= 2
-    stacks = [stacked, exchange(stacked, by_level=step)]
+    stacks = [after(stacked, c[1]), arriving]
     stacks = stacks + far_of(stacks)
     grad_ada, sums = run(
         functools.partial(ada_grad_kernel, rows, wide, factor), "ada_grad",
@@ -850,6 +869,11 @@
         [pltpu.VMEM((width, total_latents), F32), pltpu.VMEM((total_latents, length), F32)],
         flops=10**8,
     )
+
+    b = (b[0], add([after(b[1], sums), b_moving], b[1].shape))
+    b_parts = level_last(*b, 4)
+    c = (c[0], add([after(c[1], b[1]), c_moving], c[1].shape))
+    finals = [a_parts, b_parts, level_last(*c, 4)]
 
     def own_part(parts):
         whole = jnp.concatenate(parts, axis=0)

time: 179 us -> 164 us (0.916)
  waiting for transfers between devices: 68.9 us -> 59.3 us
  local copies, waits for them, and re-layouts: 11 us -> 4.29 us
  Pallas kernels: 51.9 us -> 53.8 us
    ppermute x49 -> x45, waiting for transfers between devices: 68.9 us -> 59.3 us  [exchange(): return lax.ppermute(array, ('shard', 'rep'), moves)]
    unnamed x69 -> x47, local copies, waits for them, and re-layouts: 9.35 us -> 4.26 us
    pallas_call x30 -> x32, Pallas kernels: 51.9 us -> 53.8 us  [run(): pl.pallas_call(body, out_shape=[pltpu.HBM(shape, dtype) if kind in 'hk' e...]
    ppermute x49 -> x45, starting transfers between devices: 42.1 us -> 42 us  [exchange(): return lax.ppermute(array, ('shard', 'rep'), moves)]
  transfers between devices with their start and end apart: 49 -> 45, of which waited for: 21 -> 16; matrix products, arithmetic and copies ran while one was open for 3% -> 2% of each run, Pallas kernels for 21% -> 21%
where the time goes in v3:
time: 164 us
  waiting for transfers between devices  59.3 us (36%)
  Pallas kernels  53.8 us (33%)
  starting transfers between devices  42 us (26%)
  local copies, waits for them, and re-layouts  4.29 us (3%)
  other arithmetic  3.39 us (2%)
    ppermute x45, waiting for transfers between devices, exchange(): return lax.ppermute(array, ('shard', 'rep'), moves)  59.3 us
    pallas_call x32, Pallas kernels, run(): pl.pallas_call(body, out_shape=[pltpu.HBM(shape, dtype) if kind in 'hk' e...  53.8 us
    ppermute x45, starting transfers between devices, exchange(): return lax.ppermute(array, ('shard', 'rep'), moves)  42 us
    unnamed x47, local copies, waits for them, and re-layouts  4.26 us
  transfers between devices with their start and end apart: 45, of which 16 were waited for; matrix products, arithmetic and copies ran while one was open for 2% of the time, Pallas kernels for 21%

profile of v3, /device:TPU:0, one launch (start us, length us, event | category | flops | bytes accessed | tf_op | source)
XLA Modules:
  0.0 164.0 jit_solution(10553279005561953107)
XLA Ops:
  0.6 2.2 %pack.3 = bf16[96,4608]{1,0:T(8,128)(2,1)} custom-call(bf16[2,96,1152]{2,1,0:T(8,128)(2,1)} %refs_8_.5, bf16[2,96,384]{2,1,0:T(8,128)(2,1)} %refs_9_.3, bf16[2,96,1536]{2,1,0:T(8,128)(2,1)} %refs_7_.3, bf16[2,384,384]{2,1,0:T(8,128)(2,1)} %refs_8_.4), custom_call_target="tpu_custom_call" | custom-call | flops 1 | bytes 1 | tf_op jit(solution)/shard_map/pack/pallas_call | solution.py:71
  2.9 3.0 %collective-permute-start.4 = (bf16[96,4608]{1,0:T(8,128)(2,1)}, bf16[96,4608]{1,0:T(8,128)(2,1)S(1)}, u32[]{:S(2)}, u32[]{:S(2)}) collective-permute-start(bf16[96,4608]{1,0:T(8,128)(2,1)} %pack.3), channel_id=1, source_target_pairs={{0,8},{1,17},{2,10},{3,19},{4,12},{5,21},{6,14},{7,23},{8,0},{9,25... | collective-permute-start | bytes 2654216 | tf_op jit(solution)/shard_map/ppermute | solution.py:589
  7.3 2.0 %collective-permute-start = (bf16[1,384]{1,0:T(2,128)(2,1)S(1)}, bf16[1,384]{1,0:T(2,128)(2,1)}, u32[]{:S(2)}, u32[]{:S(2)}) collective-permute-start(bf16[1,384]{1,0:T(2,128)(2,1)S(1)} %copy-done.14), channel_id=1, source_target_pairs={{0,8},{1,9},{2,10},{3,11},{4,12},{5,13},{6,14},{7,15},{8,0},{9,1},... | collective-permute-start | bytes 2312 | tf_op jit(solution)/shard_map/ppermute | solution.py:589
  10.9 15.9 %collective-permute-done.refs_8_ = bf16[1,384]{1,0:T(2,128)(2,1)} collective-permute-done((bf16[1,384]{1,0:T(2,128)(2,1)S(1)}, bf16[1,384]{1,0:T(2,128)(2,1)}, u32[]{:S(2)}, u32[]{:S(2)}) %collective-permute-start) | collective-permute-done | bytes 800 | tf_op jit(solution)/shard_map/ppermute | solution.py:589
  30.3 2.6 %modulate.1 = (f32[2,5376]{1,0:T(2,128)S(1)}, f32[2,5376]{1,0:T(2,128)S(1)}, f32[2,5376]{1,0:T(2,128)S(1)}, f32[2,5376]{1,0:T(2,128)S(1)}) custom-call(s32[3]{0:T(128)S(1)} %pad_add_fusion.refs_0_.idx, bf16[2,96,2304]{2,1,0:T(8,128)(2,1)S(1)} %copy-done.4, bf16[2,576]{1,0:T(2,128)(2,1)S(1)} %copy-done.15, bf16[2,192]{1,0:T(2,128)(2,1)S(1)} %copy-done.17, ...), custom_call_target="tpu_custom_call" | custom-call | flops 1 | bytes 1 | tf_op jit(solution)/shard_map/modulate/pallas_call | solution.py:71
  39.7 2.6 %collective-permute-done.8.refs_6_.refs_10_.refs_11_ = bf16[96,2304]{1,0:T(8,128)(2,1)S(1)} collective-permute-done((bf16[96,2304]{1,0:T(8,128)(2,1)S(1)}, bf16[96,2304]{1,0:T(8,128)(2,1)S(1)}, u32[]{:S(2)}, u32[]{:S(2)}) %collective-permute-start.8) | collective-permute-done | bytes 442400 | tf_op jit(solution)/shard_map/ppermute | solution.py:589
  44.2 4.3 %attention_forward.2 = (bf16[256,1152]{1,0:T(8,128)(2,1)}, f32[6,256,256]{2,1,0:T(8,128)}, bf16[256,384]{1,0:T(8,128)(2,1)}, f32[256,384]{1,0:T(8,128)}, f32[256,384]{1,0:T(8,128)S(1)}) custom-call(s32[3]{0:T(128)S(1)} %pad_add_fusion.refs_0_.idx, bf16[256,384]{1,0:T(8,128)(2,1)S(1)} %bitcast.7, f32[2,5376]{1,0:T(2,128)S(1)} %add_add_fusion.refs_2_, ...), custom_call_target="tpu_custom_call" | custom-call | flops 1 | bytes 1 | tf_op jit(solution)/shard_map/attention_forward/pallas_call | solution.py:71
  49.0 4.8 %mlp_forward.1 = (bf16[256,1536]{1,0:T(8,128)(2,1)}, f32[256,1536]{1,0:T(8,128)}, f32[256,384]{1,0:T(8,128)}, f32[256,384]{1,0:T(8,128)S(1)}) custom-call(s32[3]{0:T(128)S(1)} %pad_add_fusion.refs_0_.idx, f32[256,384]{1,0:T(8,128)S(1)} %get-tuple-element.112.refs_1_, f32[2,5376]{1,0:T(2,128)S(1)} %add_add_fusion.refs_2_, bf16[2,96,1536]{2,1,0:T(8,128)(2,1)S(1)} %copy-done.1, ...), custom_call_target="tpu_custom_call" | custom-call | flops 1 | bytes 1 | tf_op jit(solution)/shard_map/mlp_forward/pallas_call | solution.py:71
  53.9 3.0 %attention_forward.3 = (bf16[256,1152]{1,0:T(8,128)(2,1)S(1)}, f32[6,256,256]{2,1,0:T(8,128)S(1)}, bf16[256,384]{1,0:T(8,128)(2,1)S(1)}, f32[256,384]{1,0:T(8,128)S(1)}, f32[256,384]{1,0:T(8,128)S(1)}) custom-call(s32[3]{0:T(128)S(1)} %pad_add_fusion.refs_0_.idx, f32[256,384]{1,0:T(8,128)S(1)} %get-tuple-element.113.refs_1_, ...), custom_call_target="tpu_custom_call" | custom-call | flops 1 | bytes 1 | tf_op jit(solution)/shard_map/attention_forward/pallas_call | solution.py:71
  56.9 7.1 %mlp_both.1 = (bf16[256,384]{1,0:T(8,128)(2,1)}, f32[256,384]{1,0:T(8,128)S(1)}, f32[1,3072]{1,0:T(1,128)S(1)}, bf16[4,96,1536]{2,1,0:T(8,128)(2,1)S(1)}, bf16[4,96,1536]{2,1,0:T(8,128)(2,1)S(1)}) custom-call(s32[3]{0:T(128)S(1)} %pad_add_fusion.refs_0_.idx, f32[256,384]{1,0:T(8,128)S(1)} %get-tuple-element.116.refs_1_, f32[2,5376]{1,0:T(2,128)S(1)} %add_add_fusion.refs_2_, ...), custom_call_target="tpu_custom_call" | custom-call | flops 1 | bytes 1 | tf_op jit(solution)/shard_map/mlp_both/pallas_call | solution.py:71
  64.3 5.9 %attention_backward.2 = (f32[256,384]{1,0:T(8,128)S(1)}, f32[1,2304]{1,0:T(1,128)S(1)}, bf16[4,96,768]{2,1,0:T(8,128)(2,1)S(1)}, bf16[4,96,768]{2,1,0:T(8,128)(2,1)S(1)}) custom-call(s32[3]{0:T(128)S(1)} %pad_add_fusion.refs_0_.idx, f32[256,384]{1,0:T(8,128)S(1)} %get-tuple-element.113.refs_1_, f32[2,5376]{1,0:T(2,128)S(1)} %add_add_fusion.refs_2_, ...), custom_call_target="tpu_custom_call" | custom-call | flops 1 | bytes 1 | tf_op jit(solution)/shard_map/attention_backward/pallas_call | solution.py:71
  70.6 1.6 collective-permute-done.14.refs_2_
  73.9 4.6 %mlp_backward.1 = (f32[256,384]{1,0:T(8,128)S(1)}, f32[1,3072]{1,0:T(1,128)S(1)}, bf16[4,96,1536]{2,1,0:T(8,128)(2,1)S(1)}, bf16[4,96,1536]{2,1,0:T(8,128)(2,1)S(1)}) custom-call(s32[3]{0:T(128)S(1)} %pad_add_fusion.refs_0_.idx, f32[256,384]{1,0:T(8,128)S(1)} %get-tuple-element.112.refs_1_, f32[2,5376]{1,0:T(2,128)S(1)} %add_add_fusion.refs_2_, ...), custom_call_target="tpu_custom_call" | custom-call | flops 1 | bytes 1 | tf_op jit(solution)/shard_map/mlp_backward/pallas_call | solution.py:71
  79.0 2.0 %collective-permute-start.17 = (bf16[2,96,2304]{2,1,0:T(8,128)(2,1)S(1)}, bf16[2,96,2304]{2,1,0:T(8,128)(2,1)S(1)}, u32[]{:S(2)}, u32[]{:S(2)}) collective-permute-start(bf16[2,96,2304]{2,1,0:T(8,128)(2,1)S(1)} %get-tuple-element.150), channel_id=1, source_target_pairs={{0,8},{1,17},{2,10},{3,19},{4,12},{5,21},{6,14},{7,23},{8,0},{9,25... | collective-permute-start | bytes 2654216 | tf_op jit(solution)/shard_map/ppermute | solution.py:589
  82.6 6.8 %attention_backward.3 = (f32[256,384]{1,0:T(8,128)}, f32[1,2304]{1,0:T(1,128)S(1)}, bf16[4,96,768]{2,1,0:T(8,128)(2,1)S(1)}, bf16[4,96,768]{2,1,0:T(8,128)(2,1)S(1)}) custom-call(s32[3]{0:T(128)S(1)} %pad_add_fusion.refs_0_.idx, bf16[256,384]{1,0:T(8,128)(2,1)S(1)} %bitcast.8, f32[2,5376]{1,0:T(2,128)S(1)} %add_add_fusion.refs_2_, ...), custom_call_target="tpu_custom_call" | custom-call | flops 1 | bytes 1 | tf_op jit(solution)/shard_map/attention_backward/pallas_call | solution.py:71
  95.6 8.7 %collective-permute-done.19.other = bf16[2,96,1536]{2,1,0:T(8,128)(2,1)S(1)} collective-permute-done((bf16[2,96,1536]{2,1,0:T(8,128)(2,1)S(1)}, bf16[2,96,1536]{2,1,0:T(8,128)(2,1)S(1)}, u32[]{:S(2)}, u32[]{:S(2)}) %collective-permute-start.19) | collective-permute-done | bytes 589856 | tf_op jit(solution)/shard_map/ppermute | solution.py:589
  107.0 3.9 %collective-permute-done.20.second = bf16[1,11136]{1,0:T(2,128)(2,1)S(1)} collective-permute-done((bf16[1,11136]{1,0:T(2,128)(2,1)S(1)}, bf16[1,11136]{1,0:T(2,128)(2,1)S(1)}, u32[]{:S(2)}, u32[]{:S(2)}) %collective-permute-start.20) | collective-permute-done | bytes 22304 | tf_op jit(solution)/shard_map/ppermute | solution.py:589
  111.7 1.6 %collective-permute-start.26 = (bf16[48,2304]{1,0:T(8,128)(2,1)S(1)}, bf16[48,2304]{1,0:T(8,128)(2,1)S(1)}, u32[]{:S(2)}, u32[]{:S(2)}) collective-permute-start(bf16[48,2304]{1,0:T(8,128)(2,1)S(1)} %get-tuple-element.173), channel_id=1, source_target_pairs={{0,2},{1,3},{2,0},{3,1},{4,6},{5,7},{6,4},{7,5},{8,10},{9,11},{10,... | collective-permute-start | bytes 663560 | tf_op jit(solution)/shard_map/ppermute | solution.py:589
  114.7 2.8 %collective-permute-done.22.second = bf16[2,11136]{1,0:T(2,128)(2,1)S(1)} collective-permute-done((bf16[2,11136]{1,0:T(2,128)(2,1)S(1)}, bf16[2,11136]{1,0:T(2,128)(2,1)S(1)}, u32[]{:S(2)}, u32[]{:S(2)}) %collective-permute-start.22) | collective-permute-done | bytes 44576 | tf_op jit(solution)/shard_map/ppermute | solution.py:589
  117.4 2.0 %group.1 = (f32[2,384]{1,0:T(2,128)S(1)}, f32[2,384]{1,0:T(2,128)S(1)}, bf16[4,11136]{1,0:T(4,128)(2,1)S(1)}) custom-call(s32[3]{0:T(128)S(1)} %pad_add_fusion.refs_0_.idx, bf16[2,96,2304]{2,1,0:T(8,128)(2,1)S(1)} %copy-done.4, bf16[2,11136]{1,0:T(2,128)(2,1)S(1)} %stack.18.first, bf16[2,11136]{1,0:T(2,128)(2,1)S(1)} %collective-permute-done.22.second), custom_call_target="tpu_custom_call" | custom-call | flops 1 | bytes 1 | tf_op jit(solution)/shard_map/group/pallas_call | solution.py:71
  121.4 2.6 %collective-permute-start.30 = (bf16[48,2304]{1,0:T(8,128)(2,1)S(1)}, bf16[48,2304]{1,0:T(8,128)(2,1)S(1)}, u32[]{:S(2)}, u32[]{:S(2)}) collective-permute-start(bf16[48,2304]{1,0:T(8,128)(2,1)S(1)} %add.72.refs_0_), channel_id=1, source_target_pairs={{0,4},{1,5},{2,6},{3,7},{4,0},{5,1},{6,2},{7,3},{8,12},{9,13},{10,... | collective-permute-start | bytes 663560 | tf_op jit(solution)/shard_map/ppermute | solution.py:589
  124.7 5.0 %collective-permute-done.28.second = bf16[4,11136]{1,0:T(4,128)(2,1)S(1)} collective-permute-done((bf16[4,11136]{1,0:T(4,128)(2,1)S(1)}, bf16[4,11136]{1,0:T(4,128)(2,1)S(1)}, u32[]{:S(2)}, u32[]{:S(2)}) %collective-permute-start.28) | collective-permute-done | bytes 89120 | tf_op jit(solution)/shard_map/ppermute | solution.py:589
  129.9 1.6 collective-permute-start.34
  132.3 3.3 %collective-permute-done.23 = f32[2,384]{1,0:T(2,128)S(1)} collective-permute-done((f32[2,384]{1,0:T(2,128)S(1)}, f32[2,384]{1,0:T(2,128)S(1)}, u32[]{:S(2)}, u32[]{:S(2)}) %collective-permute-start.23) | collective-permute-done | bytes 3104 | tf_op jit(solution)/shard_map/ppermute | solution.py:589
  135.7 2.2 %collective-permute-start.24 = (f32[1,384]{1,0:T(1,128)S(1)}, f32[1,384]{1,0:T(1,128)S(1)}, u32[]{:S(2)}, u32[]{:S(2)}) collective-permute-start(f32[1,384]{1,0:T(1,128)S(1)} %slice.97), channel_id=1, source_target_pairs={{0,8},{1,17},{2,10},{3,19},{4,12},{5,21},{6,14},{7,23},{8,0},{9,25... | collective-permute-start | bytes 4616 | tf_op jit(solution)/shard_map/ppermute | solution.py:589
  140.4 2.6 %collective-permute-start.39 = (bf16[48,1536]{1,0:T(8,128)(2,1)S(1)}, bf16[48,1536]{1,0:T(8,128)(2,1)S(1)}, u32[]{:S(2)}, u32[]{:S(2)}) collective-permute-start(bf16[48,1536]{1,0:T(8,128)(2,1)S(1)} %add.75.refs_0_), channel_id=1, source_target_pairs={{0,4},{1,5},{2,6},{3,7},{4,0},{5,1},{6,2},{7,3},{8,12},{9,13},{10,... | collective-permute-start | bytes 442376 | tf_op jit(solution)/shard_map/ppermute | solution.py:589
  143.3 6.7 %collective-permute-done.31.refs_2_ = bf16[48,2304]{1,0:T(8,128)(2,1)S(1)} collective-permute-done((bf16[48,2304]{1,0:T(8,128)(2,1)S(1)}, bf16[48,2304]{1,0:T(8,128)(2,1)S(1)}, u32[]{:S(2)}, u32[]{:S(2)}) %collective-permute-start.31) | collective-permute-done | bytes 221216 | tf_op jit(solution)/shard_map/ppermute | solution.py:589
  150.0 2.3 %ada_grad.1 = (f32[2,96,2304]{2,1,0:T(8,128)}, f32[1,10752]{1,0:T(1,128)S(1)}) custom-call(s32[3]{0:T(128)S(1)} %pad_add_fusion.refs_0_.idx, bf16[8,11136]{1,0:T(8,128)(2,1)S(1)} %stack.19.refs_1_, bf16[8,11136]{1,0:T(8,128)(2,1)S(1)} %collective-permute-done.36.refs_2_, bf16[8,11136]{1,0:T(8,128)(2,1)S(1)} %collective-permute-done.37.refs_3_, ...), custom_call_target="tpu_custom_call" | custom-call | flops 1 | bytes 1 | tf_op jit(solution)/shard_map/ada_grad/pallas_call | solution.py:71
  152.4 2.2 %collective-permute-start.40 = (bf16[48,1536]{1,0:T(8,128)(2,1)S(1)}, bf16[48,1536]{1,0:T(8,128)(2,1)S(1)}, u32[]{:S(2)}, u32[]{:S(2)}) collective-permute-start(bf16[48,1536]{1,0:T(8,128)(2,1)S(1)} %add.77.refs_5_), channel_id=1, source_target_pairs={{0,2},{1,3},{2,0},{3,1},{4,6},{5,7},{6,4},{7,5},{8,10},{9,11},{10,... | collective-permute-start | bytes 442376 | tf_op jit(solution)/shard_map/ppermute | solution.py:589
  154.6 2.4 %collective-permute-done.43.refs_1_ = bf16[96,768]{1,0:T(8,128)(2,1)S(1)} collective-permute-done((bf16[96,768]{1,0:T(8,128)(2,1)S(1)}, bf16[96,768]{1,0:T(8,128)(2,1)S(1)}, u32[]{:S(2)}, u32[]{:S(2)}) %collective-permute-start.43) | collective-permute-done | bytes 147488 | tf_op jit(solution)/shard_map/ppermute | solution.py:589
  158.4 1.6 collective-permute-done.40.refs_6_
  161.4 2.6 %finish.1 = (f32[2,96,1152]{2,1,0:T(8,128)}, f32[2,96,384]{2,1,0:T(8,128)}, f32[2,96,1536]{2,1,0:T(8,128)}, f32[2,384,384]{2,1,0:T(8,128)}) custom-call(s32[3]{0:T(128)S(1)} %pad_add_fusion.refs_0_.idx, bf16[48,2304]{1,0:T(8,128)(2,1)S(1)} %add.74.refs_1_, bf16[48,2304]{1,0:T(8,128)(2,1)S(1)} %collective-permute-done.31.refs_2_, ...), custom_call_target="tpu_custom_call" | custom-call | flops 1 | bytes 1 | tf_op jit(solution)/shard_map/finish/pallas_call | solution.py:71
  (156 shorter events, 40.3 us)
Async XLA Ops:
  2.9 29.9 %collective-permute-start.4 = (bf16[96,4608]{1,0:T(8,128)(2,1)}, bf16[96,4608]{1,0:T(8,128)(2,1)S(1)}, u32[]{:S(2)}, u32[]{:S(2)}) collective-permute-start(bf16[96,4608]{1,0:T(8,128)(2,1)} %pack.3), channel_id=1, source_target_pairs={{0,8},{1,17},{2,10},{3,19},{4,12},{5,21},{6,14},{7,23},{8,0},{9,25... | collective-permute-start | bytes 2654216 | tf_op jit(solution)/shard_map/ppermute | solution.py:589
  7.1 27.0 %collective-permute-start.3 = (bf16[96,4608]{1,0:T(8,128)(2,1)S(1)}, bf16[96,4608]{1,0:T(8,128)(2,1)S(1)}, u32[]{:S(2)}, u32[]{:S(2)}) collective-permute-start(bf16[96,4608]{1,0:T(8,128)(2,1)S(1)} %pack.2), channel_id=1, source_target_pairs={{0,8},{1,17},{2,10},{3,19},{4,12},{5,21},{6,14},{7,23},{8,0},{9,25... | collective-permute-start | bytes 2654216 | tf_op jit(solution)/shard_map/ppermute | solution.py:589
  7.3 19.5 %collective-permute-start = (bf16[1,384]{1,0:T(2,128)(2,1)S(1)}, bf16[1,384]{1,0:T(2,128)(2,1)}, u32[]{:S(2)}, u32[]{:S(2)}) collective-permute-start(bf16[1,384]{1,0:T(2,128)(2,1)S(1)} %copy-done.14), channel_id=1, source_target_pairs={{0,8},{1,9},{2,10},{3,11},{4,12},{5,13},{6,14},{7,15},{8,0},{9,1},... | collective-permute-start | bytes 2312 | tf_op jit(solution)/shard_map/ppermute | solution.py:589
  9.2 17.5 %collective-permute-start.1 = (bf16[1,384]{1,0:T(2,128)(2,1)S(1)}, bf16[1,384]{1,0:T(2,128)(2,1)}, u32[]{:S(2)}, u32[]{:S(2)}) collective-permute-start(bf16[1,384]{1,0:T(2,128)(2,1)S(1)} %copy-done.14), channel_id=1, source_target_pairs={{0,16},{1,17},{2,18},{3,19},{4,20},{5,21},{6,22},{7,23},{8,24},{9,... | collective-permute-start | bytes 2312 | tf_op jit(solution)/shard_map/ppermute | solution.py:589
  10.8 17.5 %collective-permute-start.2 = (bf16[1,384]{1,0:T(2,128)(2,1)S(1)}, bf16[1,384]{1,0:T(2,128)(2,1)}, u32[]{:S(2)}, u32[]{:S(2)}) collective-permute-start(bf16[1,384]{1,0:T(2,128)(2,1)S(1)} %copy-done.14), channel_id=1, source_target_pairs={{0,24},{1,25},{2,26},{3,27},{4,28},{5,29},{6,30},{7,31},{8,16},{9,... | collective-permute-start | bytes 2312 | tf_op jit(solution)/shard_map/ppermute | solution.py:589
  33.5 8.9 %collective-permute-start.8 = (bf16[96,2304]{1,0:T(8,128)(2,1)S(1)}, bf16[96,2304]{1,0:T(8,128)(2,1)S(1)}, u32[]{:S(2)}, u32[]{:S(2)}) collective-permute-start(bf16[96,2304]{1,0:T(8,128)(2,1)S(1)} %half.2), channel_id=1, source_target_pairs={{0,16},{1,9},{2,18},{3,11},{4,20},{5,13},{6,22},{7,15},{8,24},{9,1... | collective-permute-start | bytes 1327112 | tf_op jit(solution)/shard_map/ppermute | solution.py:589
  36.3 7.0 %collective-permute-start.6 = (f32[2,5376]{1,0:T(2,128)S(1)}, f32[2,5376]{1,0:T(2,128)S(1)}, u32[]{:S(2)}, u32[]{:S(2)}) collective-permute-start(f32[2,5376]{1,0:T(2,128)S(1)} %get-tuple-element.109), channel_id=1, source_target_pairs={{0,16},{1,17},{2,18},{3,19},{4,20},{5,21},{6,22},{7,23},{8,24},{9,... | collective-permute-start | bytes 129032 | tf_op jit(solution)/shard_map/ppermute | solution.py:589
  37.7 5.5 %collective-permute-start.7 = (f32[2,5376]{1,0:T(2,128)S(1)}, f32[2,5376]{1,0:T(2,128)S(1)}, u32[]{:S(2)}, u32[]{:S(2)}) collective-permute-start(f32[2,5376]{1,0:T(2,128)S(1)} %get-tuple-element.111), channel_id=1, source_target_pairs={{0,24},{1,25},{2,26},{3,27},{4,28},{5,29},{6,30},{7,31},{8,16},{9,... | collective-permute-start | bytes 129032 | tf_op jit(solution)/shard_map/ppermute | solution.py:589
  38.2 10.4 %collective-permute-start.11 = (bf16[96,2304]{1,0:T(8,128)(2,1)S(1)}, bf16[96,2304]{1,0:T(8,128)(2,1)S(1)}, u32[]{:S(2)}, u32[]{:S(2)}) collective-permute-start(bf16[96,2304]{1,0:T(8,128)(2,1)S(1)} %half.3), channel_id=1, source_target_pairs={{0,16},{1,9},{2,18},{3,11},{4,20},{5,13},{6,22},{7,15},{8,24},{9,1... | collective-permute-start | bytes 1327112 | tf_op jit(solution)/shard_map/ppermute | solution.py:589
  48.4 5.4 %collective-permute-start.12 = (bf16[96,4608]{1,0:T(8,128)(2,1)S(1)}, bf16[96,4608]{1,0:T(8,128)(2,1)S(1)}, u32[]{:S(2)}, u32[]{:S(2)}) collective-permute-start(bf16[96,4608]{1,0:T(8,128)(2,1)S(1)} %collective-permute-done.3.whole.refs_5_.refs_6_.refs_10_), channel_id=1, source_target_pairs={{0,1},{1,0},{2,3},{3,2},{4,5},{5,4},{6,7},{7,6},{8,9},{9,8},{10,11... | collective-permute-start | bytes 2654216 | tf_op jit(solution)/shard_map/ppermute | solution.py:589
  64.1 8.1 %collective-permute-start.15 = (bf16[4,96,1536]{2,1,0:T(8,128)(2,1)S(1)}, bf16[4,96,1536]{2,1,0:T(8,128)(2,1)S(1)}, u32[]{:S(2)}, u32[]{:S(2)}) collective-permute-start(bf16[4,96,1536]{2,1,0:T(8,128)(2,1)S(1)} %get-tuple-element.128), channel_id=1, source_target_pairs={{0,1},{1,0},{2,3},{3,2},{4,5},{5,4},{6,7},{7,6},{8,9},{9,8},{10,11... | collective-permute-start | bytes 3538952 | tf_op jit(solution)/shard_map/ppermute | solution.py:589
  79.0 13.1 %collective-permute-start.17 = (bf16[2,96,2304]{2,1,0:T(8,128)(2,1)S(1)}, bf16[2,96,2304]{2,1,0:T(8,128)(2,1)S(1)}, u32[]{:S(2)}, u32[]{:S(2)}) collective-permute-start(bf16[2,96,2304]{2,1,0:T(8,128)(2,1)S(1)} %get-tuple-element.150), channel_id=1, source_target_pairs={{0,8},{1,17},{2,10},{3,19},{4,12},{5,21},{6,14},{7,23},{8,0},{9,25... | collective-permute-start | bytes 2654216 | tf_op jit(solution)/shard_map/ppermute | solution.py:589
  89.6 14.7 %collective-permute-start.19 = (bf16[2,96,1536]{2,1,0:T(8,128)(2,1)S(1)}, bf16[2,96,1536]{2,1,0:T(8,128)(2,1)S(1)}, u32[]{:S(2)}, u32[]{:S(2)}) collective-permute-start(bf16[2,96,1536]{2,1,0:T(8,128)(2,1)S(1)} %get-tuple-element.158), channel_id=1, source_target_pairs={{0,8},{1,17},{2,10},{3,19},{4,12},{5,21},{6,14},{7,23},{8,0},{9,25... | collective-permute-start | bytes 1769480 | tf_op jit(solution)/shard_map/ppermute | solution.py:589
  92.4 18.6 %collective-permute-start.21 = (bf16[96,2304]{1,0:T(8,128)(2,1)S(1)}, bf16[96,2304]{1,0:T(8,128)(2,1)S(1)}, u32[]{:S(2)}, u32[]{:S(2)}) collective-permute-start(bf16[96,2304]{1,0:T(8,128)(2,1)S(1)} %get-tuple-element.163), channel_id=1, source_target_pairs={{0,16},{1,9},{2,18},{3,11},{4,20},{5,13},{6,22},{7,15},{8,24},{9,1... | collective-permute-start | bytes 1327112 | tf_op jit(solution)/shard_map/ppermute | solution.py:589
  94.0 25.4 %collective-permute-start.25 = (bf16[2,96,768]{2,1,0:T(8,128)(2,1)S(1)}, bf16[2,96,768]{2,1,0:T(8,128)(2,1)S(1)}, u32[]{:S(2)}, u32[]{:S(2)}) collective-permute-start(bf16[2,96,768]{2,1,0:T(8,128)(2,1)S(1)} %get-tuple-element.170), channel_id=1, source_target_pairs={{0,8},{1,17},{2,10},{3,19},{4,12},{5,21},{6,14},{7,23},{8,0},{9,25... | collective-permute-start | bytes 884744 | tf_op jit(solution)/shard_map/ppermute | solution.py:589
  104.5 19.5 %collective-permute-start.27 = (bf16[96,1536]{1,0:T(8,128)(2,1)S(1)}, bf16[96,1536]{1,0:T(8,128)(2,1)S(1)}, u32[]{:S(2)}, u32[]{:S(2)}) collective-permute-start(bf16[96,1536]{1,0:T(8,128)(2,1)S(1)} %get-tuple-element.175), channel_id=1, source_target_pairs={{0,16},{1,9},{2,18},{3,11},{4,20},{5,13},{6,22},{7,15},{8,24},{9,1... | collective-permute-start | bytes 884744 | tf_op jit(solution)/shard_map/ppermute | solution.py:589
  105.6 5.3 %collective-permute-start.20 = (bf16[1,11136]{1,0:T(2,128)(2,1)S(1)}, bf16[1,11136]{1,0:T(2,128)(2,1)S(1)}, u32[]{:S(2)}, u32[]{:S(2)}) collective-permute-start(bf16[1,11136]{1,0:T(2,128)(2,1)S(1)} %constant_dynamic-update-slice_fusion.first), channel_id=1, source_target_pairs={{0,8},{1,17},{2,10},{3,19},{4,12},{5,21},{6,14},{7,23},{8,0},{9,25... | collective-permute-start | bytes 66824 | tf_op jit(solution)/shard_map/ppermute | solution.py:589
  111.7 9.6 %collective-permute-start.26 = (bf16[48,2304]{1,0:T(8,128)(2,1)S(1)}, bf16[48,2304]{1,0:T(8,128)(2,1)S(1)}, u32[]{:S(2)}, u32[]{:S(2)}) collective-permute-start(bf16[48,2304]{1,0:T(8,128)(2,1)S(1)} %get-tuple-element.173), channel_id=1, source_target_pairs={{0,2},{1,3},{2,0},{3,1},{4,6},{5,7},{6,4},{7,5},{8,10},{9,11},{10,... | collective-permute-start | bytes 663560 | tf_op jit(solution)/shard_map/ppermute | solution.py:589
  119.5 11.9 %collective-permute-start.29 = (bf16[96,768]{1,0:T(8,128)(2,1)S(1)}, bf16[96,768]{1,0:T(8,128)(2,1)S(1)}, u32[]{:S(2)}, u32[]{:S(2)}) collective-permute-start(bf16[96,768]{1,0:T(8,128)(2,1)S(1)} %get-tuple-element.179), channel_id=1, source_target_pairs={{0,16},{1,9},{2,18},{3,11},{4,20},{5,13},{6,22},{7,15},{8,24},{9,1... | collective-permute-start | bytes 442376 | tf_op jit(solution)/shard_map/ppermute | solution.py:589
  120.8 8.9 %collective-permute-start.28 = (bf16[4,11136]{1,0:T(4,128)(2,1)S(1)}, bf16[4,11136]{1,0:T(4,128)(2,1)S(1)}, u32[]{:S(2)}, u32[]{:S(2)}) collective-permute-start(bf16[4,11136]{1,0:T(4,128)(2,1)S(1)} %get-tuple-element.177.first), channel_id=1, source_target_pairs={{0,2},{1,3},{2,0},{3,1},{4,6},{5,7},{6,4},{7,5},{8,10},{9,11},{10,... | collective-permute-start | bytes 267272 | tf_op jit(solution)/shard_map/ppermute | solution.py:589
  121.4 16.6 %collective-permute-start.30 = (bf16[48,2304]{1,0:T(8,128)(2,1)S(1)}, bf16[48,2304]{1,0:T(8,128)(2,1)S(1)}, u32[]{:S(2)}, u32[]{:S(2)}) collective-permute-start(bf16[48,2304]{1,0:T(8,128)(2,1)S(1)} %add.72.refs_0_), channel_id=1, source_target_pairs={{0,4},{1,5},{2,6},{3,7},{4,0},{5,1},{6,2},{7,3},{8,12},{9,13},{10,... | collective-permute-start | bytes 663560 | tf_op jit(solution)/shard_map/ppermute | solution.py:589
  129.8 8.1 %collective-permute-start.36 = (bf16[8,11136]{1,0:T(8,128)(2,1)S(1)}, bf16[8,11136]{1,0:T(8,128)(2,1)S(1)}, u32[]{:S(2)}, u32[]{:S(2)}) collective-permute-start(bf16[8,11136]{1,0:T(8,128)(2,1)S(1)} %stack.19.refs_1_), channel_id=1, source_target_pairs={{0,4},{1,5},{2,6},{3,7},{4,0},{5,1},{6,2},{7,3},{8,12},{9,13},{10,... | collective-permute-start | bytes 534536 | tf_op jit(solution)/shard_map/ppermute | solution.py:589
  129.9 9.5 %collective-permute-start.34 = (bf16[48,1536]{1,0:T(8,128)(2,1)S(1)}, bf16[48,1536]{1,0:T(8,128)(2,1)S(1)}, u32[]{:S(2)}, u32[]{:S(2)}) collective-permute-start(bf16[48,1536]{1,0:T(8,128)(2,1)S(1)} %get-tuple-element.182), channel_id=1, source_target_pairs={{0,2},{1,3},{2,0},{3,1},{4,6},{5,7},{6,4},{7,5},{8,10},{9,11},{10,... | collective-permute-start | bytes 442376 | tf_op jit(solution)/shard_map/ppermute | solution.py:589
  131.5 7.9 %collective-permute-start.35 = (bf16[96,768]{1,0:T(8,128)(2,1)S(1)}, bf16[96,768]{1,0:T(8,128)(2,1)S(1)}, u32[]{:S(2)}, u32[]{:S(2)}) collective-permute-start(bf16[96,768]{1,0:T(8,128)(2,1)S(1)} %add.73.refs_0_), channel_id=1, source_target_pairs={{0,2},{1,3},{2,0},{3,1},{4,6},{5,7},{6,4},{7,5},{8,10},{9,11},{10,... | collective-permute-start | bytes 442376 | tf_op jit(solution)/shard_map/ppermute | solution.py:589
  138.0 12.0 %collective-permute-start.31 = (bf16[48,2304]{1,0:T(8,128)(2,1)S(1)}, bf16[48,2304]{1,0:T(8,128)(2,1)S(1)}, u32[]{:S(2)}, u32[]{:S(2)}) collective-permute-start(bf16[48,2304]{1,0:T(8,128)(2,1)S(1)} %add.74.refs_1_), channel_id=1, source_target_pairs={{0,2},{1,3},{2,0},{3,1},{4,6},{5,7},{6,4},{7,5},{8,10},{9,11},{10,... | collective-permute-start | bytes 663560 | tf_op jit(solution)/shard_map/ppermute | solution.py:589
  139.5 10.5 %collective-permute-start.37 = (bf16[8,11136]{1,0:T(8,128)(2,1)S(1)}, bf16[8,11136]{1,0:T(8,128)(2,1)S(1)}, u32[]{:S(2)}, u32[]{:S(2)}) collective-permute-start(bf16[8,11136]{1,0:T(8,128)(2,1)S(1)} %stack.19.refs_1_), channel_id=1, source_target_pairs={{0,1},{1,0},{2,3},{3,2},{4,5},{5,4},{6,7},{7,6},{8,9},{9,8},{10,11... | collective-permute-start | bytes 534536 | tf_op jit(solution)/shard_map/ppermute | solution.py:589
  140.4 12.0 %collective-permute-start.39 = (bf16[48,1536]{1,0:T(8,128)(2,1)S(1)}, bf16[48,1536]{1,0:T(8,128)(2,1)S(1)}, u32[]{:S(2)}, u32[]{:S(2)}) collective-permute-start(bf16[48,1536]{1,0:T(8,128)(2,1)S(1)} %add.75.refs_0_), channel_id=1, source_target_pairs={{0,4},{1,5},{2,6},{3,7},{4,0},{5,1},{6,2},{7,3},{8,12},{9,13},{10,... | collective-permute-start | bytes 442376 | tf_op jit(solution)/shard_map/ppermute | solution.py:589
  142.9 18.5 %collective-permute-start.32 = (bf16[48,2304]{1,0:T(8,128)(2,1)S(1)}, bf16[48,2304]{1,0:T(8,128)(2,1)S(1)}, u32[]{:S(2)}, u32[]{:S(2)}) collective-permute-start(bf16[48,2304]{1,0:T(8,128)(2,1)S(1)} %add.74.refs_1_), channel_id=1, source_target_pairs={{0,1},{1,0},{2,3},{3,2},{4,5},{5,4},{6,7},{7,6},{8,9},{9,8},{10,11... | collective-permute-start | bytes 663560 | tf_op jit(solution)/shard_map/ppermute | solution.py:589
  142.9 14.0 %collective-permute-start.43 = (bf16[96,768]{1,0:T(8,128)(2,1)S(1)}, bf16[96,768]{1,0:T(8,128)(2,1)S(1)}, u32[]{:S(2)}, u32[]{:S(2)}) collective-permute-start(bf16[96,768]{1,0:T(8,128)(2,1)S(1)} %add.76.refs_0_), channel_id=1, source_target_pairs={{0,4},{1,5},{2,6},{3,7},{4,0},{5,1},{6,2},{7,3},{8,12},{9,13},{10,... | collective-permute-start | bytes 442376 | tf_op jit(solution)/shard_map/ppermute | solution.py:589
  150.0 11.4 %collective-permute-start.33 = (bf16[48,2304]{1,0:T(8,128)(2,1)S(1)}, bf16[48,2304]{1,0:T(8,128)(2,1)S(1)}, u32[]{:S(2)}, u32[]{:S(2)}) collective-permute-start(bf16[48,2304]{1,0:T(8,128)(2,1)S(1)} %collective-permute-done.31.refs_2_), channel_id=1, source_target_pairs={{0,1},{1,0},{2,3},{3,2},{4,5},{5,4},{6,7},{7,6},{8,9},{9,8},{10,11... | collective-permute-start | bytes 663560 | tf_op jit(solution)/shard_map/ppermute | solution.py:589
  152.4 7.6 %collective-permute-start.40 = (bf16[48,1536]{1,0:T(8,128)(2,1)S(1)}, bf16[48,1536]{1,0:T(8,128)(2,1)S(1)}, u32[]{:S(2)}, u32[]{:S(2)}) collective-permute-start(bf16[48,1536]{1,0:T(8,128)(2,1)S(1)} %add.77.refs_5_), channel_id=1, source_target_pairs={{0,2},{1,3},{2,0},{3,1},{4,6},{5,7},{6,4},{7,5},{8,10},{9,11},{10,... | collective-permute-start | bytes 442376 | tf_op jit(solution)/shard_map/ppermute | solution.py:589
  154.6 6.8 %collective-permute-start.41 = (bf16[48,1536]{1,0:T(8,128)(2,1)S(1)}, bf16[48,1536]{1,0:T(8,128)(2,1)S(1)}, u32[]{:S(2)}, u32[]{:S(2)}) collective-permute-start(bf16[48,1536]{1,0:T(8,128)(2,1)S(1)} %add.77.refs_5_), channel_id=1, source_target_pairs={{0,1},{1,0},{2,3},{3,2},{4,5},{5,4},{6,7},{7,6},{8,9},{9,8},{10,11... | collective-permute-start | bytes 442376 | tf_op jit(solution)/shard_map/ppermute | solution.py:589
  (33 other events, 194.7 us)

commit v4 on v3

--- a/solution.py
+++ b/solution.py
@@ -455,40 +455,59 @@
             outs[step][layer : layer + 1, :wide] = result[step : step + 1]
 
 
-def stack_kernel(first, second, out, rows_f32):
+def stack_kernel(extra, first, second, out, rows_f32):
+    size = first.shape[0] - extra
+    rows_f32[:size] = first[:size].astype(F32)
+    rows_f32[size : 2 * size] = second[:size].astype(F32)
+    if extra:
+        rows_f32[2 * size :] = first[size:].astype(F32) + second[size:].astype(F32)
+    out[...] = rows_f32[...].astype(BF)
+
+
+def group_kernel(idx, w_ada, first, second, keep, send, stacked, rows_f32, out_f32, w_pad, sems):
+    copies = padded_rows(idx, w_ada, w_pad, sems)
+    start_all(copies)
+    width = w_pad.shape[0]
     size = first.shape[0]
     rows_f32[:size] = first[...].astype(F32)
     rows_f32[size:] = second[...].astype(F32)
-    out[...] = rows_f32[...].astype(BF)
-
-
-def group_kernel(idx, w_ada, first, second, keep, send, stacked, rows_f32, w_pad, sems):
-    copies = padded_rows(idx, w_ada, w_pad, sems)
-    start_all(copies)
-    width, wide = w_pad.shape
-    stack_kernel(first, second, stacked, rows_f32)
+    cols = stacked.shape[1]
+    biases = col_sum(rows_f32[:, cols:])
+    out_f32[...] = jnp.zeros(out_f32.shape, F32)
+    out_f32[: 2 * size] = rows_f32[:, :cols]
+    for row, at in enumerate(range(0, biases.shape[1], cols)):
+        part = biases[:, at : at + cols]
+        out_f32[2 * size + row : 2 * size + row + 1, : part.shape[1]] = part
+    stacked[...] = out_f32[...].astype(BF)
     wait_all(copies)
-    result = dot_nt(stacked[:, width : width + wide], w_pad[...])
+    result = dot_nt(rows_f32[:, width:cols].astype(BF), w_pad[...])
     half = keep.shape[0]
     keep[...] = result[:half]
     send[...] = result[half:]
 
 
-def ada_grad_kernel(rows, wide, inverse_count, *refs):
+def ada_grad_kernel(rows, wide, extra, inverse_count, *refs):
     idx, stacks = refs[0], refs[1:-4]
     grad_ada, sums, turned, gathered_f32 = refs[-4:]
     layers = grad_ada.shape[0]
     width = turned.shape[0]
-    size = stacks[0].shape[0]
+    size = stacks[0].shape[0] - extra
+    cols = stacks[0].shape[1]
+    biases = 0.0
     for number, stack in enumerate(stacks):
-        gathered_f32[number * size : (number + 1) * size] = stack[...].astype(F32)
+        gathered_f32[number * size : (number + 1) * size] = stack[:size].astype(F32)
+        biases = biases + stack[size:].astype(F32)
     gathered = gathered_f32[...].astype(BF)
     turned[...] = gathered_f32[:, :width].T
     own = turned[block_at(idx[0] * rows, rows), :].astype(BF)
     for layer in range(layers):
         at = width + layer * wide
         grad_ada[layer] = dot(own, gathered[:, at : at + wide]) * inverse_count
-    sums[...] = col_sum(gathered_f32[:, width:]) * inverse_count
+    sums[:, : cols - width] = col_sum(gathered_f32[:, width:]) * inverse_count
+    for row in range(extra):
+        at = cols - width + row * cols
+        part = min(cols, sums.shape[1] - at)
+        sums[:, at : at + part] = biases[row : row + 1, :part] * inverse_count
 
 
 def core_sum_kernel(slots, count, *refs):
@@ -634,22 +653,24 @@
 
     conditions = [condition] + [exchange(condition, by_shard=step) for step in range(1, n_shard)]
     packed = [pack((layer, ("qkv", "mlp")))[0] for layer in range(layers)]
-    near = [near_first(own) for own in packed]
+    near = [near_first(packed[0])]
+    near += [near_first(after(own, *conditions[1:])) for own in packed[1:]]
     pad_scratch = [pltpu.VMEM((width, layers * wide), BF), pltpu.SemaphoreType.DMA((layers,))]
     span = wide + 4 * width + hidden
     partial = run(
         functools.partial(modulate_kernel, n_shard), "modulate",
-        [(idx, "s"), (w_ada, "a"), (b_ada, "v"), (b_qv, "v"), (b_proj, "v"), (b_fc1, "v"),
-         (b_fc2, "v")] + [(array, "v") for array in conditions],
+        [(idx, "s"), (w_ada, "a"), (b_ada, "k"), (b_qv, "k"), (b_proj, "k"), (b_fc1, "k"),
+         (b_fc2, "k"), (conditions[0], "k")] + [(array, "v") for array in conditions[1:]],
         [((layers, span), F32, "v")] * n_shard, pad_scratch, flops=10**7,
     )
     parts = [near_half(near[0], partial[0])]
-    for own in near[1:]:
-        parts.append(near_half(own, parts[-1]))
-    near = [near_second(own, part) for own, part in zip(near, parts)]
     mod_all = partial[0]
     for step in range(1, n_shard):
-        mod_all = mod_all + exchange(after(partial[step], *parts[1:]), by_shard=step)
+        mod_all = mod_all + exchange(after(partial[step], parts[0]), by_shard=step)
+    for own in near[1:]:
+        parts.append(near_half(own, mod_all))
+    near = [near_second(own, part) for own, part in zip(near, parts)]
+    mod_all = after(mod_all, *parts[1:])
     pieces = {0: (near[0], far_of(near[0]))}
 
     big = seq * width
@@ -810,63 +831,66 @@
     while not relay and 2 ** len(masks) < n_shard:
         masks.append((2 ** len(masks),) * 2)
 
-    def stack(first, second):
-        shape = (2 * first.shape[0], length)
+    cols = width + layers * wide
+    extra = -(-(length - cols) // cols)
+
+    def stack(first, second, extra=0):
+        shape = (2 * first.shape[0] - extra, first.shape[1])
         return run(
-            stack_kernel, "stack", [(first, "v"), (second, "v")], [(shape, BF, "v")],
-            [pltpu.VMEM(shape, F32)],
+            functools.partial(stack_kernel, extra), "stack", [(first, "v"), (second, "v")],
+            [(shape, BF, "v")], [pltpu.VMEM(shape, F32)],
         )[0]
 
     (keys_first, core_first, sent_first), = waiting
     plan = [keys_first, [("mlp", 0)], [("qkv", 0)]]
     a = shard_second(core_first, sent_first, grad_stream)
-    vector = after(vector, a[0])
+    core_qkv = core_sum(plan[2], a[0])
+    sent_qkv = shard_send(core_qkv)
+    b = shard_second(core_mlp, sent_mlp, core_qkv[0])
+    a = level_first(a, True, b[0])
+    c = shard_second(core_qkv, sent_qkv, a[1])
+    vector = after(vector, b[0])
     for mask in masks[:-2]:
         vector = stack(vector, exchange(vector, turn=mask))
     arriving = exchange(vector, turn=masks[-2])
-    core_qkv = core_sum(plan[2], vector)
-    sent_qkv = shard_send(core_qkv)
-    b = shard_second(core_mlp, sent_mlp, core_qkv[0])
-    vector = after(vector, b[0])
-    vector = stack(after(vector, core_qkv[0]), arriving)
+    vector = stack(after(vector, c[0]), arriving)
     arriving = exchange(vector, turn=masks[-1])
-    a = level_first(a, True, vector)
+    b = level_first(b, True, vector)
+    a = level_second(a, b[1])
+    a_moving = exchange(a[1], by_level=2)
+    c = level_first(c, False, a[1])
     grad_cond, passed, stacked = run(
         group_kernel, "group",
-        [(idx, "s"), (w_ada, "a"), (after(vector, a[1]), "v"), (arriving, "v")],
-        [((n_shard // 2, width), F32, "v")] * 2 + [((n_shard, length), BF, "v")],
-        [pltpu.VMEM((n_shard, length), F32)] + pad_scratch, flops=10**7,
+        [(idx, "s"), (w_ada, "a"), (after(vector, c[1]), "v"), (arriving, "v")],
+        [((n_shard // 2, width), F32, "v")] * 2 + [((n_shard + extra, cols), BF, "v")],
+        [pltpu.VMEM((n_shard, length), F32), pltpu.VMEM((n_shard + extra, cols), F32)]
+        + pad_scratch, flops=10**7,
     )
     arriving = exchange(stacked, by_level=1)
-    c = shard_second(core_qkv, sent_qkv, stacked)
-    a = level_second(a, c[0])
-    a_moving = exchange(a[1], by_level=2)
-    b = level_first(b, True, a[1])
-    stacked = stack(after(stacked, b[1]), arriving)
-    step = 2
-    while 2 * step < levels:
-        stacked = stack(stacked, exchange(stacked, by_level=step))
-        step *= 2
-    arriving = exchange(stacked, by_level=step)
-    c = level_first(c, False, stacked)
-    a = (a[0], add([after(a[1], c[1]), a_moving], a[1].shape))
-    a_parts = level_last(*a, 4)
-    b = level_second(b, a[1])
+    b = level_second(b, stacked)
     b_moving = exchange(b[1], by_level=2)
     c = level_second(c, b[1])
     c_moving = exchange(c[1], by_level=2)
+    stacked = stack(after(stacked, c[1]), arriving, extra)
+    step = 2
+    while 2 * step < levels:
+        stacked = stack(stacked, exchange(stacked, by_level=step), extra)
+        step *= 2
+    arriving = exchange(stacked, by_level=step)
+    a = (a[0], add([after(a[1], stacked), a_moving], a[1].shape))
+    a_parts = level_last(*a, 4)
     grad_cond = grad_cond + exchange(passed, turn=masks[-1])
     for mask in masks[-2::-1]:
         half = grad_cond.shape[0] // 2
         grad_cond = grad_cond[:half] + exchange(grad_cond[half:], turn=mask)
     cond_grad = jax.vjp(jax.nn.silu, cond_in)[1](grad_cond)[0]
-    stacks = [after(stacked, c[1]), arriving]
+    stacks = [after(stacked, a[1]), arriving]
     stacks = stacks + far_of(stacks)
     grad_ada, sums = run(
-        functools.partial(ada_grad_kernel, rows, wide, factor), "ada_grad",
+        functools.partial(ada_grad_kernel, rows, wide, extra, factor), "ada_grad",
         [(idx, "s")] + [(array, "v") for array in stacks],
         [((layers, rows, wide), F32, "v"), ((1, length - width), F32, "v")],
-        [pltpu.VMEM((width, total_latents), F32), pltpu.VMEM((total_latents, length), F32)],
+        [pltpu.VMEM((width, total_latents), F32), pltpu.VMEM((total_latents, cols), F32)],
         flops=10**8,
     )
 

time: 164 us -> 161 us (0.982)
  local copies, waits for them, and re-layouts: 4.29 us -> 1.58 us
    unnamed x47 -> x39, local copies, waits for them, and re-layouts: 4.26 us -> 1.55 us
  transfers between devices with their start and end apart: 45 -> 45, of which waited for: 16 -> 21; matrix products, arithmetic and copies ran while one was open for 2% -> 2% of each run, Pallas kernels for 21% -> 21%
where the time goes in v4:
time: 161 us
  waiting for transfers between devices  60.3 us (37%)
  Pallas kernels  53.1 us (33%)
  starting transfers between devices  41.7 us (26%)
  other arithmetic  3.39 us (2%)
    ppermute x45, waiting for transfers between devices, exchange(): return lax.ppermute(array, ('shard', 'rep'), moves)  60.3 us
    pallas_call x32, Pallas kernels, run(): pl.pallas_call(body, out_shape=[pltpu.HBM(shape, dtype) if kind in 'hk' e...  53.1 us
    ppermute x45, starting transfers between devices, exchange(): return lax.ppermute(array, ('shard', 'rep'), moves)  41.7 us
  transfers between devices with their start and end apart: 45, of which 21 were waited for; matrix products, arithmetic and copies ran while one was open for 2% of the time, Pallas kernels for 21%

profile of v4, /device:TPU:0, one launch (start us, length us, event | category | flops | bytes accessed | tf_op | source)
XLA Modules:
  0.0 161.1 jit_solution(10412505264620505782)
XLA Ops:
  2.0 3.0 %collective-permute-start.3 = (bf16[96,4608]{1,0:T(8,128)(2,1)S(1)}, bf16[96,4608]{1,0:T(8,128)(2,1)S(1)}, u32[]{:S(2)}, u32[]{:S(2)}) collective-permute-start(bf16[96,4608]{1,0:T(8,128)(2,1)S(1)} %pack.2), channel_id=1, source_target_pairs={{0,8},{1,17},{2,10},{3,19},{4,12},{5,21},{6,14},{7,23},{8,0},{9,25... | collective-permute-start | bytes 2654216 | tf_op jit(solution)/shard_map/ppermute | solution.py:608
  5.1 2.0 %collective-permute-start.1 = (bf16[1,384]{1,0:T(2,128)(2,1)S(1)}, bf16[1,384]{1,0:T(2,128)(2,1)S(1)}, u32[]{:S(2)}, u32[]{:S(2)}) collective-permute-start(bf16[1,384]{1,0:T(2,128)(2,1)S(1)} %copy-done.14), channel_id=1, source_target_pairs={{0,16},{1,17},{2,18},{3,19},{4,20},{5,21},{6,22},{7,23},{8,24},{9,... | collective-permute-start | bytes 2312 | tf_op jit(solution)/shard_map/ppermute | solution.py:608
  8.6 7.5 %collective-permute-done.refs_8_ = bf16[1,384]{1,0:T(2,128)(2,1)S(1)} collective-permute-done((bf16[1,384]{1,0:T(2,128)(2,1)S(1)}, bf16[1,384]{1,0:T(2,128)(2,1)S(1)}, u32[]{:S(2)}, u32[]{:S(2)}) %collective-permute-start) | collective-permute-done | bytes 800 | tf_op jit(solution)/shard_map/ppermute | solution.py:608
  17.6 2.6 %modulate.1 = (f32[2,5376]{1,0:T(2,128)S(1)}, f32[2,5376]{1,0:T(2,128)S(1)}, f32[2,5376]{1,0:T(2,128)S(1)}, f32[2,5376]{1,0:T(2,128)S(1)}) custom-call(s32[3]{0:T(128)S(1)} %pad_add_fusion.refs_0_.idx, bf16[2,96,2304]{2,1,0:T(8,128)(2,1)S(1)} %copy-done.4, bf16[2,576]{1,0:T(2,128)(2,1)} %refs_2_.3, bf16[2,192]{1,0:T(2,128)(2,1)} %refs_3_.6, ...), custom_call_target="tpu_custom_call" | custom-call | flops 1 | bytes 1 | tf_op jit(solution)/shard_map/modulate/pallas_call | solution.py:71
  27.8 4.7 %collective-permute-done.8.refs_6_.refs_10_.refs_11_ = bf16[96,2304]{1,0:T(8,128)(2,1)S(1)} collective-permute-done((bf16[96,2304]{1,0:T(8,128)(2,1)S(1)}, bf16[96,2304]{1,0:T(8,128)(2,1)S(1)}, u32[]{:S(2)}, u32[]{:S(2)}) %collective-permute-start.8) | collective-permute-done | bytes 442400 | tf_op jit(solution)/shard_map/ppermute | solution.py:608
  33.5 5.9 %collective-permute-done.7.whole.refs_5_.refs_6_.refs_10_ = bf16[96,4608]{1,0:T(8,128)(2,1)S(1)} collective-permute-done((bf16[96,4608]{1,0:T(8,128)(2,1)S(1)}, bf16[96,4608]{1,0:T(8,128)(2,1)S(1)}, u32[]{:S(2)}, u32[]{:S(2)}) %collective-permute-start.7) | collective-permute-done | bytes 884768 | tf_op jit(solution)/shard_map/ppermute | solution.py:608
  41.5 4.3 %attention_forward.2 = (bf16[256,1152]{1,0:T(8,128)(2,1)}, f32[6,256,256]{2,1,0:T(8,128)}, bf16[256,384]{1,0:T(8,128)(2,1)}, f32[256,384]{1,0:T(8,128)}, f32[256,384]{1,0:T(8,128)S(1)}) custom-call(s32[3]{0:T(128)S(1)} %pad_add_fusion.refs_0_.idx, bf16[256,384]{1,0:T(8,128)(2,1)S(1)} %bitcast.7, f32[2,5376]{1,0:T(2,128)S(1)} %add_add_fusion.refs_2_, ...), custom_call_target="tpu_custom_call" | custom-call | flops 1 | bytes 1 | tf_op jit(solution)/shard_map/attention_forward/pallas_call | solution.py:71
  46.2 2.2 %collective-permute-done.11.refs_6_.refs_7_.refs_11_ = bf16[96,2304]{1,0:T(8,128)(2,1)S(1)} collective-permute-done((bf16[96,2304]{1,0:T(8,128)(2,1)S(1)}, bf16[96,2304]{1,0:T(8,128)(2,1)S(1)}, u32[]{:S(2)}, u32[]{:S(2)}) %collective-permute-start.11) | collective-permute-done | bytes 442400 | tf_op jit(solution)/shard_map/ppermute | solution.py:608
  48.4 4.8 %mlp_forward.1 = (bf16[256,1536]{1,0:T(8,128)(2,1)}, f32[256,1536]{1,0:T(8,128)}, f32[256,384]{1,0:T(8,128)}, f32[256,384]{1,0:T(8,128)S(1)}) custom-call(s32[3]{0:T(128)S(1)} %pad_add_fusion.refs_0_.idx, f32[256,384]{1,0:T(8,128)S(1)} %get-tuple-element.115.refs_1_, f32[2,5376]{1,0:T(2,128)S(1)} %add_add_fusion.refs_2_, bf16[2,96,1536]{2,1,0:T(8,128)(2,1)S(1)} %copy-done.1, ...), custom_call_target="tpu_custom_call" | custom-call | flops 1 | bytes 1 | tf_op jit(solution)/shard_map/mlp_forward/pallas_call | solution.py:71
  53.2 3.0 %attention_forward.3 = (bf16[256,1152]{1,0:T(8,128)(2,1)S(1)}, f32[6,256,256]{2,1,0:T(8,128)S(1)}, bf16[256,384]{1,0:T(8,128)(2,1)S(1)}, f32[256,384]{1,0:T(8,128)S(1)}, f32[256,384]{1,0:T(8,128)S(1)}) custom-call(s32[3]{0:T(128)S(1)} %pad_add_fusion.refs_0_.idx, f32[256,384]{1,0:T(8,128)S(1)} %get-tuple-element.116.refs_1_, ...), custom_call_target="tpu_custom_call" | custom-call | flops 1 | bytes 1 | tf_op jit(solution)/shard_map/attention_forward/pallas_call | solution.py:71
  56.3 7.1 %mlp_both.1 = (bf16[256,384]{1,0:T(8,128)(2,1)}, f32[256,384]{1,0:T(8,128)S(1)}, f32[1,3072]{1,0:T(1,128)S(1)}, bf16[4,96,1536]{2,1,0:T(8,128)(2,1)S(1)}, bf16[4,96,1536]{2,1,0:T(8,128)(2,1)S(1)}) custom-call(s32[3]{0:T(128)S(1)} %pad_add_fusion.refs_0_.idx, f32[256,384]{1,0:T(8,128)S(1)} %get-tuple-element.119.refs_1_, f32[2,5376]{1,0:T(2,128)S(1)} %add_add_fusion.refs_2_, ...), custom_call_target="tpu_custom_call" | custom-call | flops 1 | bytes 1 | tf_op jit(solution)/shard_map/mlp_both/pallas_call | solution.py:71
  64.0 5.9 %attention_backward.2 = (f32[256,384]{1,0:T(8,128)S(1)}, f32[1,2304]{1,0:T(1,128)S(1)}, bf16[4,96,768]{2,1,0:T(8,128)(2,1)S(1)}, bf16[4,96,768]{2,1,0:T(8,128)(2,1)S(1)}) custom-call(s32[3]{0:T(128)S(1)} %pad_add_fusion.refs_0_.idx, f32[256,384]{1,0:T(8,128)S(1)} %get-tuple-element.116.refs_1_, f32[2,5376]{1,0:T(2,128)S(1)} %add_add_fusion.refs_2_, ...), custom_call_target="tpu_custom_call" | custom-call | flops 1 | bytes 1 | tf_op jit(solution)/shard_map/attention_backward/pallas_call | solution.py:71
  69.9 2.0 %collective-permute-done.14.refs_2_ = bf16[4,96,768]{2,1,0:T(8,128)(2,1)S(1)} collective-permute-done((bf16[4,96,768]{2,1,0:T(8,128)(2,1)S(1)}, bf16[4,96,768]{2,1,0:T(8,128)(2,1)S(1)}, u32[]{:S(2)}, u32[]{:S(2)}) %collective-permute-start.14) | collective-permute-done | bytes 589856 | tf_op jit(solution)/shard_map/ppermute | solution.py:608
  73.6 4.6 %mlp_backward.1 = (f32[256,384]{1,0:T(8,128)S(1)}, f32[1,3072]{1,0:T(1,128)S(1)}, bf16[4,96,1536]{2,1,0:T(8,128)(2,1)S(1)}, bf16[4,96,1536]{2,1,0:T(8,128)(2,1)S(1)}) custom-call(s32[3]{0:T(128)S(1)} %pad_add_fusion.refs_0_.idx, f32[256,384]{1,0:T(8,128)S(1)} %get-tuple-element.115.refs_1_, f32[2,5376]{1,0:T(2,128)S(1)} %add_add_fusion.refs_2_, ...), custom_call_target="tpu_custom_call" | custom-call | flops 1 | bytes 1 | tf_op jit(solution)/shard_map/mlp_backward/pallas_call | solution.py:71
  81.6 6.8 %attention_backward.3 = (f32[256,384]{1,0:T(8,128)}, f32[1,2304]{1,0:T(1,128)S(1)}, bf16[4,96,768]{2,1,0:T(8,128)(2,1)S(1)}, bf16[4,96,768]{2,1,0:T(8,128)(2,1)S(1)}) custom-call(s32[3]{0:T(128)S(1)} %pad_add_fusion.refs_0_.idx, bf16[256,384]{1,0:T(8,128)(2,1)S(1)} %bitcast.8, f32[2,5376]{1,0:T(2,128)S(1)} %add_add_fusion.refs_2_, ...), custom_call_target="tpu_custom_call" | custom-call | flops 1 | bytes 1 | tf_op jit(solution)/shard_map/attention_backward/pallas_call | solution.py:71
  95.1 7.9 %collective-permute-done.19.other = bf16[2,96,1536]{2,1,0:T(8,128)(2,1)S(1)} collective-permute-done((bf16[2,96,1536]{2,1,0:T(8,128)(2,1)S(1)}, bf16[2,96,1536]{2,1,0:T(8,128)(2,1)S(1)}, u32[]{:S(2)}, u32[]{:S(2)}) %collective-permute-start.19) | collective-permute-done | bytes 589856 | tf_op jit(solution)/shard_map/ppermute | solution.py:608
  103.2 1.8 %collective-permute-done.20.refs_2_ = bf16[96,2304]{1,0:T(8,128)(2,1)S(1)} collective-permute-done((bf16[96,2304]{1,0:T(8,128)(2,1)S(1)}, bf16[96,2304]{1,0:T(8,128)(2,1)S(1)}, u32[]{:S(2)}, u32[]{:S(2)}) %collective-permute-start.20) | collective-permute-done | bytes 442400 | tf_op jit(solution)/shard_map/ppermute | solution.py:608
  107.2 1.6 collective-permute-start.24
  111.1 2.5 %collective-permute-done.22.second = bf16[1,11136]{1,0:T(2,128)(2,1)S(1)} collective-permute-done((bf16[1,11136]{1,0:T(2,128)(2,1)S(1)}, bf16[1,11136]{1,0:T(2,128)(2,1)S(1)}, u32[]{:S(2)}, u32[]{:S(2)}) %collective-permute-start.22) | collective-permute-done | bytes 22304 | tf_op jit(solution)/shard_map/ppermute | solution.py:608
  116.7 2.6 %collective-permute-start.32 = (bf16[48,2304]{1,0:T(8,128)(2,1)S(1)}, bf16[48,2304]{1,0:T(8,128)(2,1)S(1)}, u32[]{:S(2)}, u32[]{:S(2)}) collective-permute-start(bf16[48,2304]{1,0:T(8,128)(2,1)S(1)} %add.72.refs_0_), channel_id=1, source_target_pairs={{0,4},{1,5},{2,6},{3,7},{4,0},{5,1},{6,2},{7,3},{8,12},{9,13},{10,... | collective-permute-start | bytes 663560 | tf_op jit(solution)/shard_map/ppermute | solution.py:608
  120.7 2.6 %collective-permute-done.26.second = bf16[2,11136]{1,0:T(2,128)(2,1)S(1)} collective-permute-done((bf16[2,11136]{1,0:T(2,128)(2,1)S(1)}, bf16[2,11136]{1,0:T(2,128)(2,1)S(1)}, u32[]{:S(2)}, u32[]{:S(2)}) %collective-permute-start.26) | collective-permute-done | bytes 44576 | tf_op jit(solution)/shard_map/ppermute | solution.py:608
  123.3 2.1 %group.1 = (f32[2,384]{1,0:T(2,128)S(1)}, f32[2,384]{1,0:T(2,128)S(1)}, bf16[6,4992]{1,0:T(8,128)(2,1)S(1)}) custom-call(s32[3]{0:T(128)S(1)} %pad_add_fusion.refs_0_.idx, bf16[2,96,2304]{2,1,0:T(8,128)(2,1)S(1)} %copy-done.4, bf16[2,11136]{1,0:T(2,128)(2,1)S(1)} %stack.18.first, bf16[2,11136]{1,0:T(2,128)(2,1)S(1)} %collective-permute-done.26.second), custom_call_target="tpu_custom_call" | custom-call | flops 1 | bytes 1 | tf_op jit(solution)/shard_map/group/pallas_call | solution.py:71
  126.5 3.4 %collective-permute-done.31.second = bf16[6,4992]{1,0:T(8,128)(2,1)S(1)} collective-permute-done((bf16[6,4992]{1,0:T(8,128)(2,1)S(1)}, bf16[6,4992]{1,0:T(8,128)(2,1)S(1)}, u32[]{:S(2)}, u32[]{:S(2)}) %collective-permute-start.31) | collective-permute-done | bytes 59936 | tf_op jit(solution)/shard_map/ppermute | solution.py:608
  131.8 2.2 %collective-permute-done.27 = f32[2,384]{1,0:T(2,128)S(1)} collective-permute-done((f32[2,384]{1,0:T(2,128)S(1)}, f32[2,384]{1,0:T(2,128)S(1)}, u32[]{:S(2)}, u32[]{:S(2)}) %collective-permute-start.27) | collective-permute-done | bytes 3104 | tf_op jit(solution)/shard_map/ppermute | solution.py:608
  134.0 2.1 %collective-permute-start.28 = (f32[1,384]{1,0:T(1,128)S(1)}, f32[1,384]{1,0:T(1,128)S(1)}, u32[]{:S(2)}, u32[]{:S(2)}) collective-permute-start(f32[1,384]{1,0:T(1,128)S(1)} %slice.97), channel_id=1, source_target_pairs={{0,8},{1,17},{2,10},{3,19},{4,12},{5,21},{6,14},{7,23},{8,0},{9,25... | collective-permute-start | bytes 4616 | tf_op jit(solution)/shard_map/ppermute | solution.py:608
  136.1 2.0 %collective-permute-start.39 = (bf16[48,1536]{1,0:T(8,128)(2,1)S(1)}, bf16[48,1536]{1,0:T(8,128)(2,1)S(1)}, u32[]{:S(2)}, u32[]{:S(2)}) collective-permute-start(bf16[48,1536]{1,0:T(8,128)(2,1)S(1)} %add.74.refs_0_), channel_id=1, source_target_pairs={{0,4},{1,5},{2,6},{3,7},{4,0},{5,1},{6,2},{7,3},{8,12},{9,13},{10,... | collective-permute-start | bytes 442376 | tf_op jit(solution)/shard_map/ppermute | solution.py:608
  138.2 4.2 %collective-permute-done.36.refs_2_ = bf16[10,4992]{1,0:T(8,128)(2,1)S(1)} collective-permute-done((bf16[10,4992]{1,0:T(8,128)(2,1)S(1)}, bf16[10,4992]{1,0:T(8,128)(2,1)S(1)}, u32[]{:S(2)}, u32[]{:S(2)}) %collective-permute-start.36) | collective-permute-done | bytes 99872 | tf_op jit(solution)/shard_map/ppermute | solution.py:608
  143.8 2.2 %ada_grad.1 = (f32[2,96,2304]{2,1,0:T(8,128)}, f32[1,10752]{1,0:T(1,128)S(1)}) custom-call(s32[3]{0:T(128)S(1)} %pad_add_fusion.refs_0_.idx, bf16[10,4992]{1,0:T(8,128)(2,1)S(1)} %stack.19.refs_1_, bf16[10,4992]{1,0:T(8,128)(2,1)S(1)} %collective-permute-done.36.refs_2_, bf16[10,4992]{1,0:T(8,128)(2,1)S(1)} %collective-permute-done.37.refs_3_, ...), custom_call_target="tpu_custom_call" | custom-call | flops 1 | bytes 1 | tf_op jit(solution)/shard_map/ada_grad/pallas_call | solution.py:71
  147.7 2.8 %collective-permute-done.43.refs_1_ = bf16[96,768]{1,0:T(8,128)(2,1)S(1)} collective-permute-done((bf16[96,768]{1,0:T(8,128)(2,1)S(1)}, bf16[96,768]{1,0:T(8,128)(2,1)S(1)}, u32[]{:S(2)}, u32[]{:S(2)}) %collective-permute-start.43) | collective-permute-done | bytes 147488 | tf_op jit(solution)/shard_map/ppermute | solution.py:608
  151.9 2.5 %collective-permute-done.33.refs_2_ = bf16[48,2304]{1,0:T(8,128)(2,1)S(1)} collective-permute-done((bf16[48,2304]{1,0:T(8,128)(2,1)S(1)}, bf16[48,2304]{1,0:T(8,128)(2,1)S(1)}, u32[]{:S(2)}, u32[]{:S(2)}) %collective-permute-start.33) | collective-permute-done | bytes 221216 | tf_op jit(solution)/shard_map/ppermute | solution.py:608
  154.4 2.8 %collective-permute-done.40.refs_6_ = bf16[48,1536]{1,0:T(8,128)(2,1)S(1)} collective-permute-done((bf16[48,1536]{1,0:T(8,128)(2,1)S(1)}, bf16[48,1536]{1,0:T(8,128)(2,1)S(1)}, u32[]{:S(2)}, u32[]{:S(2)}) %collective-permute-start.40) | collective-permute-done | bytes 147488 | tf_op jit(solution)/shard_map/ppermute | solution.py:608
  158.6 2.6 %finish.1 = (f32[2,96,1152]{2,1,0:T(8,128)}, f32[2,96,384]{2,1,0:T(8,128)}, f32[2,96,1536]{2,1,0:T(8,128)}, f32[2,384,384]{2,1,0:T(8,128)}) custom-call(s32[3]{0:T(128)S(1)} %pad_add_fusion.refs_0_.idx, bf16[48,2304]{1,0:T(8,128)(2,1)S(1)} %add.76.refs_1_, bf16[48,2304]{1,0:T(8,128)(2,1)S(1)} %collective-permute-done.33.refs_2_, ...), custom_call_target="tpu_custom_call" | custom-call | flops 1 | bytes 1 | tf_op jit(solution)/shard_map/finish/pallas_call | solution.py:71
  (148 shorter events, 45.7 us)
Async XLA Ops:
  2.0 18.2 %collective-permute-start.3 = (bf16[96,4608]{1,0:T(8,128)(2,1)S(1)}, bf16[96,4608]{1,0:T(8,128)(2,1)S(1)}, u32[]{:S(2)}, u32[]{:S(2)}) collective-permute-start(bf16[96,4608]{1,0:T(8,128)(2,1)S(1)} %pack.2), channel_id=1, source_target_pairs={{0,8},{1,17},{2,10},{3,19},{4,12},{5,21},{6,14},{7,23},{8,0},{9,25... | collective-permute-start | bytes 2654216 | tf_op jit(solution)/shard_map/ppermute | solution.py:608
  5.0 11.1 %collective-permute-start = (bf16[1,384]{1,0:T(2,128)(2,1)S(1)}, bf16[1,384]{1,0:T(2,128)(2,1)S(1)}, u32[]{:S(2)}, u32[]{:S(2)}) collective-permute-start(bf16[1,384]{1,0:T(2,128)(2,1)S(1)} %copy-done.14), channel_id=1, source_target_pairs={{0,8},{1,9},{2,10},{3,11},{4,12},{5,13},{6,14},{7,15},{8,0},{9,1},... | collective-permute-start | bytes 2312 | tf_op jit(solution)/shard_map/ppermute | solution.py:608
  5.1 11.0 %collective-permute-start.1 = (bf16[1,384]{1,0:T(2,128)(2,1)S(1)}, bf16[1,384]{1,0:T(2,128)(2,1)S(1)}, u32[]{:S(2)}, u32[]{:S(2)}) collective-permute-start(bf16[1,384]{1,0:T(2,128)(2,1)S(1)} %copy-done.14), channel_id=1, source_target_pairs={{0,16},{1,17},{2,18},{3,19},{4,20},{5,21},{6,22},{7,23},{8,24},{9,... | collective-permute-start | bytes 2312 | tf_op jit(solution)/shard_map/ppermute | solution.py:608
  7.1 10.5 %collective-permute-start.2 = (bf16[1,384]{1,0:T(2,128)(2,1)S(1)}, bf16[1,384]{1,0:T(2,128)(2,1)S(1)}, u32[]{:S(2)}, u32[]{:S(2)}) collective-permute-start(bf16[1,384]{1,0:T(2,128)(2,1)S(1)} %copy-done.14), channel_id=1, source_target_pairs={{0,24},{1,25},{2,26},{3,27},{4,28},{5,29},{6,30},{7,31},{8,16},{9,... | collective-permute-start | bytes 2312 | tf_op jit(solution)/shard_map/ppermute | solution.py:608
  20.8 11.7 %collective-permute-start.8 = (bf16[96,2304]{1,0:T(8,128)(2,1)S(1)}, bf16[96,2304]{1,0:T(8,128)(2,1)S(1)}, u32[]{:S(2)}, u32[]{:S(2)}) collective-permute-start(bf16[96,2304]{1,0:T(8,128)(2,1)S(1)} %half.2), channel_id=1, source_target_pairs={{0,16},{1,9},{2,18},{3,11},{4,20},{5,13},{6,22},{7,15},{8,24},{9,1... | collective-permute-start | bytes 1327112 | tf_op jit(solution)/shard_map/ppermute | solution.py:608
  23.0 10.5 %collective-permute-start.5 = (f32[2,5376]{1,0:T(2,128)S(1)}, f32[2,5376]{1,0:T(2,128)S(1)}, u32[]{:S(2)}, u32[]{:S(2)}) collective-permute-start(f32[2,5376]{1,0:T(2,128)S(1)} %get-tuple-element.109), channel_id=1, source_target_pairs={{0,16},{1,17},{2,18},{3,19},{4,20},{5,21},{6,22},{7,23},{8,24},{9,... | collective-permute-start | bytes 129032 | tf_op jit(solution)/shard_map/ppermute | solution.py:608
  24.4 9.0 %collective-permute-start.6 = (f32[2,5376]{1,0:T(2,128)S(1)}, f32[2,5376]{1,0:T(2,128)S(1)}, u32[]{:S(2)}, u32[]{:S(2)}) collective-permute-start(f32[2,5376]{1,0:T(2,128)S(1)} %get-tuple-element.111), channel_id=1, source_target_pairs={{0,24},{1,25},{2,26},{3,27},{4,28},{5,29},{6,30},{7,31},{8,16},{9,... | collective-permute-start | bytes 129032 | tf_op jit(solution)/shard_map/ppermute | solution.py:608
  26.3 13.1 %collective-permute-start.7 = (bf16[96,4608]{1,0:T(8,128)(2,1)S(1)}, bf16[96,4608]{1,0:T(8,128)(2,1)S(1)}, u32[]{:S(2)}, u32[]{:S(2)}) collective-permute-start(bf16[96,4608]{1,0:T(8,128)(2,1)S(1)} %pack.3), channel_id=1, source_target_pairs={{0,8},{1,17},{2,10},{3,19},{4,12},{5,21},{6,14},{7,23},{8,0},{9,25... | collective-permute-start | bytes 2654216 | tf_op jit(solution)/shard_map/ppermute | solution.py:608
  27.8 13.7 %collective-permute-start.9 = (bf16[96,4608]{1,0:T(8,128)(2,1)S(1)}, bf16[96,4608]{1,0:T(8,128)(2,1)S(1)}, u32[]{:S(2)}, u32[]{:S(2)}) collective-permute-start(bf16[96,4608]{1,0:T(8,128)(2,1)S(1)} %collective-permute-done.3.whole.refs_5_.refs_9_.refs_10_), channel_id=1, source_target_pairs={{0,1},{1,0},{2,3},{3,2},{4,5},{5,4},{6,7},{7,6},{8,9},{9,8},{10,11... | collective-permute-start | bytes 2654216 | tf_op jit(solution)/shard_map/ppermute | solution.py:608
  32.5 9.0 %collective-permute-start.10 = (bf16[96,2304]{1,0:T(8,128)(2,1)S(1)}, bf16[96,2304]{1,0:T(8,128)(2,1)S(1)}, u32[]{:S(2)}, u32[]{:S(2)}) collective-permute-start(bf16[96,2304]{1,0:T(8,128)(2,1)S(1)} %collective-permute-done.8.refs_6_.refs_10_.refs_11_), channel_id=1, source_target_pairs={{0,1},{1,0},{2,3},{3,2},{4,5},{5,4},{6,7},{7,6},{8,9},{9,8},{10,11... | collective-permute-start | bytes 1327112 | tf_op jit(solution)/shard_map/ppermute | solution.py:608
  40.0 8.4 %collective-permute-start.11 = (bf16[96,2304]{1,0:T(8,128)(2,1)S(1)}, bf16[96,2304]{1,0:T(8,128)(2,1)S(1)}, u32[]{:S(2)}, u32[]{:S(2)}) collective-permute-start(bf16[96,2304]{1,0:T(8,128)(2,1)S(1)} %half.3), channel_id=1, source_target_pairs={{0,16},{1,9},{2,18},{3,11},{4,20},{5,13},{6,22},{7,15},{8,24},{9,1... | collective-permute-start | bytes 1327112 | tf_op jit(solution)/shard_map/ppermute | solution.py:608
  45.8 7.4 %collective-permute-start.12 = (bf16[96,4608]{1,0:T(8,128)(2,1)S(1)}, bf16[96,4608]{1,0:T(8,128)(2,1)S(1)}, u32[]{:S(2)}, u32[]{:S(2)}) collective-permute-start(bf16[96,4608]{1,0:T(8,128)(2,1)S(1)} %collective-permute-done.7.whole.refs_5_.refs_6_.refs_10_), channel_id=1, source_target_pairs={{0,1},{1,0},{2,3},{3,2},{4,5},{5,4},{6,7},{7,6},{8,9},{9,8},{10,11... | collective-permute-start | bytes 2654216 | tf_op jit(solution)/shard_map/ppermute | solution.py:608
  63.4 8.5 %collective-permute-start.15 = (bf16[4,96,1536]{2,1,0:T(8,128)(2,1)S(1)}, bf16[4,96,1536]{2,1,0:T(8,128)(2,1)S(1)}, u32[]{:S(2)}, u32[]{:S(2)}) collective-permute-start(bf16[4,96,1536]{2,1,0:T(8,128)(2,1)S(1)} %get-tuple-element.131), channel_id=1, source_target_pairs={{0,1},{1,0},{2,3},{3,2},{4,5},{5,4},{6,7},{7,6},{8,9},{9,8},{10,11... | collective-permute-start | bytes 3538952 | tf_op jit(solution)/shard_map/ppermute | solution.py:608
  78.5 13.0 %collective-permute-start.17 = (bf16[2,96,2304]{2,1,0:T(8,128)(2,1)S(1)}, bf16[2,96,2304]{2,1,0:T(8,128)(2,1)S(1)}, u32[]{:S(2)}, u32[]{:S(2)}) collective-permute-start(bf16[2,96,2304]{2,1,0:T(8,128)(2,1)S(1)} %get-tuple-element.154), channel_id=1, source_target_pairs={{0,8},{1,17},{2,10},{3,19},{4,12},{5,21},{6,14},{7,23},{8,0},{9,25... | collective-permute-start | bytes 2654216 | tf_op jit(solution)/shard_map/ppermute | solution.py:608
  88.6 14.4 %collective-permute-start.19 = (bf16[2,96,1536]{2,1,0:T(8,128)(2,1)S(1)}, bf16[2,96,1536]{2,1,0:T(8,128)(2,1)S(1)}, u32[]{:S(2)}, u32[]{:S(2)}) collective-permute-start(bf16[2,96,1536]{2,1,0:T(8,128)(2,1)S(1)} %get-tuple-element.160), channel_id=1, source_target_pairs={{0,8},{1,17},{2,10},{3,19},{4,12},{5,21},{6,14},{7,23},{8,0},{9,25... | collective-permute-start | bytes 1769480 | tf_op jit(solution)/shard_map/ppermute | solution.py:608
  91.8 13.2 %collective-permute-start.20 = (bf16[96,2304]{1,0:T(8,128)(2,1)S(1)}, bf16[96,2304]{1,0:T(8,128)(2,1)S(1)}, u32[]{:S(2)}, u32[]{:S(2)}) collective-permute-start(bf16[96,2304]{1,0:T(8,128)(2,1)S(1)} %get-tuple-element.164), channel_id=1, source_target_pairs={{0,16},{1,9},{2,18},{3,11},{4,20},{5,13},{6,22},{7,15},{8,24},{9,1... | collective-permute-start | bytes 1327112 | tf_op jit(solution)/shard_map/ppermute | solution.py:608
  93.5 15.3 %collective-permute-start.21 = (bf16[2,96,768]{2,1,0:T(8,128)(2,1)S(1)}, bf16[2,96,768]{2,1,0:T(8,128)(2,1)S(1)}, u32[]{:S(2)}, u32[]{:S(2)}) collective-permute-start(bf16[2,96,768]{2,1,0:T(8,128)(2,1)S(1)} %get-tuple-element.167), channel_id=1, source_target_pairs={{0,8},{1,17},{2,10},{3,19},{4,12},{5,21},{6,14},{7,23},{8,0},{9,25... | collective-permute-start | bytes 884744 | tf_op jit(solution)/shard_map/ppermute | solution.py:608
  105.7 8.0 %collective-permute-start.23 = (bf16[96,1536]{1,0:T(8,128)(2,1)S(1)}, bf16[96,1536]{1,0:T(8,128)(2,1)S(1)}, u32[]{:S(2)}, u32[]{:S(2)}) collective-permute-start(bf16[96,1536]{1,0:T(8,128)(2,1)S(1)} %get-tuple-element.171), channel_id=1, source_target_pairs={{0,16},{1,9},{2,18},{3,11},{4,20},{5,13},{6,22},{7,15},{8,24},{9,1... | collective-permute-start | bytes 884744 | tf_op jit(solution)/shard_map/ppermute | solution.py:608
  107.2 7.2 %collective-permute-start.24 = (bf16[48,2304]{1,0:T(8,128)(2,1)S(1)}, bf16[48,2304]{1,0:T(8,128)(2,1)S(1)}, u32[]{:S(2)}, u32[]{:S(2)}) collective-permute-start(bf16[48,2304]{1,0:T(8,128)(2,1)S(1)} %get-tuple-element.174), channel_id=1, source_target_pairs={{0,2},{1,3},{2,0},{3,1},{4,6},{5,7},{6,4},{7,5},{8,10},{9,11},{10,... | collective-permute-start | bytes 663560 | tf_op jit(solution)/shard_map/ppermute | solution.py:608
  108.9 6.5 %collective-permute-start.25 = (bf16[96,768]{1,0:T(8,128)(2,1)S(1)}, bf16[96,768]{1,0:T(8,128)(2,1)S(1)}, u32[]{:S(2)}, u32[]{:S(2)}) collective-permute-start(bf16[96,768]{1,0:T(8,128)(2,1)S(1)} %get-tuple-element.176), channel_id=1, source_target_pairs={{0,16},{1,9},{2,18},{3,11},{4,20},{5,13},{6,22},{7,15},{8,24},{9,1... | collective-permute-start | bytes 442376 | tf_op jit(solution)/shard_map/ppermute | solution.py:608
  114.5 11.8 %collective-permute-start.29 = (bf16[48,1536]{1,0:T(8,128)(2,1)S(1)}, bf16[48,1536]{1,0:T(8,128)(2,1)S(1)}, u32[]{:S(2)}, u32[]{:S(2)}) collective-permute-start(bf16[48,1536]{1,0:T(8,128)(2,1)S(1)} %get-tuple-element.182), channel_id=1, source_target_pairs={{0,2},{1,3},{2,0},{3,1},{4,6},{5,7},{6,4},{7,5},{8,10},{9,11},{10,... | collective-permute-start | bytes 442376 | tf_op jit(solution)/shard_map/ppermute | solution.py:608
  115.4 11.0 %collective-permute-start.30 = (bf16[96,768]{1,0:T(8,128)(2,1)S(1)}, bf16[96,768]{1,0:T(8,128)(2,1)S(1)}, u32[]{:S(2)}, u32[]{:S(2)}) collective-permute-start(bf16[96,768]{1,0:T(8,128)(2,1)S(1)} %add.73.refs_0_), channel_id=1, source_target_pairs={{0,2},{1,3},{2,0},{3,1},{4,6},{5,7},{6,4},{7,5},{8,10},{9,11},{10,... | collective-permute-start | bytes 442376 | tf_op jit(solution)/shard_map/ppermute | solution.py:608
  116.7 21.4 %collective-permute-start.32 = (bf16[48,2304]{1,0:T(8,128)(2,1)S(1)}, bf16[48,2304]{1,0:T(8,128)(2,1)S(1)}, u32[]{:S(2)}, u32[]{:S(2)}) collective-permute-start(bf16[48,2304]{1,0:T(8,128)(2,1)S(1)} %add.72.refs_0_), channel_id=1, source_target_pairs={{0,4},{1,5},{2,6},{3,7},{4,0},{5,1},{6,2},{7,3},{8,12},{9,13},{10,... | collective-permute-start | bytes 663560 | tf_op jit(solution)/shard_map/ppermute | solution.py:608
  130.0 12.5 %collective-permute-start.36 = (bf16[10,4992]{1,0:T(8,128)(2,1)S(1)}, bf16[10,4992]{1,0:T(8,128)(2,1)S(1)}, u32[]{:S(2)}, u32[]{:S(2)}) collective-permute-start(bf16[10,4992]{1,0:T(8,128)(2,1)S(1)} %stack.19.refs_1_), channel_id=1, source_target_pairs={{0,4},{1,5},{2,6},{3,7},{4,0},{5,1},{6,2},{7,3},{8,12},{9,13},{10,... | collective-permute-start | bytes 299528 | tf_op jit(solution)/shard_map/ppermute | solution.py:608
  134.0 8.5 %collective-permute-start.28 = (f32[1,384]{1,0:T(1,128)S(1)}, f32[1,384]{1,0:T(1,128)S(1)}, u32[]{:S(2)}, u32[]{:S(2)}) collective-permute-start(f32[1,384]{1,0:T(1,128)S(1)} %slice.97), channel_id=1, source_target_pairs={{0,8},{1,17},{2,10},{3,19},{4,12},{5,21},{6,14},{7,23},{8,0},{9,25... | collective-permute-start | bytes 4616 | tf_op jit(solution)/shard_map/ppermute | solution.py:608
  136.1 10.0 %collective-permute-start.39 = (bf16[48,1536]{1,0:T(8,128)(2,1)S(1)}, bf16[48,1536]{1,0:T(8,128)(2,1)S(1)}, u32[]{:S(2)}, u32[]{:S(2)}) collective-permute-start(bf16[48,1536]{1,0:T(8,128)(2,1)S(1)} %add.74.refs_0_), channel_id=1, source_target_pairs={{0,4},{1,5},{2,6},{3,7},{4,0},{5,1},{6,2},{7,3},{8,12},{9,13},{10,... | collective-permute-start | bytes 442376 | tf_op jit(solution)/shard_map/ppermute | solution.py:608
  143.0 7.5 %collective-permute-start.43 = (bf16[96,768]{1,0:T(8,128)(2,1)S(1)}, bf16[96,768]{1,0:T(8,128)(2,1)S(1)}, u32[]{:S(2)}, u32[]{:S(2)}) collective-permute-start(bf16[96,768]{1,0:T(8,128)(2,1)S(1)} %add.75.refs_0_), channel_id=1, source_target_pairs={{0,4},{1,5},{2,6},{3,7},{4,0},{5,1},{6,2},{7,3},{8,12},{9,13},{10,... | collective-permute-start | bytes 442376 | tf_op jit(solution)/shard_map/ppermute | solution.py:608
  143.0 11.4 %collective-permute-start.33 = (bf16[48,2304]{1,0:T(8,128)(2,1)S(1)}, bf16[48,2304]{1,0:T(8,128)(2,1)S(1)}, u32[]{:S(2)}, u32[]{:S(2)}) collective-permute-start(bf16[48,2304]{1,0:T(8,128)(2,1)S(1)} %add.76.refs_1_), channel_id=1, source_target_pairs={{0,2},{1,3},{2,0},{3,1},{4,6},{5,7},{6,4},{7,5},{8,10},{9,11},{10,... | collective-permute-start | bytes 663560 | tf_op jit(solution)/shard_map/ppermute | solution.py:608
  143.3 15.2 %collective-permute-start.34 = (bf16[48,2304]{1,0:T(8,128)(2,1)S(1)}, bf16[48,2304]{1,0:T(8,128)(2,1)S(1)}, u32[]{:S(2)}, u32[]{:S(2)}) collective-permute-start(bf16[48,2304]{1,0:T(8,128)(2,1)S(1)} %add.76.refs_1_), channel_id=1, source_target_pairs={{0,1},{1,0},{2,3},{3,2},{4,5},{5,4},{6,7},{7,6},{8,9},{9,8},{10,11... | collective-permute-start | bytes 663560 | tf_op jit(solution)/shard_map/ppermute | solution.py:608
  146.1 11.1 %collective-permute-start.40 = (bf16[48,1536]{1,0:T(8,128)(2,1)S(1)}, bf16[48,1536]{1,0:T(8,128)(2,1)S(1)}, u32[]{:S(2)}, u32[]{:S(2)}) collective-permute-start(bf16[48,1536]{1,0:T(8,128)(2,1)S(1)} %add.77.refs_5_), channel_id=1, source_target_pairs={{0,2},{1,3},{2,0},{3,1},{4,6},{5,7},{6,4},{7,5},{8,10},{9,11},{10,... | collective-permute-start | bytes 442376 | tf_op jit(solution)/shard_map/ppermute | solution.py:608
  147.6 10.9 %collective-permute-start.41 = (bf16[48,1536]{1,0:T(8,128)(2,1)S(1)}, bf16[48,1536]{1,0:T(8,128)(2,1)S(1)}, u32[]{:S(2)}, u32[]{:S(2)}) collective-permute-start(bf16[48,1536]{1,0:T(8,128)(2,1)S(1)} %add.77.refs_5_), channel_id=1, source_target_pairs={{0,1},{1,0},{2,3},{3,2},{4,5},{5,4},{6,7},{7,6},{8,9},{9,8},{10,11... | collective-permute-start | bytes 442376 | tf_op jit(solution)/shard_map/ppermute | solution.py:608
  150.5 8.0 %collective-permute-start.44 = (bf16[96,768]{1,0:T(8,128)(2,1)S(1)}, bf16[96,768]{1,0:T(8,128)(2,1)S(1)}, u32[]{:S(2)}, u32[]{:S(2)}) collective-permute-start(bf16[96,768]{1,0:T(8,128)(2,1)S(1)} %add.78.refs_9_), channel_id=1, source_target_pairs={{0,1},{1,0},{2,3},{3,2},{4,5},{5,4},{6,7},{7,6},{8,9},{9,8},{10,11... | collective-permute-start | bytes 442376 | tf_op jit(solution)/shard_map/ppermute | solution.py:608
  (29 other events, 156.5 us)

commit v5 on v4

--- a/solution.py
+++ b/solution.py
@@ -879,12 +879,14 @@
     arriving = exchange(stacked, by_level=step)
     a = (a[0], add([after(a[1], stacked), a_moving], a[1].shape))
     a_parts = level_last(*a, 4)
+    b = (b[0], add([after(b[1], a[1]), b_moving], b[1].shape))
+    b_parts = level_last(*b, 4)
     grad_cond = grad_cond + exchange(passed, turn=masks[-1])
     for mask in masks[-2::-1]:
         half = grad_cond.shape[0] // 2
         grad_cond = grad_cond[:half] + exchange(grad_cond[half:], turn=mask)
     cond_grad = jax.vjp(jax.nn.silu, cond_in)[1](grad_cond)[0]
-    stacks = [after(stacked, a[1]), arriving]
+    stacks = [after(stacked, b[1]), arriving]
     stacks = stacks + far_of(stacks)
     grad_ada, sums = run(
         functools.partial(ada_grad_kernel, rows, wide, extra, factor), "ada_grad",
@@ -894,9 +896,7 @@
         flops=10**8,
     )
 
-    b = (b[0], add([after(b[1], sums), b_moving], b[1].shape))
-    b_parts = level_last(*b, 4)
-    c = (c[0], add([after(c[1], b[1]), c_moving], c[1].shape))
+    c = (c[0], add([after(c[1], sums), c_moving], c[1].shape))
     finals = [a_parts, b_parts, level_last(*c, 4)]
 
     def own_part(parts):

time: 161 us -> 158 us (0.981)
  waiting for transfers between devices: 60.3 us -> 56.5 us
    ppermute x45, waiting for transfers between devices: 60.3 us -> 56.5 us  [exchange(): return lax.ppermute(array, ('shard', 'rep'), moves)]
  transfers between devices with their start and end apart: 45 -> 45, of which waited for: 21 -> 20; matrix products, arithmetic and copies ran while one was open for 2% -> 2% of each run, Pallas kernels for 21% -> 21%
where the time goes in v5:
time: 158 us
  waiting for transfers between devices  56.5 us (36%)
  Pallas kernels  53.1 us (34%)
  starting transfers between devices  42.5 us (27%)
  other arithmetic  3.39 us (2%)
  local copies, waits for them, and re-layouts  1.58 us (1%)
    ppermute x45, waiting for transfers between devices, exchange(): return lax.ppermute(array, ('shard', 'rep'), moves)  56.5 us
    pallas_call x32, Pallas kernels, run(): pl.pallas_call(body, out_shape=[pltpu.HBM(shape, dtype) if kind in 'hk' e...  53.1 us
    ppermute x45, starting transfers between devices, exchange(): return lax.ppermute(array, ('shard', 'rep'), moves)  42.5 us
  transfers between devices with their start and end apart: 45, of which 20 were waited for; matrix products, arithmetic and copies ran while one was open for 2% of the time, Pallas kernels for 21%

profile of v5, /device:TPU:0, one launch (start us, length us, event | category | flops | bytes accessed | tf_op | source)
XLA Modules:
  0.0 158.2 jit_solution(13690756987010376924)
XLA Ops:
  2.0 3.0 %collective-permute-start.3 = (bf16[96,4608]{1,0:T(8,128)(2,1)S(1)}, bf16[96,4608]{1,0:T(8,128)(2,1)S(1)}, u32[]{:S(2)}, u32[]{:S(2)}) collective-permute-start(bf16[96,4608]{1,0:T(8,128)(2,1)S(1)} %pack.2), channel_id=1, source_target_pairs={{0,8},{1,17},{2,10},{3,19},{4,12},{5,21},{6,14},{7,23},{8,0},{9,25... | collective-permute-start | bytes 2654216 | tf_op jit(solution)/shard_map/ppermute | solution.py:608
  5.1 2.0 %collective-permute-start.1 = (bf16[1,384]{1,0:T(2,128)(2,1)S(1)}, bf16[1,384]{1,0:T(2,128)(2,1)S(1)}, u32[]{:S(2)}, u32[]{:S(2)}) collective-permute-start(bf16[1,384]{1,0:T(2,128)(2,1)S(1)} %copy-done.14), channel_id=1, source_target_pairs={{0,16},{1,17},{2,18},{3,19},{4,20},{5,21},{6,22},{7,23},{8,24},{9,... | collective-permute-start | bytes 2312 | tf_op jit(solution)/shard_map/ppermute | solution.py:608
  8.6 7.5 %collective-permute-done.refs_8_ = bf16[1,384]{1,0:T(2,128)(2,1)S(1)} collective-permute-done((bf16[1,384]{1,0:T(2,128)(2,1)S(1)}, bf16[1,384]{1,0:T(2,128)(2,1)S(1)}, u32[]{:S(2)}, u32[]{:S(2)}) %collective-permute-start) | collective-permute-done | bytes 800 | tf_op jit(solution)/shard_map/ppermute | solution.py:608
  17.6 2.6 %modulate.1 = (f32[2,5376]{1,0:T(2,128)S(1)}, f32[2,5376]{1,0:T(2,128)S(1)}, f32[2,5376]{1,0:T(2,128)S(1)}, f32[2,5376]{1,0:T(2,128)S(1)}) custom-call(s32[3]{0:T(128)S(1)} %pad_add_fusion.refs_0_.idx, bf16[2,96,2304]{2,1,0:T(8,128)(2,1)S(1)} %copy-done.4, bf16[2,576]{1,0:T(2,128)(2,1)} %refs_2_.3, bf16[2,192]{1,0:T(2,128)(2,1)} %refs_3_.6, ...), custom_call_target="tpu_custom_call" | custom-call | flops 1 | bytes 1 | tf_op jit(solution)/shard_map/modulate/pallas_call | solution.py:71
  26.3 1.6 collective-permute-start.7
  27.8 4.7 %collective-permute-done.8.refs_6_.refs_10_.refs_11_ = bf16[96,2304]{1,0:T(8,128)(2,1)S(1)} collective-permute-done((bf16[96,2304]{1,0:T(8,128)(2,1)S(1)}, bf16[96,2304]{1,0:T(8,128)(2,1)S(1)}, u32[]{:S(2)}, u32[]{:S(2)}) %collective-permute-start.8) | collective-permute-done | bytes 442400 | tf_op jit(solution)/shard_map/ppermute | solution.py:608
  33.5 5.9 %collective-permute-done.7.whole.refs_5_.refs_6_.refs_10_ = bf16[96,4608]{1,0:T(8,128)(2,1)S(1)} collective-permute-done((bf16[96,4608]{1,0:T(8,128)(2,1)S(1)}, bf16[96,4608]{1,0:T(8,128)(2,1)S(1)}, u32[]{:S(2)}, u32[]{:S(2)}) %collective-permute-start.7) | collective-permute-done | bytes 884768 | tf_op jit(solution)/shard_map/ppermute | solution.py:608
  41.5 4.3 %attention_forward.2 = (bf16[256,1152]{1,0:T(8,128)(2,1)}, f32[6,256,256]{2,1,0:T(8,128)}, bf16[256,384]{1,0:T(8,128)(2,1)}, f32[256,384]{1,0:T(8,128)}, f32[256,384]{1,0:T(8,128)S(1)}) custom-call(s32[3]{0:T(128)S(1)} %pad_add_fusion.refs_0_.idx, bf16[256,384]{1,0:T(8,128)(2,1)S(1)} %bitcast.7, f32[2,5376]{1,0:T(2,128)S(1)} %add_add_fusion.refs_2_, ...), custom_call_target="tpu_custom_call" | custom-call | flops 1 | bytes 1 | tf_op jit(solution)/shard_map/attention_forward/pallas_call | solution.py:71
  46.2 2.2 %collective-permute-done.11.refs_6_.refs_7_.refs_11_ = bf16[96,2304]{1,0:T(8,128)(2,1)S(1)} collective-permute-done((bf16[96,2304]{1,0:T(8,128)(2,1)S(1)}, bf16[96,2304]{1,0:T(8,128)(2,1)S(1)}, u32[]{:S(2)}, u32[]{:S(2)}) %collective-permute-start.11) | collective-permute-done | bytes 442400 | tf_op jit(solution)/shard_map/ppermute | solution.py:608
  48.4 4.8 %mlp_forward.1 = (bf16[256,1536]{1,0:T(8,128)(2,1)}, f32[256,1536]{1,0:T(8,128)}, f32[256,384]{1,0:T(8,128)}, f32[256,384]{1,0:T(8,128)S(1)}) custom-call(s32[3]{0:T(128)S(1)} %pad_add_fusion.refs_0_.idx, f32[256,384]{1,0:T(8,128)S(1)} %get-tuple-element.115.refs_1_, f32[2,5376]{1,0:T(2,128)S(1)} %add_add_fusion.refs_2_, bf16[2,96,1536]{2,1,0:T(8,128)(2,1)S(1)} %copy-done.1, ...), custom_call_target="tpu_custom_call" | custom-call | flops 1 | bytes 1 | tf_op jit(solution)/shard_map/mlp_forward/pallas_call | solution.py:71
  53.2 3.0 %attention_forward.3 = (bf16[256,1152]{1,0:T(8,128)(2,1)S(1)}, f32[6,256,256]{2,1,0:T(8,128)S(1)}, bf16[256,384]{1,0:T(8,128)(2,1)S(1)}, f32[256,384]{1,0:T(8,128)S(1)}, f32[256,384]{1,0:T(8,128)S(1)}) custom-call(s32[3]{0:T(128)S(1)} %pad_add_fusion.refs_0_.idx, f32[256,384]{1,0:T(8,128)S(1)} %get-tuple-element.116.refs_1_, ...), custom_call_target="tpu_custom_call" | custom-call | flops 1 | bytes 1 | tf_op jit(solution)/shard_map/attention_forward/pallas_call | solution.py:71
  56.3 7.1 %mlp_both.1 = (bf16[256,384]{1,0:T(8,128)(2,1)}, f32[256,384]{1,0:T(8,128)S(1)}, f32[1,3072]{1,0:T(1,128)S(1)}, bf16[4,96,1536]{2,1,0:T(8,128)(2,1)S(1)}, bf16[4,96,1536]{2,1,0:T(8,128)(2,1)S(1)}) custom-call(s32[3]{0:T(128)S(1)} %pad_add_fusion.refs_0_.idx, f32[256,384]{1,0:T(8,128)S(1)} %get-tuple-element.119.refs_1_, f32[2,5376]{1,0:T(2,128)S(1)} %add_add_fusion.refs_2_, ...), custom_call_target="tpu_custom_call" | custom-call | flops 1 | bytes 1 | tf_op jit(solution)/shard_map/mlp_both/pallas_call | solution.py:71
  64.0 5.9 %attention_backward.2 = (f32[256,384]{1,0:T(8,128)S(1)}, f32[1,2304]{1,0:T(1,128)S(1)}, bf16[4,96,768]{2,1,0:T(8,128)(2,1)S(1)}, bf16[4,96,768]{2,1,0:T(8,128)(2,1)S(1)}) custom-call(s32[3]{0:T(128)S(1)} %pad_add_fusion.refs_0_.idx, f32[256,384]{1,0:T(8,128)S(1)} %get-tuple-element.116.refs_1_, f32[2,5376]{1,0:T(2,128)S(1)} %add_add_fusion.refs_2_, ...), custom_call_target="tpu_custom_call" | custom-call | flops 1 | bytes 1 | tf_op jit(solution)/shard_map/attention_backward/pallas_call | solution.py:71
  69.9 2.0 %collective-permute-done.14.refs_2_ = bf16[4,96,768]{2,1,0:T(8,128)(2,1)S(1)} collective-permute-done((bf16[4,96,768]{2,1,0:T(8,128)(2,1)S(1)}, bf16[4,96,768]{2,1,0:T(8,128)(2,1)S(1)}, u32[]{:S(2)}, u32[]{:S(2)}) %collective-permute-start.14) | collective-permute-done | bytes 589856 | tf_op jit(solution)/shard_map/ppermute | solution.py:608
  73.6 4.6 %mlp_backward.1 = (f32[256,384]{1,0:T(8,128)S(1)}, f32[1,3072]{1,0:T(1,128)S(1)}, bf16[4,96,1536]{2,1,0:T(8,128)(2,1)S(1)}, bf16[4,96,1536]{2,1,0:T(8,128)(2,1)S(1)}) custom-call(s32[3]{0:T(128)S(1)} %pad_add_fusion.refs_0_.idx, f32[256,384]{1,0:T(8,128)S(1)} %get-tuple-element.115.refs_1_, f32[2,5376]{1,0:T(2,128)S(1)} %add_add_fusion.refs_2_, ...), custom_call_target="tpu_custom_call" | custom-call | flops 1 | bytes 1 | tf_op jit(solution)/shard_map/mlp_backward/pallas_call | solution.py:71
  81.6 6.8 %attention_backward.3 = (f32[256,384]{1,0:T(8,128)}, f32[1,2304]{1,0:T(1,128)S(1)}, bf16[4,96,768]{2,1,0:T(8,128)(2,1)S(1)}, bf16[4,96,768]{2,1,0:T(8,128)(2,1)S(1)}) custom-call(s32[3]{0:T(128)S(1)} %pad_add_fusion.refs_0_.idx, bf16[256,384]{1,0:T(8,128)(2,1)S(1)} %bitcast.8, f32[2,5376]{1,0:T(2,128)S(1)} %add_add_fusion.refs_2_, ...), custom_call_target="tpu_custom_call" | custom-call | flops 1 | bytes 1 | tf_op jit(solution)/shard_map/attention_backward/pallas_call | solution.py:71
  95.1 7.9 %collective-permute-done.19.other = bf16[2,96,1536]{2,1,0:T(8,128)(2,1)S(1)} collective-permute-done((bf16[2,96,1536]{2,1,0:T(8,128)(2,1)S(1)}, bf16[2,96,1536]{2,1,0:T(8,128)(2,1)S(1)}, u32[]{:S(2)}, u32[]{:S(2)}) %collective-permute-start.19) | collective-permute-done | bytes 589856 | tf_op jit(solution)/shard_map/ppermute | solution.py:608
  103.2 1.8 %collective-permute-done.20.refs_2_ = bf16[96,2304]{1,0:T(8,128)(2,1)S(1)} collective-permute-done((bf16[96,2304]{1,0:T(8,128)(2,1)S(1)}, bf16[96,2304]{1,0:T(8,128)(2,1)S(1)}, u32[]{:S(2)}, u32[]{:S(2)}) %collective-permute-start.20) | collective-permute-done | bytes 442400 | tf_op jit(solution)/shard_map/ppermute | solution.py:608
  107.2 1.6 collective-permute-start.24
  109.5 1.6 collective-permute-start.22
  111.1 2.5 %collective-permute-done.22.second = bf16[1,11136]{1,0:T(2,128)(2,1)S(1)} collective-permute-done((bf16[1,11136]{1,0:T(2,128)(2,1)S(1)}, bf16[1,11136]{1,0:T(2,128)(2,1)S(1)}, u32[]{:S(2)}, u32[]{:S(2)}) %collective-permute-start.22) | collective-permute-done | bytes 22304 | tf_op jit(solution)/shard_map/ppermute | solution.py:608
  116.7 2.6 %collective-permute-start.32 = (bf16[48,2304]{1,0:T(8,128)(2,1)S(1)}, bf16[48,2304]{1,0:T(8,128)(2,1)S(1)}, u32[]{:S(2)}, u32[]{:S(2)}) collective-permute-start(bf16[48,2304]{1,0:T(8,128)(2,1)S(1)} %add.72.refs_0_), channel_id=1, source_target_pairs={{0,4},{1,5},{2,6},{3,7},{4,0},{5,1},{6,2},{7,3},{8,12},{9,13},{10,... | collective-permute-start | bytes 663560 | tf_op jit(solution)/shard_map/ppermute | solution.py:608
  120.7 2.6 %collective-permute-done.26.second = bf16[2,11136]{1,0:T(2,128)(2,1)S(1)} collective-permute-done((bf16[2,11136]{1,0:T(2,128)(2,1)S(1)}, bf16[2,11136]{1,0:T(2,128)(2,1)S(1)}, u32[]{:S(2)}, u32[]{:S(2)}) %collective-permute-start.26) | collective-permute-done | bytes 44576 | tf_op jit(solution)/shard_map/ppermute | solution.py:608
  123.3 2.1 %group.1 = (f32[2,384]{1,0:T(2,128)S(1)}, f32[2,384]{1,0:T(2,128)S(1)}, bf16[6,4992]{1,0:T(8,128)(2,1)S(1)}) custom-call(s32[3]{0:T(128)S(1)} %pad_add_fusion.refs_0_.idx, bf16[2,96,2304]{2,1,0:T(8,128)(2,1)S(1)} %copy-done.4, bf16[2,11136]{1,0:T(2,128)(2,1)S(1)} %stack.18.first, bf16[2,11136]{1,0:T(2,128)(2,1)S(1)} %collective-permute-done.26.second), custom_call_target="tpu_custom_call" | custom-call | flops 1 | bytes 1 | tf_op jit(solution)/shard_map/group/pallas_call | solution.py:71
  126.8 3.1 %collective-permute-done.31.second = bf16[6,4992]{1,0:T(8,128)(2,1)S(1)} collective-permute-done((bf16[6,4992]{1,0:T(8,128)(2,1)S(1)}, bf16[6,4992]{1,0:T(8,128)(2,1)S(1)}, u32[]{:S(2)}, u32[]{:S(2)}) %collective-permute-start.31) | collective-permute-done | bytes 59936 | tf_op jit(solution)/shard_map/ppermute | solution.py:608
  130.0 2.3 %collective-permute-start.40 = (bf16[10,4992]{1,0:T(8,128)(2,1)S(1)}, bf16[10,4992]{1,0:T(8,128)(2,1)S(1)}, u32[]{:S(2)}, u32[]{:S(2)}) collective-permute-start(bf16[10,4992]{1,0:T(8,128)(2,1)S(1)} %stack.19.refs_1_), channel_id=1, source_target_pairs={{0,4},{1,5},{2,6},{3,7},{4,0},{5,1},{6,2},{7,3},{8,12},{9,13},{10,... | collective-permute-start | bytes 299528 | tf_op jit(solution)/shard_map/ppermute | solution.py:608
  133.7 2.2 %collective-permute-done.27 = f32[2,384]{1,0:T(2,128)S(1)} collective-permute-done((f32[2,384]{1,0:T(2,128)S(1)}, f32[2,384]{1,0:T(2,128)S(1)}, u32[]{:S(2)}, u32[]{:S(2)}) %collective-permute-start.27) | collective-permute-done | bytes 3104 | tf_op jit(solution)/shard_map/ppermute | solution.py:608
  135.9 1.6 %collective-permute-start.28 = (f32[1,384]{1,0:T(1,128)S(1)}, f32[1,384]{1,0:T(1,128)S(1)}, u32[]{:S(2)}, u32[]{:S(2)}) collective-permute-start(f32[1,384]{1,0:T(1,128)S(1)} %slice.97), channel_id=1, source_target_pairs={{0,8},{1,17},{2,10},{3,19},{4,12},{5,21},{6,14},{7,23},{8,0},{9,25... | collective-permute-start | bytes 4616 | tf_op jit(solution)/shard_map/ppermute | solution.py:608
  139.0 2.4 %collective-permute-done.40.refs_2_ = bf16[10,4992]{1,0:T(8,128)(2,1)S(1)} collective-permute-done((bf16[10,4992]{1,0:T(8,128)(2,1)S(1)}, bf16[10,4992]{1,0:T(8,128)(2,1)S(1)}, u32[]{:S(2)}, u32[]{:S(2)}) %collective-permute-start.40) | collective-permute-done | bytes 99872 | tf_op jit(solution)/shard_map/ppermute | solution.py:608
  145.2 2.2 %ada_grad.1 = (f32[2,96,2304]{2,1,0:T(8,128)}, f32[1,10752]{1,0:T(1,128)S(1)}) custom-call(s32[3]{0:T(128)S(1)} %pad_add_fusion.refs_0_.idx, bf16[10,4992]{1,0:T(8,128)(2,1)S(1)} %stack.19.refs_1_, bf16[10,4992]{1,0:T(8,128)(2,1)S(1)} %collective-permute-done.40.refs_2_, bf16[10,4992]{1,0:T(8,128)(2,1)S(1)} %collective-permute-done.41.refs_3_, ...), custom_call_target="tpu_custom_call" | custom-call | flops 1 | bytes 1 | tf_op jit(solution)/shard_map/ada_grad/pallas_call | solution.py:71
  147.4 4.2 %collective-permute-done.43.refs_1_ = bf16[96,768]{1,0:T(8,128)(2,1)S(1)} collective-permute-done((bf16[96,768]{1,0:T(8,128)(2,1)S(1)}, bf16[96,768]{1,0:T(8,128)(2,1)S(1)}, u32[]{:S(2)}, u32[]{:S(2)}) %collective-permute-start.43) | collective-permute-done | bytes 147488 | tf_op jit(solution)/shard_map/ppermute | solution.py:608
  155.6 2.6 %finish.1 = (f32[2,96,1152]{2,1,0:T(8,128)}, f32[2,96,384]{2,1,0:T(8,128)}, f32[2,96,1536]{2,1,0:T(8,128)}, f32[2,384,384]{2,1,0:T(8,128)}) custom-call(s32[3]{0:T(128)S(1)} %pad_add_fusion.refs_0_.idx, bf16[48,2304]{1,0:T(8,128)(2,1)S(1)} %add.76.refs_1_, bf16[48,2304]{1,0:T(8,128)(2,1)S(1)} %collective-permute-done.33.refs_2_, ...), custom_call_target="tpu_custom_call" | custom-call | flops 1 | bytes 1 | tf_op jit(solution)/shard_map/finish/pallas_call | solution.py:71
  (148 shorter events, 45.7 us)
Async XLA Ops:
  2.0 18.2 %collective-permute-start.3 = (bf16[96,4608]{1,0:T(8,128)(2,1)S(1)}, bf16[96,4608]{1,0:T(8,128)(2,1)S(1)}, u32[]{:S(2)}, u32[]{:S(2)}) collective-permute-start(bf16[96,4608]{1,0:T(8,128)(2,1)S(1)} %pack.2), channel_id=1, source_target_pairs={{0,8},{1,17},{2,10},{3,19},{4,12},{5,21},{6,14},{7,23},{8,0},{9,25... | collective-permute-start | bytes 2654216 | tf_op jit(solution)/shard_map/ppermute | solution.py:608
  5.0 11.1 %collective-permute-start = (bf16[1,384]{1,0:T(2,128)(2,1)S(1)}, bf16[1,384]{1,0:T(2,128)(2,1)S(1)}, u32[]{:S(2)}, u32[]{:S(2)}) collective-permute-start(bf16[1,384]{1,0:T(2,128)(2,1)S(1)} %copy-done.14), channel_id=1, source_target_pairs={{0,8},{1,9},{2,10},{3,11},{4,12},{5,13},{6,14},{7,15},{8,0},{9,1},... | collective-permute-start | bytes 2312 | tf_op jit(solution)/shard_map/ppermute | solution.py:608
  5.1 11.0 %collective-permute-start.1 = (bf16[1,384]{1,0:T(2,128)(2,1)S(1)}, bf16[1,384]{1,0:T(2,128)(2,1)S(1)}, u32[]{:S(2)}, u32[]{:S(2)}) collective-permute-start(bf16[1,384]{1,0:T(2,128)(2,1)S(1)} %copy-done.14), channel_id=1, source_target_pairs={{0,16},{1,17},{2,18},{3,19},{4,20},{5,21},{6,22},{7,23},{8,24},{9,... | collective-permute-start | bytes 2312 | tf_op jit(solution)/shard_map/ppermute | solution.py:608
  7.1 10.5 %collective-permute-start.2 = (bf16[1,384]{1,0:T(2,128)(2,1)S(1)}, bf16[1,384]{1,0:T(2,128)(2,1)S(1)}, u32[]{:S(2)}, u32[]{:S(2)}) collective-permute-start(bf16[1,384]{1,0:T(2,128)(2,1)S(1)} %copy-done.14), channel_id=1, source_target_pairs={{0,24},{1,25},{2,26},{3,27},{4,28},{5,29},{6,30},{7,31},{8,16},{9,... | collective-permute-start | bytes 2312 | tf_op jit(solution)/shard_map/ppermute | solution.py:608
  20.8 11.7 %collective-permute-start.8 = (bf16[96,2304]{1,0:T(8,128)(2,1)S(1)}, bf16[96,2304]{1,0:T(8,128)(2,1)S(1)}, u32[]{:S(2)}, u32[]{:S(2)}) collective-permute-start(bf16[96,2304]{1,0:T(8,128)(2,1)S(1)} %half.2), channel_id=1, source_target_pairs={{0,16},{1,9},{2,18},{3,11},{4,20},{5,13},{6,22},{7,15},{8,24},{9,1... | collective-permute-start | bytes 1327112 | tf_op jit(solution)/shard_map/ppermute | solution.py:608
  21.5 6.4 %collective-permute-start.4 = (f32[2,5376]{1,0:T(2,128)S(1)}, f32[2,5376]{1,0:T(2,128)S(1)}, u32[]{:S(2)}, u32[]{:S(2)}) collective-permute-start(f32[2,5376]{1,0:T(2,128)S(1)} %get-tuple-element.107), channel_id=1, source_target_pairs={{0,8},{1,9},{2,10},{3,11},{4,12},{5,13},{6,14},{7,15},{8,0},{9,1},... | collective-permute-start | bytes 129032 | tf_op jit(solution)/shard_map/ppermute | solution.py:608
  23.0 10.5 %collective-permute-start.5 = (f32[2,5376]{1,0:T(2,128)S(1)}, f32[2,5376]{1,0:T(2,128)S(1)}, u32[]{:S(2)}, u32[]{:S(2)}) collective-permute-start(f32[2,5376]{1,0:T(2,128)S(1)} %get-tuple-element.109), channel_id=1, source_target_pairs={{0,16},{1,17},{2,18},{3,19},{4,20},{5,21},{6,22},{7,23},{8,24},{9,... | collective-permute-start | bytes 129032 | tf_op jit(solution)/shard_map/ppermute | solution.py:608
  24.4 9.0 %collective-permute-start.6 = (f32[2,5376]{1,0:T(2,128)S(1)}, f32[2,5376]{1,0:T(2,128)S(1)}, u32[]{:S(2)}, u32[]{:S(2)}) collective-permute-start(f32[2,5376]{1,0:T(2,128)S(1)} %get-tuple-element.111), channel_id=1, source_target_pairs={{0,24},{1,25},{2,26},{3,27},{4,28},{5,29},{6,30},{7,31},{8,16},{9,... | collective-permute-start | bytes 129032 | tf_op jit(solution)/shard_map/ppermute | solution.py:608
  26.3 13.1 %collective-permute-start.7 = (bf16[96,4608]{1,0:T(8,128)(2,1)S(1)}, bf16[96,4608]{1,0:T(8,128)(2,1)S(1)}, u32[]{:S(2)}, u32[]{:S(2)}) collective-permute-start(bf16[96,4608]{1,0:T(8,128)(2,1)S(1)} %pack.3), channel_id=1, source_target_pairs={{0,8},{1,17},{2,10},{3,19},{4,12},{5,21},{6,14},{7,23},{8,0},{9,25... | collective-permute-start | bytes 2654216 | tf_op jit(solution)/shard_map/ppermute | solution.py:608
  27.8 13.7 %collective-permute-start.9 = (bf16[96,4608]{1,0:T(8,128)(2,1)S(1)}, bf16[96,4608]{1,0:T(8,128)(2,1)S(1)}, u32[]{:S(2)}, u32[]{:S(2)}) collective-permute-start(bf16[96,4608]{1,0:T(8,128)(2,1)S(1)} %collective-permute-done.3.whole.refs_5_.refs_9_.refs_10_), channel_id=1, source_target_pairs={{0,1},{1,0},{2,3},{3,2},{4,5},{5,4},{6,7},{7,6},{8,9},{9,8},{10,11... | collective-permute-start | bytes 2654216 | tf_op jit(solution)/shard_map/ppermute | solution.py:608
  32.5 9.0 %collective-permute-start.10 = (bf16[96,2304]{1,0:T(8,128)(2,1)S(1)}, bf16[96,2304]{1,0:T(8,128)(2,1)S(1)}, u32[]{:S(2)}, u32[]{:S(2)}) collective-permute-start(bf16[96,2304]{1,0:T(8,128)(2,1)S(1)} %collective-permute-done.8.refs_6_.refs_10_.refs_11_), channel_id=1, source_target_pairs={{0,1},{1,0},{2,3},{3,2},{4,5},{5,4},{6,7},{7,6},{8,9},{9,8},{10,11... | collective-permute-start | bytes 1327112 | tf_op jit(solution)/shard_map/ppermute | solution.py:608
  40.0 8.4 %collective-permute-start.11 = (bf16[96,2304]{1,0:T(8,128)(2,1)S(1)}, bf16[96,2304]{1,0:T(8,128)(2,1)S(1)}, u32[]{:S(2)}, u32[]{:S(2)}) collective-permute-start(bf16[96,2304]{1,0:T(8,128)(2,1)S(1)} %half.3), channel_id=1, source_target_pairs={{0,16},{1,9},{2,18},{3,11},{4,20},{5,13},{6,22},{7,15},{8,24},{9,1... | collective-permute-start | bytes 1327112 | tf_op jit(solution)/shard_map/ppermute | solution.py:608
  45.8 7.4 %collective-permute-start.12 = (bf16[96,4608]{1,0:T(8,128)(2,1)S(1)}, bf16[96,4608]{1,0:T(8,128)(2,1)S(1)}, u32[]{:S(2)}, u32[]{:S(2)}) collective-permute-start(bf16[96,4608]{1,0:T(8,128)(2,1)S(1)} %collective-permute-done.7.whole.refs_5_.refs_6_.refs_10_), channel_id=1, source_target_pairs={{0,1},{1,0},{2,3},{3,2},{4,5},{5,4},{6,7},{7,6},{8,9},{9,8},{10,11... | collective-permute-start | bytes 2654216 | tf_op jit(solution)/shard_map/ppermute | solution.py:608
  63.4 8.5 %collective-permute-start.15 = (bf16[4,96,1536]{2,1,0:T(8,128)(2,1)S(1)}, bf16[4,96,1536]{2,1,0:T(8,128)(2,1)S(1)}, u32[]{:S(2)}, u32[]{:S(2)}) collective-permute-start(bf16[4,96,1536]{2,1,0:T(8,128)(2,1)S(1)} %get-tuple-element.131), channel_id=1, source_target_pairs={{0,1},{1,0},{2,3},{3,2},{4,5},{5,4},{6,7},{7,6},{8,9},{9,8},{10,11... | collective-permute-start | bytes 3538952 | tf_op jit(solution)/shard_map/ppermute | solution.py:608
  78.5 13.0 %collective-permute-start.17 = (bf16[2,96,2304]{2,1,0:T(8,128)(2,1)S(1)}, bf16[2,96,2304]{2,1,0:T(8,128)(2,1)S(1)}, u32[]{:S(2)}, u32[]{:S(2)}) collective-permute-start(bf16[2,96,2304]{2,1,0:T(8,128)(2,1)S(1)} %get-tuple-element.154), channel_id=1, source_target_pairs={{0,8},{1,17},{2,10},{3,19},{4,12},{5,21},{6,14},{7,23},{8,0},{9,25... | collective-permute-start | bytes 2654216 | tf_op jit(solution)/shard_map/ppermute | solution.py:608
  88.6 14.4 %collective-permute-start.19 = (bf16[2,96,1536]{2,1,0:T(8,128)(2,1)S(1)}, bf16[2,96,1536]{2,1,0:T(8,128)(2,1)S(1)}, u32[]{:S(2)}, u32[]{:S(2)}) collective-permute-start(bf16[2,96,1536]{2,1,0:T(8,128)(2,1)S(1)} %get-tuple-element.160), channel_id=1, source_target_pairs={{0,8},{1,17},{2,10},{3,19},{4,12},{5,21},{6,14},{7,23},{8,0},{9,25... | collective-permute-start | bytes 1769480 | tf_op jit(solution)/shard_map/ppermute | solution.py:608
  91.8 13.2 %collective-permute-start.20 = (bf16[96,2304]{1,0:T(8,128)(2,1)S(1)}, bf16[96,2304]{1,0:T(8,128)(2,1)S(1)}, u32[]{:S(2)}, u32[]{:S(2)}) collective-permute-start(bf16[96,2304]{1,0:T(8,128)(2,1)S(1)} %get-tuple-element.164), channel_id=1, source_target_pairs={{0,16},{1,9},{2,18},{3,11},{4,20},{5,13},{6,22},{7,15},{8,24},{9,1... | collective-permute-start | bytes 1327112 | tf_op jit(solution)/shard_map/ppermute | solution.py:608
  93.5 15.3 %collective-permute-start.21 = (bf16[2,96,768]{2,1,0:T(8,128)(2,1)S(1)}, bf16[2,96,768]{2,1,0:T(8,128)(2,1)S(1)}, u32[]{:S(2)}, u32[]{:S(2)}) collective-permute-start(bf16[2,96,768]{2,1,0:T(8,128)(2,1)S(1)} %get-tuple-element.167), channel_id=1, source_target_pairs={{0,8},{1,17},{2,10},{3,19},{4,12},{5,21},{6,14},{7,23},{8,0},{9,25... | collective-permute-start | bytes 884744 | tf_op jit(solution)/shard_map/ppermute | solution.py:608
  105.7 8.0 %collective-permute-start.23 = (bf16[96,1536]{1,0:T(8,128)(2,1)S(1)}, bf16[96,1536]{1,0:T(8,128)(2,1)S(1)}, u32[]{:S(2)}, u32[]{:S(2)}) collective-permute-start(bf16[96,1536]{1,0:T(8,128)(2,1)S(1)} %get-tuple-element.171), channel_id=1, source_target_pairs={{0,16},{1,9},{2,18},{3,11},{4,20},{5,13},{6,22},{7,15},{8,24},{9,1... | collective-permute-start | bytes 884744 | tf_op jit(solution)/shard_map/ppermute | solution.py:608
  107.2 8.1 %collective-permute-start.24 = (bf16[48,2304]{1,0:T(8,128)(2,1)S(1)}, bf16[48,2304]{1,0:T(8,128)(2,1)S(1)}, u32[]{:S(2)}, u32[]{:S(2)}) collective-permute-start(bf16[48,2304]{1,0:T(8,128)(2,1)S(1)} %get-tuple-element.174), channel_id=1, source_target_pairs={{0,2},{1,3},{2,0},{3,1},{4,6},{5,7},{6,4},{7,5},{8,10},{9,11},{10,... | collective-permute-start | bytes 663560 | tf_op jit(solution)/shard_map/ppermute | solution.py:608
  108.9 6.5 %collective-permute-start.25 = (bf16[96,768]{1,0:T(8,128)(2,1)S(1)}, bf16[96,768]{1,0:T(8,128)(2,1)S(1)}, u32[]{:S(2)}, u32[]{:S(2)}) collective-permute-start(bf16[96,768]{1,0:T(8,128)(2,1)S(1)} %get-tuple-element.176), channel_id=1, source_target_pairs={{0,16},{1,9},{2,18},{3,11},{4,20},{5,13},{6,22},{7,15},{8,24},{9,1... | collective-permute-start | bytes 442376 | tf_op jit(solution)/shard_map/ppermute | solution.py:608
  114.4 11.9 %collective-permute-start.29 = (bf16[48,1536]{1,0:T(8,128)(2,1)S(1)}, bf16[48,1536]{1,0:T(8,128)(2,1)S(1)}, u32[]{:S(2)}, u32[]{:S(2)}) collective-permute-start(bf16[48,1536]{1,0:T(8,128)(2,1)S(1)} %get-tuple-element.182), channel_id=1, source_target_pairs={{0,2},{1,3},{2,0},{3,1},{4,6},{5,7},{6,4},{7,5},{8,10},{9,11},{10,... | collective-permute-start | bytes 442376 | tf_op jit(solution)/shard_map/ppermute | solution.py:608
  115.4 11.3 %collective-permute-start.30 = (bf16[96,768]{1,0:T(8,128)(2,1)S(1)}, bf16[96,768]{1,0:T(8,128)(2,1)S(1)}, u32[]{:S(2)}, u32[]{:S(2)}) collective-permute-start(bf16[96,768]{1,0:T(8,128)(2,1)S(1)} %add.73.refs_0_), channel_id=1, source_target_pairs={{0,2},{1,3},{2,0},{3,1},{4,6},{5,7},{6,4},{7,5},{8,10},{9,11},{10,... | collective-permute-start | bytes 442376 | tf_op jit(solution)/shard_map/ppermute | solution.py:608
  116.7 20.8 %collective-permute-start.32 = (bf16[48,2304]{1,0:T(8,128)(2,1)S(1)}, bf16[48,2304]{1,0:T(8,128)(2,1)S(1)}, u32[]{:S(2)}, u32[]{:S(2)}) collective-permute-start(bf16[48,2304]{1,0:T(8,128)(2,1)S(1)} %add.72.refs_0_), channel_id=1, source_target_pairs={{0,4},{1,5},{2,6},{3,7},{4,0},{5,1},{6,2},{7,3},{8,12},{9,13},{10,... | collective-permute-start | bytes 663560 | tf_op jit(solution)/shard_map/ppermute | solution.py:608
  126.3 12.5 %collective-permute-start.36 = (bf16[48,1536]{1,0:T(8,128)(2,1)S(1)}, bf16[48,1536]{1,0:T(8,128)(2,1)S(1)}, u32[]{:S(2)}, u32[]{:S(2)}) collective-permute-start(bf16[48,1536]{1,0:T(8,128)(2,1)S(1)} %add.74.refs_0_), channel_id=1, source_target_pairs={{0,4},{1,5},{2,6},{3,7},{4,0},{5,1},{6,2},{7,3},{8,12},{9,13},{10,... | collective-permute-start | bytes 442376 | tf_op jit(solution)/shard_map/ppermute | solution.py:608
  130.0 11.5 %collective-permute-start.40 = (bf16[10,4992]{1,0:T(8,128)(2,1)S(1)}, bf16[10,4992]{1,0:T(8,128)(2,1)S(1)}, u32[]{:S(2)}, u32[]{:S(2)}) collective-permute-start(bf16[10,4992]{1,0:T(8,128)(2,1)S(1)} %stack.19.refs_1_), channel_id=1, source_target_pairs={{0,4},{1,5},{2,6},{3,7},{4,0},{5,1},{6,2},{7,3},{8,12},{9,13},{10,... | collective-permute-start | bytes 299528 | tf_op jit(solution)/shard_map/ppermute | solution.py:608
  138.9 5.8 %collective-permute-start.37 = (bf16[48,1536]{1,0:T(8,128)(2,1)S(1)}, bf16[48,1536]{1,0:T(8,128)(2,1)S(1)}, u32[]{:S(2)}, u32[]{:S(2)}) collective-permute-start(bf16[48,1536]{1,0:T(8,128)(2,1)S(1)} %add.77.refs_5_), channel_id=1, source_target_pairs={{0,2},{1,3},{2,0},{3,1},{4,6},{5,7},{6,4},{7,5},{8,10},{9,11},{10,... | collective-permute-start | bytes 442376 | tf_op jit(solution)/shard_map/ppermute | solution.py:608
  142.1 9.6 %collective-permute-start.43 = (bf16[96,768]{1,0:T(8,128)(2,1)S(1)}, bf16[96,768]{1,0:T(8,128)(2,1)S(1)}, u32[]{:S(2)}, u32[]{:S(2)}) collective-permute-start(bf16[96,768]{1,0:T(8,128)(2,1)S(1)} %add.75.refs_0_), channel_id=1, source_target_pairs={{0,4},{1,5},{2,6},{3,7},{4,0},{5,1},{6,2},{7,3},{8,12},{9,13},{10,... | collective-permute-start | bytes 442376 | tf_op jit(solution)/shard_map/ppermute | solution.py:608
  143.2 12.3 %collective-permute-start.38 = (bf16[48,1536]{1,0:T(8,128)(2,1)S(1)}, bf16[48,1536]{1,0:T(8,128)(2,1)S(1)}, u32[]{:S(2)}, u32[]{:S(2)}) collective-permute-start(bf16[48,1536]{1,0:T(8,128)(2,1)S(1)} %add.77.refs_5_), channel_id=1, source_target_pairs={{0,1},{1,0},{2,3},{3,2},{4,5},{5,4},{6,7},{7,6},{8,9},{9,8},{10,11... | collective-permute-start | bytes 442376 | tf_op jit(solution)/shard_map/ppermute | solution.py:608
  143.2 11.0 %collective-permute-start.33 = (bf16[48,2304]{1,0:T(8,128)(2,1)S(1)}, bf16[48,2304]{1,0:T(8,128)(2,1)S(1)}, u32[]{:S(2)}, u32[]{:S(2)}) collective-permute-start(bf16[48,2304]{1,0:T(8,128)(2,1)S(1)} %add.76.refs_1_), channel_id=1, source_target_pairs={{0,2},{1,3},{2,0},{3,1},{4,6},{5,7},{6,4},{7,5},{8,10},{9,11},{10,... | collective-permute-start | bytes 663560 | tf_op jit(solution)/shard_map/ppermute | solution.py:608
  144.6 10.8 %collective-permute-start.34 = (bf16[48,2304]{1,0:T(8,128)(2,1)S(1)}, bf16[48,2304]{1,0:T(8,128)(2,1)S(1)}, u32[]{:S(2)}, u32[]{:S(2)}) collective-permute-start(bf16[48,2304]{1,0:T(8,128)(2,1)S(1)} %add.76.refs_1_), channel_id=1, source_target_pairs={{0,1},{1,0},{2,3},{3,2},{4,5},{5,4},{6,7},{7,6},{8,9},{9,8},{10,11... | collective-permute-start | bytes 663560 | tf_op jit(solution)/shard_map/ppermute | solution.py:608
  144.7 10.8 %collective-permute-start.39 = (bf16[48,1536]{1,0:T(8,128)(2,1)S(1)}, bf16[48,1536]{1,0:T(8,128)(2,1)S(1)}, u32[]{:S(2)}, u32[]{:S(2)}) collective-permute-start(bf16[48,1536]{1,0:T(8,128)(2,1)S(1)} %collective-permute-done.37.refs_6_), channel_id=1, source_target_pairs={{0,1},{1,0},{2,3},{3,2},{4,5},{5,4},{6,7},{7,6},{8,9},{9,8},{10,11... | collective-permute-start | bytes 442376 | tf_op jit(solution)/shard_map/ppermute | solution.py:608
  (29 other events, 156.5 us)

commit v6 on v5

--- a/solution.py
+++ b/solution.py
@@ -670,7 +670,6 @@
     for own in near[1:]:
         parts.append(near_half(own, mod_all))
     near = [near_second(own, part) for own, part in zip(near, parts)]
-    mod_all = after(mod_all, *parts[1:])
     pieces = {0: (near[0], far_of(near[0]))}
 
     big = seq * width
@@ -705,6 +704,8 @@
             [w_qkv_all, qkv_sems], flops=10 * big * width,
         )
         pair, offset = pieces[layer], 2 * width
+        if layer == 0:
+            middle = after(middle, *parts[1:])
         entry = dict(stream=stream, qkv=qkv, probs=probs, attended=attended, branch=branch,
                      middle=middle)
         if layer + 1 < layers:

time: 158 us -> 158 us (level)
  no operation moved by 1% of the time
where the time goes in v6:
time: 158 us
  waiting for transfers between devices  56.5 us (36%)
  Pallas kernels  53.1 us (34%)
  starting transfers between devices  42.5 us (27%)
  other arithmetic  3.39 us (2%)
  local copies, waits for them, and re-layouts  1.58 us (1%)
    ppermute x45, waiting for transfers between devices, exchange(): return lax.ppermute(array, ('shard', 'rep'), moves)  56.5 us
    pallas_call x32, Pallas kernels, run(): pl.pallas_call(body, out_shape=[pltpu.HBM(shape, dtype) if kind in 'hk' e...  53.1 us
    ppermute x45, starting transfers between devices, exchange(): return lax.ppermute(array, ('shard', 'rep'), moves)  42.5 us
  transfers between devices with their start and end apart: 45, of which 20 were waited for; matrix products, arithmetic and copies ran while one was open for 2% of the time, Pallas kernels for 21%

profile of v6, /device:TPU:0, one launch (start us, length us, event | category | flops | bytes accessed | tf_op | source)
XLA Modules:
  0.0 158.2 jit_solution(13690756987010376924)
XLA Ops:
  2.0 3.0 %collective-permute-start.3 = (bf16[96,4608]{1,0:T(8,128)(2,1)S(1)}, bf16[96,4608]{1,0:T(8,128)(2,1)S(1)}, u32[]{:S(2)}, u32[]{:S(2)}) collective-permute-start(bf16[96,4608]{1,0:T(8,128)(2,1)S(1)} %pack.2), channel_id=1, source_target_pairs={{0,8},{1,17},{2,10},{3,19},{4,12},{5,21},{6,14},{7,23},{8,0},{9,25... | collective-permute-start | bytes 2654216 | tf_op jit(solution)/shard_map/ppermute | solution.py:608
  5.1 2.0 %collective-permute-start.1 = (bf16[1,384]{1,0:T(2,128)(2,1)S(1)}, bf16[1,384]{1,0:T(2,128)(2,1)S(1)}, u32[]{:S(2)}, u32[]{:S(2)}) collective-permute-start(bf16[1,384]{1,0:T(2,128)(2,1)S(1)} %copy-done.14), channel_id=1, source_target_pairs={{0,16},{1,17},{2,18},{3,19},{4,20},{5,21},{6,22},{7,23},{8,24},{9,... | collective-permute-start | bytes 2312 | tf_op jit(solution)/shard_map/ppermute | solution.py:608
  8.6 7.5 %collective-permute-done.refs_8_ = bf16[1,384]{1,0:T(2,128)(2,1)S(1)} collective-permute-done((bf16[1,384]{1,0:T(2,128)(2,1)S(1)}, bf16[1,384]{1,0:T(2,128)(2,1)S(1)}, u32[]{:S(2)}, u32[]{:S(2)}) %collective-permute-start) | collective-permute-done | bytes 800 | tf_op jit(solution)/shard_map/ppermute | solution.py:608
  17.6 2.6 %modulate.1 = (f32[2,5376]{1,0:T(2,128)S(1)}, f32[2,5376]{1,0:T(2,128)S(1)}, f32[2,5376]{1,0:T(2,128)S(1)}, f32[2,5376]{1,0:T(2,128)S(1)}) custom-call(s32[3]{0:T(128)S(1)} %pad_add_fusion.refs_0_.idx, bf16[2,96,2304]{2,1,0:T(8,128)(2,1)S(1)} %copy-done.4, bf16[2,576]{1,0:T(2,128)(2,1)} %refs_2_.3, bf16[2,192]{1,0:T(2,128)(2,1)} %refs_3_.6, ...), custom_call_target="tpu_custom_call" | custom-call | flops 1 | bytes 1 | tf_op jit(solution)/shard_map/modulate/pallas_call | solution.py:71
  26.3 1.6 collective-permute-start.10
  27.8 4.7 %collective-permute-done.7.refs_6_.refs_10_.refs_11_ = bf16[96,2304]{1,0:T(8,128)(2,1)S(1)} collective-permute-done((bf16[96,2304]{1,0:T(8,128)(2,1)S(1)}, bf16[96,2304]{1,0:T(8,128)(2,1)S(1)}, u32[]{:S(2)}, u32[]{:S(2)}) %collective-permute-start.7) | collective-permute-done | bytes 442400 | tf_op jit(solution)/shard_map/ppermute | solution.py:608
  33.5 5.9 %collective-permute-done.10.whole.refs_5_.refs_6_.refs_10_ = bf16[96,4608]{1,0:T(8,128)(2,1)S(1)} collective-permute-done((bf16[96,4608]{1,0:T(8,128)(2,1)S(1)}, bf16[96,4608]{1,0:T(8,128)(2,1)S(1)}, u32[]{:S(2)}, u32[]{:S(2)}) %collective-permute-start.10) | collective-permute-done | bytes 884768 | tf_op jit(solution)/shard_map/ppermute | solution.py:608
  41.5 4.3 %attention_forward.2 = (bf16[256,1152]{1,0:T(8,128)(2,1)}, f32[6,256,256]{2,1,0:T(8,128)}, bf16[256,384]{1,0:T(8,128)(2,1)}, f32[256,384]{1,0:T(8,128)}, f32[256,384]{1,0:T(8,128)S(1)}) custom-call(s32[3]{0:T(128)S(1)} %pad_add_fusion.refs_0_.idx, bf16[256,384]{1,0:T(8,128)(2,1)S(1)} %bitcast.7, f32[2,5376]{1,0:T(2,128)S(1)} %add_add_fusion.refs_2_, ...), custom_call_target="tpu_custom_call" | custom-call | flops 1 | bytes 1 | tf_op jit(solution)/shard_map/attention_forward/pallas_call | solution.py:71
  46.2 2.2 %collective-permute-done.11.refs_6_.refs_7_.refs_11_ = bf16[96,2304]{1,0:T(8,128)(2,1)S(1)} collective-permute-done((bf16[96,2304]{1,0:T(8,128)(2,1)S(1)}, bf16[96,2304]{1,0:T(8,128)(2,1)S(1)}, u32[]{:S(2)}, u32[]{:S(2)}) %collective-permute-start.11) | collective-permute-done | bytes 442400 | tf_op jit(solution)/shard_map/ppermute | solution.py:608
  48.4 4.8 %mlp_forward.1 = (bf16[256,1536]{1,0:T(8,128)(2,1)}, f32[256,1536]{1,0:T(8,128)}, f32[256,384]{1,0:T(8,128)}, f32[256,384]{1,0:T(8,128)S(1)}) custom-call(s32[3]{0:T(128)S(1)} %pad_add_fusion.refs_0_.idx, f32[256,384]{1,0:T(8,128)S(1)} %get-tuple-element.115.refs_1_, f32[2,5376]{1,0:T(2,128)S(1)} %add_add_fusion.refs_2_, bf16[2,96,1536]{2,1,0:T(8,128)(2,1)S(1)} %copy-done.1, ...), custom_call_target="tpu_custom_call" | custom-call | flops 1 | bytes 1 | tf_op jit(solution)/shard_map/mlp_forward/pallas_call | solution.py:71
  53.2 3.0 %attention_forward.3 = (bf16[256,1152]{1,0:T(8,128)(2,1)S(1)}, f32[6,256,256]{2,1,0:T(8,128)S(1)}, bf16[256,384]{1,0:T(8,128)(2,1)S(1)}, f32[256,384]{1,0:T(8,128)S(1)}, f32[256,384]{1,0:T(8,128)S(1)}) custom-call(s32[3]{0:T(128)S(1)} %pad_add_fusion.refs_0_.idx, f32[256,384]{1,0:T(8,128)S(1)} %get-tuple-element.116.refs_1_, ...), custom_call_target="tpu_custom_call" | custom-call | flops 1 | bytes 1 | tf_op jit(solution)/shard_map/attention_forward/pallas_call | solution.py:71
  56.3 7.1 %mlp_both.1 = (bf16[256,384]{1,0:T(8,128)(2,1)}, f32[256,384]{1,0:T(8,128)S(1)}, f32[1,3072]{1,0:T(1,128)S(1)}, bf16[4,96,1536]{2,1,0:T(8,128)(2,1)S(1)}, bf16[4,96,1536]{2,1,0:T(8,128)(2,1)S(1)}) custom-call(s32[3]{0:T(128)S(1)} %pad_add_fusion.refs_0_.idx, f32[256,384]{1,0:T(8,128)S(1)} %get-tuple-element.119.refs_1_, f32[2,5376]{1,0:T(2,128)S(1)} %add_add_fusion.refs_2_, ...), custom_call_target="tpu_custom_call" | custom-call | flops 1 | bytes 1 | tf_op jit(solution)/shard_map/mlp_both/pallas_call | solution.py:71
  64.0 5.9 %attention_backward.2 = (f32[256,384]{1,0:T(8,128)S(1)}, f32[1,2304]{1,0:T(1,128)S(1)}, bf16[4,96,768]{2,1,0:T(8,128)(2,1)S(1)}, bf16[4,96,768]{2,1,0:T(8,128)(2,1)S(1)}) custom-call(s32[3]{0:T(128)S(1)} %pad_add_fusion.refs_0_.idx, f32[256,384]{1,0:T(8,128)S(1)} %get-tuple-element.116.refs_1_, f32[2,5376]{1,0:T(2,128)S(1)} %add_add_fusion.refs_2_, ...), custom_call_target="tpu_custom_call" | custom-call | flops 1 | bytes 1 | tf_op jit(solution)/shard_map/attention_backward/pallas_call | solution.py:71
  69.9 2.0 %collective-permute-done.14.refs_2_ = bf16[4,96,768]{2,1,0:T(8,128)(2,1)S(1)} collective-permute-done((bf16[4,96,768]{2,1,0:T(8,128)(2,1)S(1)}, bf16[4,96,768]{2,1,0:T(8,128)(2,1)S(1)}, u32[]{:S(2)}, u32[]{:S(2)}) %collective-permute-start.14) | collective-permute-done | bytes 589856 | tf_op jit(solution)/shard_map/ppermute | solution.py:608
  73.6 4.6 %mlp_backward.1 = (f32[256,384]{1,0:T(8,128)S(1)}, f32[1,3072]{1,0:T(1,128)S(1)}, bf16[4,96,1536]{2,1,0:T(8,128)(2,1)S(1)}, bf16[4,96,1536]{2,1,0:T(8,128)(2,1)S(1)}) custom-call(s32[3]{0:T(128)S(1)} %pad_add_fusion.refs_0_.idx, f32[256,384]{1,0:T(8,128)S(1)} %get-tuple-element.115.refs_1_, f32[2,5376]{1,0:T(2,128)S(1)} %add_add_fusion.refs_2_, ...), custom_call_target="tpu_custom_call" | custom-call | flops 1 | bytes 1 | tf_op jit(solution)/shard_map/mlp_backward/pallas_call | solution.py:71
  81.6 6.8 %attention_backward.3 = (f32[256,384]{1,0:T(8,128)}, f32[1,2304]{1,0:T(1,128)S(1)}, bf16[4,96,768]{2,1,0:T(8,128)(2,1)S(1)}, bf16[4,96,768]{2,1,0:T(8,128)(2,1)S(1)}) custom-call(s32[3]{0:T(128)S(1)} %pad_add_fusion.refs_0_.idx, bf16[256,384]{1,0:T(8,128)(2,1)S(1)} %bitcast.8, f32[2,5376]{1,0:T(2,128)S(1)} %add_add_fusion.refs_2_, ...), custom_call_target="tpu_custom_call" | custom-call | flops 1 | bytes 1 | tf_op jit(solution)/shard_map/attention_backward/pallas_call | solution.py:71
  95.1 7.9 %collective-permute-done.19.other = bf16[2,96,1536]{2,1,0:T(8,128)(2,1)S(1)} collective-permute-done((bf16[2,96,1536]{2,1,0:T(8,128)(2,1)S(1)}, bf16[2,96,1536]{2,1,0:T(8,128)(2,1)S(1)}, u32[]{:S(2)}, u32[]{:S(2)}) %collective-permute-start.19) | collective-permute-done | bytes 589856 | tf_op jit(solution)/shard_map/ppermute | solution.py:608
  103.2 1.8 %collective-permute-done.20.refs_2_ = bf16[96,2304]{1,0:T(8,128)(2,1)S(1)} collective-permute-done((bf16[96,2304]{1,0:T(8,128)(2,1)S(1)}, bf16[96,2304]{1,0:T(8,128)(2,1)S(1)}, u32[]{:S(2)}, u32[]{:S(2)}) %collective-permute-start.20) | collective-permute-done | bytes 442400 | tf_op jit(solution)/shard_map/ppermute | solution.py:608
  107.2 1.6 collective-permute-start.24
  109.5 1.6 collective-permute-start.22
  111.1 2.5 %collective-permute-done.22.second = bf16[1,11136]{1,0:T(2,128)(2,1)S(1)} collective-permute-done((bf16[1,11136]{1,0:T(2,128)(2,1)S(1)}, bf16[1,11136]{1,0:T(2,128)(2,1)S(1)}, u32[]{:S(2)}, u32[]{:S(2)}) %collective-permute-start.22) | collective-permute-done | bytes 22304 | tf_op jit(solution)/shard_map/ppermute | solution.py:608
  116.7 2.6 %collective-permute-start.32 = (bf16[48,2304]{1,0:T(8,128)(2,1)S(1)}, bf16[48,2304]{1,0:T(8,128)(2,1)S(1)}, u32[]{:S(2)}, u32[]{:S(2)}) collective-permute-start(bf16[48,2304]{1,0:T(8,128)(2,1)S(1)} %add.72.refs_0_), channel_id=1, source_target_pairs={{0,4},{1,5},{2,6},{3,7},{4,0},{5,1},{6,2},{7,3},{8,12},{9,13},{10,... | collective-permute-start | bytes 663560 | tf_op jit(solution)/shard_map/ppermute | solution.py:608
  120.7 2.6 %collective-permute-done.26.second = bf16[2,11136]{1,0:T(2,128)(2,1)S(1)} collective-permute-done((bf16[2,11136]{1,0:T(2,128)(2,1)S(1)}, bf16[2,11136]{1,0:T(2,128)(2,1)S(1)}, u32[]{:S(2)}, u32[]{:S(2)}) %collective-permute-start.26) | collective-permute-done | bytes 44576 | tf_op jit(solution)/shard_map/ppermute | solution.py:608
  123.3 2.1 %group.1 = (f32[2,384]{1,0:T(2,128)S(1)}, f32[2,384]{1,0:T(2,128)S(1)}, bf16[6,4992]{1,0:T(8,128)(2,1)S(1)}) custom-call(s32[3]{0:T(128)S(1)} %pad_add_fusion.refs_0_.idx, bf16[2,96,2304]{2,1,0:T(8,128)(2,1)S(1)} %copy-done.4, bf16[2,11136]{1,0:T(2,128)(2,1)S(1)} %stack.18.first, bf16[2,11136]{1,0:T(2,128)(2,1)S(1)} %collective-permute-done.26.second), custom_call_target="tpu_custom_call" | custom-call | flops 1 | bytes 1 | tf_op jit(solution)/shard_map/group/pallas_call | solution.py:71
  126.8 3.1 %collective-permute-done.31.second = bf16[6,4992]{1,0:T(8,128)(2,1)S(1)} collective-permute-done((bf16[6,4992]{1,0:T(8,128)(2,1)S(1)}, bf16[6,4992]{1,0:T(8,128)(2,1)S(1)}, u32[]{:S(2)}, u32[]{:S(2)}) %collective-permute-start.31) | collective-permute-done | bytes 59936 | tf_op jit(solution)/shard_map/ppermute | solution.py:608
  130.0 2.3 %collective-permute-start.40 = (bf16[10,4992]{1,0:T(8,128)(2,1)S(1)}, bf16[10,4992]{1,0:T(8,128)(2,1)S(1)}, u32[]{:S(2)}, u32[]{:S(2)}) collective-permute-start(bf16[10,4992]{1,0:T(8,128)(2,1)S(1)} %stack.19.refs_1_), channel_id=1, source_target_pairs={{0,4},{1,5},{2,6},{3,7},{4,0},{5,1},{6,2},{7,3},{8,12},{9,13},{10,... | collective-permute-start | bytes 299528 | tf_op jit(solution)/shard_map/ppermute | solution.py:608
  133.7 2.2 %collective-permute-done.27 = f32[2,384]{1,0:T(2,128)S(1)} collective-permute-done((f32[2,384]{1,0:T(2,128)S(1)}, f32[2,384]{1,0:T(2,128)S(1)}, u32[]{:S(2)}, u32[]{:S(2)}) %collective-permute-start.27) | collective-permute-done | bytes 3104 | tf_op jit(solution)/shard_map/ppermute | solution.py:608
  135.9 1.6 %collective-permute-start.28 = (f32[1,384]{1,0:T(1,128)S(1)}, f32[1,384]{1,0:T(1,128)S(1)}, u32[]{:S(2)}, u32[]{:S(2)}) collective-permute-start(f32[1,384]{1,0:T(1,128)S(1)} %slice.97), channel_id=1, source_target_pairs={{0,8},{1,17},{2,10},{3,19},{4,12},{5,21},{6,14},{7,23},{8,0},{9,25... | collective-permute-start | bytes 4616 | tf_op jit(solution)/shard_map/ppermute | solution.py:608
  139.0 2.4 %collective-permute-done.40.refs_2_ = bf16[10,4992]{1,0:T(8,128)(2,1)S(1)} collective-permute-done((bf16[10,4992]{1,0:T(8,128)(2,1)S(1)}, bf16[10,4992]{1,0:T(8,128)(2,1)S(1)}, u32[]{:S(2)}, u32[]{:S(2)}) %collective-permute-start.40) | collective-permute-done | bytes 99872 | tf_op jit(solution)/shard_map/ppermute | solution.py:608
  145.2 2.2 %ada_grad.1 = (f32[2,96,2304]{2,1,0:T(8,128)}, f32[1,10752]{1,0:T(1,128)S(1)}) custom-call(s32[3]{0:T(128)S(1)} %pad_add_fusion.refs_0_.idx, bf16[10,4992]{1,0:T(8,128)(2,1)S(1)} %stack.19.refs_1_, bf16[10,4992]{1,0:T(8,128)(2,1)S(1)} %collective-permute-done.40.refs_2_, bf16[10,4992]{1,0:T(8,128)(2,1)S(1)} %collective-permute-done.41.refs_3_, ...), custom_call_target="tpu_custom_call" | custom-call | flops 1 | bytes 1 | tf_op jit(solution)/shard_map/ada_grad/pallas_call | solution.py:71
  147.4 4.2 %collective-permute-done.43.refs_1_ = bf16[96,768]{1,0:T(8,128)(2,1)S(1)} collective-permute-done((bf16[96,768]{1,0:T(8,128)(2,1)S(1)}, bf16[96,768]{1,0:T(8,128)(2,1)S(1)}, u32[]{:S(2)}, u32[]{:S(2)}) %collective-permute-start.43) | collective-permute-done | bytes 147488 | tf_op jit(solution)/shard_map/ppermute | solution.py:608
  155.6 2.6 %finish.1 = (f32[2,96,1152]{2,1,0:T(8,128)}, f32[2,96,384]{2,1,0:T(8,128)}, f32[2,96,1536]{2,1,0:T(8,128)}, f32[2,384,384]{2,1,0:T(8,128)}) custom-call(s32[3]{0:T(128)S(1)} %pad_add_fusion.refs_0_.idx, bf16[48,2304]{1,0:T(8,128)(2,1)S(1)} %add.76.refs_1_, bf16[48,2304]{1,0:T(8,128)(2,1)S(1)} %collective-permute-done.33.refs_2_, ...), custom_call_target="tpu_custom_call" | custom-call | flops 1 | bytes 1 | tf_op jit(solution)/shard_map/finish/pallas_call | solution.py:71
  (148 shorter events, 45.7 us)
Async XLA Ops:
  2.0 18.2 %collective-permute-start.3 = (bf16[96,4608]{1,0:T(8,128)(2,1)S(1)}, bf16[96,4608]{1,0:T(8,128)(2,1)S(1)}, u32[]{:S(2)}, u32[]{:S(2)}) collective-permute-start(bf16[96,4608]{1,0:T(8,128)(2,1)S(1)} %pack.2), channel_id=1, source_target_pairs={{0,8},{1,17},{2,10},{3,19},{4,12},{5,21},{6,14},{7,23},{8,0},{9,25... | collective-permute-start | bytes 2654216 | tf_op jit(solution)/shard_map/ppermute | solution.py:608
  5.0 11.1 %collective-permute-start = (bf16[1,384]{1,0:T(2,128)(2,1)S(1)}, bf16[1,384]{1,0:T(2,128)(2,1)S(1)}, u32[]{:S(2)}, u32[]{:S(2)}) collective-permute-start(bf16[1,384]{1,0:T(2,128)(2,1)S(1)} %copy-done.14), channel_id=1, source_target_pairs={{0,8},{1,9},{2,10},{3,11},{4,12},{5,13},{6,14},{7,15},{8,0},{9,1},... | collective-permute-start | bytes 2312 | tf_op jit(solution)/shard_map/ppermute | solution.py:608
  5.1 11.0 %collective-permute-start.1 = (bf16[1,384]{1,0:T(2,128)(2,1)S(1)}, bf16[1,384]{1,0:T(2,128)(2,1)S(1)}, u32[]{:S(2)}, u32[]{:S(2)}) collective-permute-start(bf16[1,384]{1,0:T(2,128)(2,1)S(1)} %copy-done.14), channel_id=1, source_target_pairs={{0,16},{1,17},{2,18},{3,19},{4,20},{5,21},{6,22},{7,23},{8,24},{9,... | collective-permute-start | bytes 2312 | tf_op jit(solution)/shard_map/ppermute | solution.py:608
  7.1 10.5 %collective-permute-start.2 = (bf16[1,384]{1,0:T(2,128)(2,1)S(1)}, bf16[1,384]{1,0:T(2,128)(2,1)S(1)}, u32[]{:S(2)}, u32[]{:S(2)}) collective-permute-start(bf16[1,384]{1,0:T(2,128)(2,1)S(1)} %copy-done.14), channel_id=1, source_target_pairs={{0,24},{1,25},{2,26},{3,27},{4,28},{5,29},{6,30},{7,31},{8,16},{9,... | collective-permute-start | bytes 2312 | tf_op jit(solution)/shard_map/ppermute | solution.py:608
  20.8 11.7 %collective-permute-start.7 = (bf16[96,2304]{1,0:T(8,128)(2,1)S(1)}, bf16[96,2304]{1,0:T(8,128)(2,1)S(1)}, u32[]{:S(2)}, u32[]{:S(2)}) collective-permute-start(bf16[96,2304]{1,0:T(8,128)(2,1)S(1)} %half.2), channel_id=1, source_target_pairs={{0,16},{1,9},{2,18},{3,11},{4,20},{5,13},{6,22},{7,15},{8,24},{9,1... | collective-permute-start | bytes 1327112 | tf_op jit(solution)/shard_map/ppermute | solution.py:608
  21.5 6.4 %collective-permute-start.4 = (f32[2,5376]{1,0:T(2,128)S(1)}, f32[2,5376]{1,0:T(2,128)S(1)}, u32[]{:S(2)}, u32[]{:S(2)}) collective-permute-start(f32[2,5376]{1,0:T(2,128)S(1)} %get-tuple-element.107), channel_id=1, source_target_pairs={{0,8},{1,9},{2,10},{3,11},{4,12},{5,13},{6,14},{7,15},{8,0},{9,1},... | collective-permute-start | bytes 129032 | tf_op jit(solution)/shard_map/ppermute | solution.py:608
  23.0 10.5 %collective-permute-start.5 = (f32[2,5376]{1,0:T(2,128)S(1)}, f32[2,5376]{1,0:T(2,128)S(1)}, u32[]{:S(2)}, u32[]{:S(2)}) collective-permute-start(f32[2,5376]{1,0:T(2,128)S(1)} %get-tuple-element.109), channel_id=1, source_target_pairs={{0,16},{1,17},{2,18},{3,19},{4,20},{5,21},{6,22},{7,23},{8,24},{9,... | collective-permute-start | bytes 129032 | tf_op jit(solution)/shard_map/ppermute | solution.py:608
  24.4 9.0 %collective-permute-start.6 = (f32[2,5376]{1,0:T(2,128)S(1)}, f32[2,5376]{1,0:T(2,128)S(1)}, u32[]{:S(2)}, u32[]{:S(2)}) collective-permute-start(f32[2,5376]{1,0:T(2,128)S(1)} %get-tuple-element.111), channel_id=1, source_target_pairs={{0,24},{1,25},{2,26},{3,27},{4,28},{5,29},{6,30},{7,31},{8,16},{9,... | collective-permute-start | bytes 129032 | tf_op jit(solution)/shard_map/ppermute | solution.py:608
  26.3 13.1 %collective-permute-start.10 = (bf16[96,4608]{1,0:T(8,128)(2,1)S(1)}, bf16[96,4608]{1,0:T(8,128)(2,1)S(1)}, u32[]{:S(2)}, u32[]{:S(2)}) collective-permute-start(bf16[96,4608]{1,0:T(8,128)(2,1)S(1)} %pack.3), channel_id=1, source_target_pairs={{0,8},{1,17},{2,10},{3,19},{4,12},{5,21},{6,14},{7,23},{8,0},{9,25... | collective-permute-start | bytes 2654216 | tf_op jit(solution)/shard_map/ppermute | solution.py:608
  27.8 13.7 %collective-permute-start.8 = (bf16[96,4608]{1,0:T(8,128)(2,1)S(1)}, bf16[96,4608]{1,0:T(8,128)(2,1)S(1)}, u32[]{:S(2)}, u32[]{:S(2)}) collective-permute-start(bf16[96,4608]{1,0:T(8,128)(2,1)S(1)} %collective-permute-done.3.whole.refs_5_.refs_9_.refs_10_), channel_id=1, source_target_pairs={{0,1},{1,0},{2,3},{3,2},{4,5},{5,4},{6,7},{7,6},{8,9},{9,8},{10,11... | collective-permute-start | bytes 2654216 | tf_op jit(solution)/shard_map/ppermute | solution.py:608
  32.5 9.0 %collective-permute-start.9 = (bf16[96,2304]{1,0:T(8,128)(2,1)S(1)}, bf16[96,2304]{1,0:T(8,128)(2,1)S(1)}, u32[]{:S(2)}, u32[]{:S(2)}) collective-permute-start(bf16[96,2304]{1,0:T(8,128)(2,1)S(1)} %collective-permute-done.7.refs_6_.refs_10_.refs_11_), channel_id=1, source_target_pairs={{0,1},{1,0},{2,3},{3,2},{4,5},{5,4},{6,7},{7,6},{8,9},{9,8},{10,11... | collective-permute-start | bytes 1327112 | tf_op jit(solution)/shard_map/ppermute | solution.py:608
  40.0 8.4 %collective-permute-start.11 = (bf16[96,2304]{1,0:T(8,128)(2,1)S(1)}, bf16[96,2304]{1,0:T(8,128)(2,1)S(1)}, u32[]{:S(2)}, u32[]{:S(2)}) collective-permute-start(bf16[96,2304]{1,0:T(8,128)(2,1)S(1)} %half.3), channel_id=1, source_target_pairs={{0,16},{1,9},{2,18},{3,11},{4,20},{5,13},{6,22},{7,15},{8,24},{9,1... | collective-permute-start | bytes 1327112 | tf_op jit(solution)/shard_map/ppermute | solution.py:608
  45.8 7.4 %collective-permute-start.12 = (bf16[96,4608]{1,0:T(8,128)(2,1)S(1)}, bf16[96,4608]{1,0:T(8,128)(2,1)S(1)}, u32[]{:S(2)}, u32[]{:S(2)}) collective-permute-start(bf16[96,4608]{1,0:T(8,128)(2,1)S(1)} %collective-permute-done.10.whole.refs_5_.refs_6_.refs_10_), channel_id=1, source_target_pairs={{0,1},{1,0},{2,3},{3,2},{4,5},{5,4},{6,7},{7,6},{8,9},{9,8},{10,11... | collective-permute-start | bytes 2654216 | tf_op jit(solution)/shard_map/ppermute | solution.py:608
  63.4 8.5 %collective-permute-start.15 = (bf16[4,96,1536]{2,1,0:T(8,128)(2,1)S(1)}, bf16[4,96,1536]{2,1,0:T(8,128)(2,1)S(1)}, u32[]{:S(2)}, u32[]{:S(2)}) collective-permute-start(bf16[4,96,1536]{2,1,0:T(8,128)(2,1)S(1)} %get-tuple-element.131), channel_id=1, source_target_pairs={{0,1},{1,0},{2,3},{3,2},{4,5},{5,4},{6,7},{7,6},{8,9},{9,8},{10,11... | collective-permute-start | bytes 3538952 | tf_op jit(solution)/shard_map/ppermute | solution.py:608
  78.5 13.0 %collective-permute-start.17 = (bf16[2,96,2304]{2,1,0:T(8,128)(2,1)S(1)}, bf16[2,96,2304]{2,1,0:T(8,128)(2,1)S(1)}, u32[]{:S(2)}, u32[]{:S(2)}) collective-permute-start(bf16[2,96,2304]{2,1,0:T(8,128)(2,1)S(1)} %get-tuple-element.154), channel_id=1, source_target_pairs={{0,8},{1,17},{2,10},{3,19},{4,12},{5,21},{6,14},{7,23},{8,0},{9,25... | collective-permute-start | bytes 2654216 | tf_op jit(solution)/shard_map/ppermute | solution.py:608
  88.6 14.4 %collective-permute-start.19 = (bf16[2,96,1536]{2,1,0:T(8,128)(2,1)S(1)}, bf16[2,96,1536]{2,1,0:T(8,128)(2,1)S(1)}, u32[]{:S(2)}, u32[]{:S(2)}) collective-permute-start(bf16[2,96,1536]{2,1,0:T(8,128)(2,1)S(1)} %get-tuple-element.160), channel_id=1, source_target_pairs={{0,8},{1,17},{2,10},{3,19},{4,12},{5,21},{6,14},{7,23},{8,0},{9,25... | collective-permute-start | bytes 1769480 | tf_op jit(solution)/shard_map/ppermute | solution.py:608
  91.8 13.2 %collective-permute-start.20 = (bf16[96,2304]{1,0:T(8,128)(2,1)S(1)}, bf16[96,2304]{1,0:T(8,128)(2,1)S(1)}, u32[]{:S(2)}, u32[]{:S(2)}) collective-permute-start(bf16[96,2304]{1,0:T(8,128)(2,1)S(1)} %get-tuple-element.164), channel_id=1, source_target_pairs={{0,16},{1,9},{2,18},{3,11},{4,20},{5,13},{6,22},{7,15},{8,24},{9,1... | collective-permute-start | bytes 1327112 | tf_op jit(solution)/shard_map/ppermute | solution.py:608
  93.5 15.3 %collective-permute-start.21 = (bf16[2,96,768]{2,1,0:T(8,128)(2,1)S(1)}, bf16[2,96,768]{2,1,0:T(8,128)(2,1)S(1)}, u32[]{:S(2)}, u32[]{:S(2)}) collective-permute-start(bf16[2,96,768]{2,1,0:T(8,128)(2,1)S(1)} %get-tuple-element.167), channel_id=1, source_target_pairs={{0,8},{1,17},{2,10},{3,19},{4,12},{5,21},{6,14},{7,23},{8,0},{9,25... | collective-permute-start | bytes 884744 | tf_op jit(solution)/shard_map/ppermute | solution.py:608
  105.7 8.0 %collective-permute-start.23 = (bf16[96,1536]{1,0:T(8,128)(2,1)S(1)}, bf16[96,1536]{1,0:T(8,128)(2,1)S(1)}, u32[]{:S(2)}, u32[]{:S(2)}) collective-permute-start(bf16[96,1536]{1,0:T(8,128)(2,1)S(1)} %get-tuple-element.171), channel_id=1, source_target_pairs={{0,16},{1,9},{2,18},{3,11},{4,20},{5,13},{6,22},{7,15},{8,24},{9,1... | collective-permute-start | bytes 884744 | tf_op jit(solution)/shard_map/ppermute | solution.py:608
  107.2 8.1 %collective-permute-start.24 = (bf16[48,2304]{1,0:T(8,128)(2,1)S(1)}, bf16[48,2304]{1,0:T(8,128)(2,1)S(1)}, u32[]{:S(2)}, u32[]{:S(2)}) collective-permute-start(bf16[48,2304]{1,0:T(8,128)(2,1)S(1)} %get-tuple-element.174), channel_id=1, source_target_pairs={{0,2},{1,3},{2,0},{3,1},{4,6},{5,7},{6,4},{7,5},{8,10},{9,11},{10,... | collective-permute-start | bytes 663560 | tf_op jit(solution)/shard_map/ppermute | solution.py:608
  108.9 6.5 %collective-permute-start.25 = (bf16[96,768]{1,0:T(8,128)(2,1)S(1)}, bf16[96,768]{1,0:T(8,128)(2,1)S(1)}, u32[]{:S(2)}, u32[]{:S(2)}) collective-permute-start(bf16[96,768]{1,0:T(8,128)(2,1)S(1)} %get-tuple-element.176), channel_id=1, source_target_pairs={{0,16},{1,9},{2,18},{3,11},{4,20},{5,13},{6,22},{7,15},{8,24},{9,1... | collective-permute-start | bytes 442376 | tf_op jit(solution)/shard_map/ppermute | solution.py:608
  114.4 11.9 %collective-permute-start.29 = (bf16[48,1536]{1,0:T(8,128)(2,1)S(1)}, bf16[48,1536]{1,0:T(8,128)(2,1)S(1)}, u32[]{:S(2)}, u32[]{:S(2)}) collective-permute-start(bf16[48,1536]{1,0:T(8,128)(2,1)S(1)} %get-tuple-element.182), channel_id=1, source_target_pairs={{0,2},{1,3},{2,0},{3,1},{4,6},{5,7},{6,4},{7,5},{8,10},{9,11},{10,... | collective-permute-start | bytes 442376 | tf_op jit(solution)/shard_map/ppermute | solution.py:608
  115.4 11.3 %collective-permute-start.30 = (bf16[96,768]{1,0:T(8,128)(2,1)S(1)}, bf16[96,768]{1,0:T(8,128)(2,1)S(1)}, u32[]{:S(2)}, u32[]{:S(2)}) collective-permute-start(bf16[96,768]{1,0:T(8,128)(2,1)S(1)} %add.73.refs_0_), channel_id=1, source_target_pairs={{0,2},{1,3},{2,0},{3,1},{4,6},{5,7},{6,4},{7,5},{8,10},{9,11},{10,... | collective-permute-start | bytes 442376 | tf_op jit(solution)/shard_map/ppermute | solution.py:608
  116.7 20.8 %collective-permute-start.32 = (bf16[48,2304]{1,0:T(8,128)(2,1)S(1)}, bf16[48,2304]{1,0:T(8,128)(2,1)S(1)}, u32[]{:S(2)}, u32[]{:S(2)}) collective-permute-start(bf16[48,2304]{1,0:T(8,128)(2,1)S(1)} %add.72.refs_0_), channel_id=1, source_target_pairs={{0,4},{1,5},{2,6},{3,7},{4,0},{5,1},{6,2},{7,3},{8,12},{9,13},{10,... | collective-permute-start | bytes 663560 | tf_op jit(solution)/shard_map/ppermute | solution.py:608
  126.3 12.5 %collective-permute-start.36 = (bf16[48,1536]{1,0:T(8,128)(2,1)S(1)}, bf16[48,1536]{1,0:T(8,128)(2,1)S(1)}, u32[]{:S(2)}, u32[]{:S(2)}) collective-permute-start(bf16[48,1536]{1,0:T(8,128)(2,1)S(1)} %add.74.refs_0_), channel_id=1, source_target_pairs={{0,4},{1,5},{2,6},{3,7},{4,0},{5,1},{6,2},{7,3},{8,12},{9,13},{10,... | collective-permute-start | bytes 442376 | tf_op jit(solution)/shard_map/ppermute | solution.py:608
  130.0 11.5 %collective-permute-start.40 = (bf16[10,4992]{1,0:T(8,128)(2,1)S(1)}, bf16[10,4992]{1,0:T(8,128)(2,1)S(1)}, u32[]{:S(2)}, u32[]{:S(2)}) collective-permute-start(bf16[10,4992]{1,0:T(8,128)(2,1)S(1)} %stack.19.refs_1_), channel_id=1, source_target_pairs={{0,4},{1,5},{2,6},{3,7},{4,0},{5,1},{6,2},{7,3},{8,12},{9,13},{10,... | collective-permute-start | bytes 299528 | tf_op jit(solution)/shard_map/ppermute | solution.py:608
  138.9 5.8 %collective-permute-start.37 = (bf16[48,1536]{1,0:T(8,128)(2,1)S(1)}, bf16[48,1536]{1,0:T(8,128)(2,1)S(1)}, u32[]{:S(2)}, u32[]{:S(2)}) collective-permute-start(bf16[48,1536]{1,0:T(8,128)(2,1)S(1)} %add.77.refs_5_), channel_id=1, source_target_pairs={{0,2},{1,3},{2,0},{3,1},{4,6},{5,7},{6,4},{7,5},{8,10},{9,11},{10,... | collective-permute-start | bytes 442376 | tf_op jit(solution)/shard_map/ppermute | solution.py:608
  142.1 9.6 %collective-permute-start.43 = (bf16[96,768]{1,0:T(8,128)(2,1)S(1)}, bf16[96,768]{1,0:T(8,128)(2,1)S(1)}, u32[]{:S(2)}, u32[]{:S(2)}) collective-permute-start(bf16[96,768]{1,0:T(8,128)(2,1)S(1)} %add.75.refs_0_), channel_id=1, source_target_pairs={{0,4},{1,5},{2,6},{3,7},{4,0},{5,1},{6,2},{7,3},{8,12},{9,13},{10,... | collective-permute-start | bytes 442376 | tf_op jit(solution)/shard_map/ppermute | solution.py:608
  143.2 12.3 %collective-permute-start.38 = (bf16[48,1536]{1,0:T(8,128)(2,1)S(1)}, bf16[48,1536]{1,0:T(8,128)(2,1)S(1)}, u32[]{:S(2)}, u32[]{:S(2)}) collective-permute-start(bf16[48,1536]{1,0:T(8,128)(2,1)S(1)} %add.77.refs_5_), channel_id=1, source_target_pairs={{0,1},{1,0},{2,3},{3,2},{4,5},{5,4},{6,7},{7,6},{8,9},{9,8},{10,11... | collective-permute-start | bytes 442376 | tf_op jit(solution)/shard_map/ppermute | solution.py:608
  143.2 11.0 %collective-permute-start.33 = (bf16[48,2304]{1,0:T(8,128)(2,1)S(1)}, bf16[48,2304]{1,0:T(8,128)(2,1)S(1)}, u32[]{:S(2)}, u32[]{:S(2)}) collective-permute-start(bf16[48,2304]{1,0:T(8,128)(2,1)S(1)} %add.76.refs_1_), channel_id=1, source_target_pairs={{0,2},{1,3},{2,0},{3,1},{4,6},{5,7},{6,4},{7,5},{8,10},{9,11},{10,... | collective-permute-start | bytes 663560 | tf_op jit(solution)/shard_map/ppermute | solution.py:608
  144.6 10.8 %collective-permute-start.34 = (bf16[48,2304]{1,0:T(8,128)(2,1)S(1)}, bf16[48,2304]{1,0:T(8,128)(2,1)S(1)}, u32[]{:S(2)}, u32[]{:S(2)}) collective-permute-start(bf16[48,2304]{1,0:T(8,128)(2,1)S(1)} %add.76.refs_1_), channel_id=1, source_target_pairs={{0,1},{1,0},{2,3},{3,2},{4,5},{5,4},{6,7},{7,6},{8,9},{9,8},{10,11... | collective-permute-start | bytes 663560 | tf_op jit(solution)/shard_map/ppermute | solution.py:608
  144.7 10.8 %collective-permute-start.39 = (bf16[48,1536]{1,0:T(8,128)(2,1)S(1)}, bf16[48,1536]{1,0:T(8,128)(2,1)S(1)}, u32[]{:S(2)}, u32[]{:S(2)}) collective-permute-start(bf16[48,1536]{1,0:T(8,128)(2,1)S(1)} %collective-permute-done.37.refs_6_), channel_id=1, source_target_pairs={{0,1},{1,0},{2,3},{3,2},{4,5},{5,4},{6,7},{7,6},{8,9},{9,8},{10,11... | collective-permute-start | bytes 442376 | tf_op jit(solution)/shard_map/ppermute | solution.py:608
  (29 other events, 156.5 us)
